TPU v7x, 256 devices: a whole 4x4x8 slice. The times are simulated.
256 devices in a mesh: blk: 64 (over y_hi, z, x), layer: 4 (over y_lo, core).
Axes of the slice: x: 4, y: 4 (y_hi: 2, y_lo: 2; y = y_hi * 2 + y_lo), z: 8, core: 2. Of those that a mesh axis runs over, the one named last changes fastest.
Arguments:
- ref_pos: float32 [64, 4, 3, 8192], P('blk', 'layer'), may hold values from -9 to 9
- disk_disp: float32 [64, 4, 3, 8192], P('blk', 'layer'), may hold values from -2 to 2
- disk_vel: float32 [64, 4, 3, 8192], P('blk', 'layer'), may hold values from -6 to 6
- damage: float32 [64, 4, 8192], P('blk', 'layer'), may hold values from 0 to 0.6
- modulus: float32 [64, 4, 8192], P('blk', 'layer'), may hold values from 0.5 to 2
- body_load: float32 [64, 4, 3, 8192], P('blk', 'layer'), may hold values from -6 to 6
- nbr_tiles: int32 [64, 4, 64, 15], P('blk', 'layer'), may hold values from 0 to 959, as said below
- break_flags: int32 [64, 4, 32], P('blk', 'layer'), may hold values from 0 to 1073741823, as said below
- blade_disp: float32 [64, 4, 3, 512], P('blk', 'layer'), may hold values from -2 to 2
- blade_vel: float32 [64, 4, 3, 512], P('blk', 'layer'), may hold values from -6 to 6
- elem_nodes: int32 [64, 4, 8, 128], P('blk', 'layer'), may hold values from 0 to 511
- elem_modulus: float32 [64, 4, 128], P('blk', 'layer'), may hold values from 0.5 to 2
- elem_stiff: float32 [24, 24], replicated, may hold values from -0.2 to 6, as said below
- root_nodes: int32 [64, 4, 64, 8], P('blk', 'layer'), may hold values from 0 to 511
- rim_points: int32 [64, 4, 64, 8], P('blk', 'layer'), may hold values from 0 to 8191
Outputs:
- disk_disp_new: float32 [64, 4, 3, 8192], P('blk', 'layer')
- disk_vel_new: float32 [64, 4, 3, 8192], P('blk', 'layer')
- blade_disp_new: float32 [64, 4, 3, 512], P('blk', 'layer')
- blade_vel_new: float32 [64, 4, 3, 512], P('blk', 'layer')
Inputs may be any that keep to these rules, and one draw needn't show every extreme that they name: `nbr_tiles`: entry k of every list names block k, except where slab l + (k mod 3) - 1 lies outside 0 to 3; there it names block k - (k mod 3) + 1 of the own slab. The tile within the block is arbitrary; tiles may repeat. `break_flags`: only bits 0 to 29 are used; a set bit marks a neighbour tile whose bonds are all broken. `elem_stiff`: Symmetric.
All inputs are finite; a program needn't handle non-finite values.
Results may differ from a plain program's by a relative error of at most 0.0003.
Values sent between devices are 32-bit elements; how exact they have to be, the bound alone decides.
No kernel may reach another device: no remote copies, remote signals or barrier semaphores. Data moves between devices by JAX's collectives and lax.ppermute only.
A program may use at most 64 MiB of HBM per device.

v0:
```python
import jax
import jax.numpy as jnp
from jax import lax
from jax.sharding import PartitionSpec as P

bond_scale = 0.5
spring = 0.5
time_step = 0.5
horizon_sq = 9.0


def extended(shard, sides, width):
    for axis, dim in sides:
        size, length = (lax.axis_size(axis), shard.shape[dim])
        up = [(i, (i + 1) % size) for i in range(size - 1)]
        down = [(j, i) for i, j in up]
        last = lax.slice_in_dim(shard, length - width, length, axis=dim)
        initial = lax.slice_in_dim(shard, 0, width, axis=dim)
        before = lax.ppermute(last, axis, up)
        after = lax.ppermute(initial, axis, down)
        shard = jnp.concatenate([before, shard, after], axis=dim)
    return shard


def from_behind(shard, axis, by):
    length = lax.axis_size(axis)
    return lax.ppermute(shard, axis, [(i, (i + by) % length) for i in range(length)])


def pair_force(own_tile, neighbours, alive_row):
    bond_ref = neighbours[:, 0:3, None, :] - own_tile[0:3, :, None]
    bond_now = bond_ref + neighbours[:, 3:6, None, :] - own_tile[3:6, :, None]
    ref_sq = jnp.sum(bond_ref * bond_ref, axis=1)
    now_sq = jnp.sum(bond_now * bond_now, axis=1)
    strain = (now_sq - ref_sq) / (2.0 * (ref_sq + 1.0))
    intact = (1.0 - own_tile[6])[None, :, None] * (1.0 - neighbours[:, 6])[:, None, :]
    stiffness = 0.5 * (own_tile[7][None, :, None] + neighbours[:, 7][:, None, :])
    coeff = (
        bond_scale
        * stiffness
        * intact
        * jnp.exp(-ref_sq / horizon_sq)
        * strain
        * alive_row[:, None, None]
    )
    return jnp.sum(coeff[:, None] * bond_now, axis=(0, 3))


def alive_flags(flag_words, tile_count, slot_count):
    tile_ids = jnp.arange(tile_count, dtype=jnp.int32)
    word_tile = flag_words[tile_ids // 2]
    offsets = (tile_ids % 2)[:, None] * slot_count + jnp.arange(slot_count, dtype=jnp.int32)[
        None, :
    ]
    bits = jnp.right_shift(word_tile[:, None], offsets) & 1
    return (1 - bits).astype(jnp.float32)


def on_device(
    ref_pos,
    disk_disp,
    disk_vel,
    damage,
    modulus,
    body_load,
    nbr_tiles,
    break_flags,
    blade_disp,
    blade_vel,
    elem_nodes,
    elem_modulus,
    elem_stiff,
    root_nodes,
    rim_points,
):
    tile_count = ref_pos.shape[3] // 128
    slot_count = nbr_tiles.shape[3]
    packed = jnp.concatenate(
        [ref_pos, disk_disp, damage[:, :, None, :], modulus[:, :, None, :]], axis=2
    )
    slab_stack = extended(packed, (("layer", 1),), 1)
    behind = []
    current = slab_stack
    for repeat in range(2):
        current = from_behind(current, "blk", 1)
        behind.append(current)
    ahead = []
    current = slab_stack
    for repeat in range(2):
        current = from_behind(current, "blk", -1)
        ahead.append(current)
    window = jnp.concatenate([behind[1], behind[0], slab_stack, ahead[0], ahead[1]], axis=0)
    window = window.reshape(15, 8, tile_count, 128)
    own_field = packed[0, 0].reshape(8, tile_count, 128)
    alive_rows = alive_flags(break_flags[0, 0], tile_count, slot_count)
    name_rows = nbr_tiles[0, 0]
    tile_ids = jnp.arange(tile_count, dtype=jnp.int32)

    def fetch(name_row):
        return window[name_row // tile_count, :, name_row % tile_count]

    def tile_force(inputs):
        tile_id, name_row, alive_row = inputs
        return pair_force(own_field[:, tile_id], fetch(name_row), alive_row)

    forces = lax.map(tile_force, (tile_ids, name_rows, alive_rows), batch_size=4)
    bond_force = forces.transpose(1, 0, 2).reshape(3, tile_count * 128)
    disk_now = disk_disp[0, 0]
    blade_now = blade_disp[0, 0]
    rim_flat = rim_points[0, 0].reshape(-1)
    root_flat = root_nodes[0, 0].reshape(-1)
    rim_values = disk_now[:, rim_flat]
    at_roots = lax.all_to_all(rim_values, "blk", split_axis=1, concat_axis=1, tiled=True)
    loads = spring * (at_roots - blade_now[:, root_flat])
    coupling = jnp.zeros_like(blade_now).at[:, root_flat].add(loads)
    returned = lax.all_to_all(loads, "blk", split_axis=1, concat_axis=1, tiled=True)
    reaction = jnp.zeros_like(disk_now).at[:, rim_flat].add(-returned)
    connect = elem_nodes[0, 0]
    elem_count = connect.shape[1]
    gathered = blade_now[:, connect].reshape(24, elem_count)
    elem_force = elem_modulus[0, 0][None, :] * jnp.dot(
        elem_stiff, gathered, precision=lax.Precision.HIGHEST, preferred_element_type=jnp.float32
    )
    internal = jnp.zeros_like(blade_now).at[:, connect.reshape(-1)].add(-elem_force.reshape(3, -1))
    disk_vel_new = disk_vel[0, 0] + time_step * (bond_force + body_load[0, 0] + reaction)
    disk_disp_new = disk_now + time_step * disk_vel_new
    blade_vel_new = blade_vel[0, 0] + time_step * (internal + coupling)
    blade_disp_new = blade_now + time_step * blade_vel_new
    return (
        disk_disp_new[None, None],
        disk_vel_new[None, None],
        blade_disp_new[None, None],
        blade_vel_new[None, None],
    )


def solution(mesh):
    in_specs = (
        P("blk", "layer", None, None),
        P("blk", "layer", None, None),
        P("blk", "layer", None, None),
        P("blk", "layer", None),
        P("blk", "layer", None),
        P("blk", "layer", None, None),
        P("blk", "layer", None, None),
        P("blk", "layer", None),
        P("blk", "layer", None, None),
        P("blk", "layer", None, None),
        P("blk", "layer", None, None),
        P("blk", "layer", None),
        P(),
        P("blk", "layer", None, None),
        P("blk", "layer", None, None),
    )
    out_specs = (
        P("blk", "layer", None, None),
        P("blk", "layer", None, None),
        P("blk", "layer", None, None),
        P("blk", "layer", None, None),
    )
    return jax.shard_map(
        on_device, mesh=mesh, in_specs=in_specs, out_specs=out_specs, check_vma=False
    )
```

profile of v0, /device:TPU:1, one launch (start us, length us, event | category | flops | bytes accessed | tf_op | source)
XLA Modules:
  0.0 460.7 jit_solution(8238015721917443764)
XLA Ops:
  2.0 4.7 %collective-permute-start = (f32[1,1,8,8192]{3,1,2,0:T(1,128)S(1)}, f32[1,1,8,8192]{3,1,2,0:T(1,128)S(1)}, u32[]{:S(2)}, u32[]{:S(2)}) collective-permute-start(f32[1,1,8,8192]{3,1,2,0:T(1,128)S(1)} %pad_maximum_fusion.5), channel_id=1, source_target_pairs={{0,1},{1,2},{2,3},{4,5},{5,6},{6,7},{8,9},{9,10},{10,11},{12,13},{... | collective-permute-start | bytes 786440 | tf_op jit(solution)/shard_map/ppermute | solution.py:19
  8.7 3.4 copy.184
  12.3 3.2 gather_fusion.3
  16.6 14.0 %all-to-all-start = ((f32[3,64,8]{2,0,1:T(4,128)}), f32[3,64,8]{2,0,1:T(4,128)S(1)}, u32[]{:S(2)}, u32[]{:S(2)}) async-start(f32[3,64,8]{2,0,1:T(4,128)} %copy.193), calls=%async_computation | async-start | bytes 262144 | tf_op jit(solution)/shard_map/all_to_all | solution.py:113
  38.9 6.2 %collective-permute-start.4 = (f32[1,3,8,8192]{3,1,2,0:T(4,128)S(1)}, f32[1,3,8,8192]{3,1,2,0:T(4,128)}, u32[]{:S(2)}, u32[]{:S(2)}) collective-permute-start(f32[1,3,8,8192]{3,1,2,0:T(4,128)S(1)} %pad_maximum_fusion.1), channel_id=1, source_target_pairs={{0,252},{4,0},{8,4},{12,8},{16,12},{20,16},{24,20},{28,24},{32,28}... | collective-permute-start | bytes 2359304 | tf_op jit(solution)/shard_map/ppermute | solution.py:27
  45.1 20.5 %collective-permute-done.2 = f32[1,3,8,8192]{3,1,2,0:T(4,128)} collective-permute-done((f32[1,3,8,8192]{3,1,2,0:T(4,128)S(1)}, f32[1,3,8,8192]{3,1,2,0:T(4,128)}, u32[]{:S(2)}, u32[]{:S(2)}) %collective-permute-start.2) | collective-permute-done | bytes 786464 | tf_op jit(solution)/shard_map/ppermute | solution.py:27
  74.7 6.2 %scatter_custom_fusion.1 = f32[3,512]{0,1:T(8,128)S(1)} fusion(s32[1024]{0:T(1024)} %bitcast.177, f32[3,1024]{0,1:T(8,128)S(1)} %copy.205, f32[]{:T(128)} %constant.145.clone.1), kind=kCustom, calls=%fused_computation.57 | custom fusion | flops 3072 | bytes 18944 | tf_op jit(solution)/shard_map/scatter-add | solution.py:124
  82.5 10.5 %all-to-all-start.1 = ((f32[3,64,8]{2,0,1:T(4,128)}), f32[3,64,8]{2,0,1:T(4,128)}, u32[]{:S(2)}, u32[]{:S(2)}) async-start(f32[3,64,8]{2,0,1:T(4,128)} %copy.199), calls=%async_computation.1 | async-start | bytes 262144 | tf_op jit(solution)/shard_map/all_to_all | solution.py:116
  97.4 6.6 %all-to-all-done.1 = f32[3,64,8]{2,0,1:T(4,128)} async-done(((f32[3,64,8]{2,0,1:T(4,128)}), f32[3,64,8]{2,0,1:T(4,128)}, u32[]{:S(2)}, u32[]{:S(2)}) %all-to-all-start.1) | async-done | bytes 6176 | tf_op jit(solution)/shard_map/all_to_all | solution.py:116
  111.9 16.3 %collective-permute-done.5 = f32[1,3,8,8192]{3,1,2,0:T(4,128)S(1)} collective-permute-done((f32[1,3,8,8192]{3,1,2,0:T(4,128)}, f32[1,3,8,8192]{3,1,2,0:T(4,128)S(1)}, u32[]{:S(2)}, u32[]{:S(2)}) %collective-permute-start.5) | collective-permute-done | bytes 786464 | tf_op jit(solution)/shard_map/ppermute | solution.py:27
  128.5 4.1 copy.187
  132.6 297.0 %while.12 = (s32[]{:T(128)}, f32[16,4,3,128]{3,2,1,0:T(4,128)S(1)}, s32[16,4]{1,0:T(8,128)}, f32[8,64,128]{2,0,1:T(8,128)}, s32[16,4,15]{2,1,0:T(4,128)}, /*inde...) while((s32[]{:T(128)}, f32[16,4,3,128]{3,2,1,0:T(4,128)S(1)}, s32[16,4]{1,0:T(8,128)}, ...), condition=%wide.region_4.5_spmd, body=%wide.region_0.4_spmd.sunk | while | flops 46211356 | bytes 25370916 | solution.py:106
  133.4 2.9 gather_fusion.1
  138.5 6.5 %fusion.52 = (f32[4,15,128,128]{3,2,1,0:T(8,128)S(1)}, f32[4,15,128,128]{3,2,1,0:T(8,128)S(1)}) fusion(f32[4,3,128]{2,1,0:T(4,128)S(1)} %get-tuple-element.262, f32[4,15,3,128]{3,2,1,0:T(4,128)S(1)} %get-tuple-element.263, f32[4,3,128]{2,1,0:T(4,128)S(1)} %get-tuple-element.264, f32[4,15,3,128]{3,2,1,0:T(4,128)S(1)} %get-tuple-element.265), kind=kLoop, calls=%fused_computation.15.clone.1 | loop fusion | flops 18677760 | bytes 8060928 | tf_op jit(solution)/shard_map/while/body/eval_jaxpr/vmap()/reduce_sum | solution.py:34
  151.9 2.9 gather_fusion.1
  157.1 6.5 %fusion.52 = (f32[4,15,128,128]{3,2,1,0:T(8,128)S(1)}, f32[4,15,128,128]{3,2,1,0:T(8,128)S(1)}) fusion(f32[4,3,128]{2,1,0:T(4,128)S(1)} %get-tuple-element.262, f32[4,15,3,128]{3,2,1,0:T(4,128)S(1)} %get-tuple-element.263, f32[4,3,128]{2,1,0:T(4,128)S(1)} %get-tuple-element.264, f32[4,15,3,128]{3,2,1,0:T(4,128)S(1)} %get-tuple-element.265), kind=kLoop, calls=%fused_computation.15.clone.1 | loop fusion | flops 18677760 | bytes 8060928 | tf_op jit(solution)/shard_map/while/body/eval_jaxpr/vmap()/reduce_sum | solution.py:34
  170.5 2.9 gather_fusion.1
  175.7 6.5 %fusion.52 = (f32[4,15,128,128]{3,2,1,0:T(8,128)S(1)}, f32[4,15,128,128]{3,2,1,0:T(8,128)S(1)}) fusion(f32[4,3,128]{2,1,0:T(4,128)S(1)} %get-tuple-element.262, f32[4,15,3,128]{3,2,1,0:T(4,128)S(1)} %get-tuple-element.263, f32[4,3,128]{2,1,0:T(4,128)S(1)} %get-tuple-element.264, f32[4,15,3,128]{3,2,1,0:T(4,128)S(1)} %get-tuple-element.265), kind=kLoop, calls=%fused_computation.15.clone.1 | loop fusion | flops 18677760 | bytes 8060928 | tf_op jit(solution)/shard_map/while/body/eval_jaxpr/vmap()/reduce_sum | solution.py:34
  189.0 2.9 gather_fusion.1
  194.2 6.5 %fusion.52 = (f32[4,15,128,128]{3,2,1,0:T(8,128)S(1)}, f32[4,15,128,128]{3,2,1,0:T(8,128)S(1)}) fusion(f32[4,3,128]{2,1,0:T(4,128)S(1)} %get-tuple-element.262, f32[4,15,3,128]{3,2,1,0:T(4,128)S(1)} %get-tuple-element.263, f32[4,3,128]{2,1,0:T(4,128)S(1)} %get-tuple-element.264, f32[4,15,3,128]{3,2,1,0:T(4,128)S(1)} %get-tuple-element.265), kind=kLoop, calls=%fused_computation.15.clone.1 | loop fusion | flops 18677760 | bytes 8060928 | tf_op jit(solution)/shard_map/while/body/eval_jaxpr/vmap()/reduce_sum | solution.py:34
  207.6 2.9 gather_fusion.1
  212.8 6.5 %fusion.52 = (f32[4,15,128,128]{3,2,1,0:T(8,128)S(1)}, f32[4,15,128,128]{3,2,1,0:T(8,128)S(1)}) fusion(f32[4,3,128]{2,1,0:T(4,128)S(1)} %get-tuple-element.262, f32[4,15,3,128]{3,2,1,0:T(4,128)S(1)} %get-tuple-element.263, f32[4,3,128]{2,1,0:T(4,128)S(1)} %get-tuple-element.264, f32[4,15,3,128]{3,2,1,0:T(4,128)S(1)} %get-tuple-element.265), kind=kLoop, calls=%fused_computation.15.clone.1 | loop fusion | flops 18677760 | bytes 8060928 | tf_op jit(solution)/shard_map/while/body/eval_jaxpr/vmap()/reduce_sum | solution.py:34
  226.2 2.9 gather_fusion.1
  231.4 6.5 %fusion.52 = (f32[4,15,128,128]{3,2,1,0:T(8,128)S(1)}, f32[4,15,128,128]{3,2,1,0:T(8,128)S(1)}) fusion(f32[4,3,128]{2,1,0:T(4,128)S(1)} %get-tuple-element.262, f32[4,15,3,128]{3,2,1,0:T(4,128)S(1)} %get-tuple-element.263, f32[4,3,128]{2,1,0:T(4,128)S(1)} %get-tuple-element.264, f32[4,15,3,128]{3,2,1,0:T(4,128)S(1)} %get-tuple-element.265), kind=kLoop, calls=%fused_computation.15.clone.1 | loop fusion | flops 18677760 | bytes 8060928 | tf_op jit(solution)/shard_map/while/body/eval_jaxpr/vmap()/reduce_sum | solution.py:34
  244.7 2.9 gather_fusion.1
  249.9 6.5 %fusion.52 = (f32[4,15,128,128]{3,2,1,0:T(8,128)S(1)}, f32[4,15,128,128]{3,2,1,0:T(8,128)S(1)}) fusion(f32[4,3,128]{2,1,0:T(4,128)S(1)} %get-tuple-element.262, f32[4,15,3,128]{3,2,1,0:T(4,128)S(1)} %get-tuple-element.263, f32[4,3,128]{2,1,0:T(4,128)S(1)} %get-tuple-element.264, f32[4,15,3,128]{3,2,1,0:T(4,128)S(1)} %get-tuple-element.265), kind=kLoop, calls=%fused_computation.15.clone.1 | loop fusion | flops 18677760 | bytes 8060928 | tf_op jit(solution)/shard_map/while/body/eval_jaxpr/vmap()/reduce_sum | solution.py:34
  263.3 2.9 gather_fusion.1
  268.5 6.5 %fusion.52 = (f32[4,15,128,128]{3,2,1,0:T(8,128)S(1)}, f32[4,15,128,128]{3,2,1,0:T(8,128)S(1)}) fusion(f32[4,3,128]{2,1,0:T(4,128)S(1)} %get-tuple-element.262, f32[4,15,3,128]{3,2,1,0:T(4,128)S(1)} %get-tuple-element.263, f32[4,3,128]{2,1,0:T(4,128)S(1)} %get-tuple-element.264, f32[4,15,3,128]{3,2,1,0:T(4,128)S(1)} %get-tuple-element.265), kind=kLoop, calls=%fused_computation.15.clone.1 | loop fusion | flops 18677760 | bytes 8060928 | tf_op jit(solution)/shard_map/while/body/eval_jaxpr/vmap()/reduce_sum | solution.py:34
  281.9 2.9 gather_fusion.1
  287.1 6.5 %fusion.52 = (f32[4,15,128,128]{3,2,1,0:T(8,128)S(1)}, f32[4,15,128,128]{3,2,1,0:T(8,128)S(1)}) fusion(f32[4,3,128]{2,1,0:T(4,128)S(1)} %get-tuple-element.262, f32[4,15,3,128]{3,2,1,0:T(4,128)S(1)} %get-tuple-element.263, f32[4,3,128]{2,1,0:T(4,128)S(1)} %get-tuple-element.264, f32[4,15,3,128]{3,2,1,0:T(4,128)S(1)} %get-tuple-element.265), kind=kLoop, calls=%fused_computation.15.clone.1 | loop fusion | flops 18677760 | bytes 8060928 | tf_op jit(solution)/shard_map/while/body/eval_jaxpr/vmap()/reduce_sum | solution.py:34
  300.4 2.9 gather_fusion.1
  305.6 6.5 %fusion.52 = (f32[4,15,128,128]{3,2,1,0:T(8,128)S(1)}, f32[4,15,128,128]{3,2,1,0:T(8,128)S(1)}) fusion(f32[4,3,128]{2,1,0:T(4,128)S(1)} %get-tuple-element.262, f32[4,15,3,128]{3,2,1,0:T(4,128)S(1)} %get-tuple-element.263, f32[4,3,128]{2,1,0:T(4,128)S(1)} %get-tuple-element.264, f32[4,15,3,128]{3,2,1,0:T(4,128)S(1)} %get-tuple-element.265), kind=kLoop, calls=%fused_computation.15.clone.1 | loop fusion | flops 18677760 | bytes 8060928 | tf_op jit(solution)/shard_map/while/body/eval_jaxpr/vmap()/reduce_sum | solution.py:34
  319.0 2.9 gather_fusion.1
  324.2 6.5 %fusion.52 = (f32[4,15,128,128]{3,2,1,0:T(8,128)S(1)}, f32[4,15,128,128]{3,2,1,0:T(8,128)S(1)}) fusion(f32[4,3,128]{2,1,0:T(4,128)S(1)} %get-tuple-element.262, f32[4,15,3,128]{3,2,1,0:T(4,128)S(1)} %get-tuple-element.263, f32[4,3,128]{2,1,0:T(4,128)S(1)} %get-tuple-element.264, f32[4,15,3,128]{3,2,1,0:T(4,128)S(1)} %get-tuple-element.265), kind=kLoop, calls=%fused_computation.15.clone.1 | loop fusion | flops 18677760 | bytes 8060928 | tf_op jit(solution)/shard_map/while/body/eval_jaxpr/vmap()/reduce_sum | solution.py:34
  337.6 2.9 gather_fusion.1
  342.8 6.5 %fusion.52 = (f32[4,15,128,128]{3,2,1,0:T(8,128)S(1)}, f32[4,15,128,128]{3,2,1,0:T(8,128)S(1)}) fusion(f32[4,3,128]{2,1,0:T(4,128)S(1)} %get-tuple-element.262, f32[4,15,3,128]{3,2,1,0:T(4,128)S(1)} %get-tuple-element.263, f32[4,3,128]{2,1,0:T(4,128)S(1)} %get-tuple-element.264, f32[4,15,3,128]{3,2,1,0:T(4,128)S(1)} %get-tuple-element.265), kind=kLoop, calls=%fused_computation.15.clone.1 | loop fusion | flops 18677760 | bytes 8060928 | tf_op jit(solution)/shard_map/while/body/eval_jaxpr/vmap()/reduce_sum | solution.py:34
  356.1 2.9 gather_fusion.1
  361.3 6.5 %fusion.52 = (f32[4,15,128,128]{3,2,1,0:T(8,128)S(1)}, f32[4,15,128,128]{3,2,1,0:T(8,128)S(1)}) fusion(f32[4,3,128]{2,1,0:T(4,128)S(1)} %get-tuple-element.262, f32[4,15,3,128]{3,2,1,0:T(4,128)S(1)} %get-tuple-element.263, f32[4,3,128]{2,1,0:T(4,128)S(1)} %get-tuple-element.264, f32[4,15,3,128]{3,2,1,0:T(4,128)S(1)} %get-tuple-element.265), kind=kLoop, calls=%fused_computation.15.clone.1 | loop fusion | flops 18677760 | bytes 8060928 | tf_op jit(solution)/shard_map/while/body/eval_jaxpr/vmap()/reduce_sum | solution.py:34
  374.7 2.9 gather_fusion.1
  379.9 6.5 %fusion.52 = (f32[4,15,128,128]{3,2,1,0:T(8,128)S(1)}, f32[4,15,128,128]{3,2,1,0:T(8,128)S(1)}) fusion(f32[4,3,128]{2,1,0:T(4,128)S(1)} %get-tuple-element.262, f32[4,15,3,128]{3,2,1,0:T(4,128)S(1)} %get-tuple-element.263, f32[4,3,128]{2,1,0:T(4,128)S(1)} %get-tuple-element.264, f32[4,15,3,128]{3,2,1,0:T(4,128)S(1)} %get-tuple-element.265), kind=kLoop, calls=%fused_computation.15.clone.1 | loop fusion | flops 18677760 | bytes 8060928 | tf_op jit(solution)/shard_map/while/body/eval_jaxpr/vmap()/reduce_sum | solution.py:34
  393.3 2.9 gather_fusion.1
  398.5 6.5 %fusion.52 = (f32[4,15,128,128]{3,2,1,0:T(8,128)S(1)}, f32[4,15,128,128]{3,2,1,0:T(8,128)S(1)}) fusion(f32[4,3,128]{2,1,0:T(4,128)S(1)} %get-tuple-element.262, f32[4,15,3,128]{3,2,1,0:T(4,128)S(1)} %get-tuple-element.263, f32[4,3,128]{2,1,0:T(4,128)S(1)} %get-tuple-element.264, f32[4,15,3,128]{3,2,1,0:T(4,128)S(1)} %get-tuple-element.265), kind=kLoop, calls=%fused_computation.15.clone.1 | loop fusion | flops 18677760 | bytes 8060928 | tf_op jit(solution)/shard_map/while/body/eval_jaxpr/vmap()/reduce_sum | solution.py:34
  417.0 6.5 %fusion.52 = (f32[4,15,128,128]{3,2,1,0:T(8,128)S(1)}, f32[4,15,128,128]{3,2,1,0:T(8,128)S(1)}) fusion(f32[4,3,128]{2,1,0:T(4,128)S(1)} %get-tuple-element.262, f32[4,15,3,128]{3,2,1,0:T(4,128)S(1)} %get-tuple-element.263, f32[4,3,128]{2,1,0:T(4,128)S(1)} %get-tuple-element.264, f32[4,15,3,128]{3,2,1,0:T(4,128)S(1)} %get-tuple-element.265), kind=kLoop, calls=%fused_computation.15.clone.1 | loop fusion | flops 18677760 | bytes 8060928 | tf_op jit(solution)/shard_map/while/body/eval_jaxpr/vmap()/reduce_sum | solution.py:34
  432.3 5.8 %bitcast_add_fusion = f32[3,8192]{0,1:T(8,128)} fusion(f32[64,3,128]{1,2,0:T(8,128)} %copy.190, f32[1,1,3,8192]{2,3,1,0:T(8,128)} %copy.191), kind=kLoop, calls=%fused_computation.45 | loop fusion | flops 24576 | bytes 294912 | tf_op jit(solution)/shard_map/add | solution.py:125
  438.1 7.1 %scatter_fusion = f32[3,8192]{0,1:T(8,128)} fusion(f32[3,8192]{0,1:T(8,128)} %bitcast_add_fusion, s32[512]{0:T(512)S(1)} %bitcast.173, f32[512,3]{1,0:T(8,128)S(1)} %copy.202), kind=kCustom, calls=%fused_computation.6 | custom fusion | flops 1536 | bytes 20480 | tf_op jit(solution)/shard_map/scatter-add | solution.py:117
  445.2 8.6 %fusion.16 = (f32[1,1,3,8192]{2,3,1,0:T(8,128)}, f32[1,1,3,8192]{2,3,1,0:T(8,128)}) fusion(f32[3,8192]{0,1:T(8,128)} %scatter_fusion, f32[1,1,3,8192]{2,3,1,0:T(8,128)} %copy.185, f32[1,1,3,8192]{2,3,1,0:T(8,128)} %copy.184), kind=kLoop, calls=%fused_computation.48 | loop fusion | flops 98304 | bytes 491520 | tf_op jit(solution)/shard_map/broadcast_in_dim | solution.py:131
  453.8 3.5 copy.207
  457.3 3.5 copy.208
  (353 shorter events, 185.5 us)
Async XLA Ops:
  0.6 37.4 %copy-start = (f32[24,24]{1,0:T(8,128)S(1)}, f32[24,24]{1,0:T(8,128)}, u32[]{:S(2)}) copy-start(f32[24,24]{1,0:T(8,128)} %param.29) | copy-start | bytes 6916
  0.6 34.3 %copy-start.5 = (f32[1,1,8192]{2,1,0:T(1,128)S(1)}, f32[1,1,8192]{2,1,0:T(1,128)}, u32[]{:S(2)}) copy-start(f32[1,1,8192]{2,1,0:T(1,128)} %param.20) | copy-start | bytes 98308
  0.7 34.3 %copy-start.4 = (f32[1,1,8192]{2,1,0:T(1,128)S(1)}, f32[1,1,8192]{2,1,0:T(1,128)}, u32[]{:S(2)}) copy-start(f32[1,1,8192]{2,1,0:T(1,128)} %param.21) | copy-start | bytes 98308
  0.7 34.3 %copy-start.3 = (f32[1,1,3,8192]{3,1,2,0:T(1,128)S(1)}, f32[1,1,3,8192]{3,1,2,0:T(1,128)}, u32[]{:S(2)}) copy-start(f32[1,1,3,8192]{3,1,2,0:T(1,128)} %param.17) | copy-start | bytes 294916
  0.7 34.3 %copy-start.2 = (f32[1,1,3,8192]{3,1,2,0:T(1,128)S(1)}, f32[1,1,3,8192]{3,1,2,0:T(1,128)}, u32[]{:S(2)}) copy-start(f32[1,1,3,8192]{3,1,2,0:T(1,128)} %param.18) | copy-start | bytes 294916
  0.7 11.4 %copy-start.14 = (s32[1,1,64,8]{2,3,1,0:T(8,128)S(1)}, s32[1,1,64,8]{2,3,1,0:T(8,128)}, u32[]{:S(2)}) copy-start(s32[1,1,64,8]{2,3,1,0:T(8,128)} %param.31) | copy-start | bytes 6148
  0.7 11.6 %copy-start.9 = (s32[1,1,8,128]{3,2,1,0:T(8,128)S(1)}, s32[1,1,8,128]{3,2,1,0:T(8,128)}, u32[]{:S(2)}) copy-start(s32[1,1,8,128]{3,2,1,0:T(8,128)} %param.27) | copy-start | bytes 12292
  0.7 30.0 %copy-start.1 = (s32[1,1,32]{2,1,0:T(1,128)S(1)}, s32[1,1,32]{2,1,0:T(1,128)}, u32[]{:S(2)}) copy-start(s32[1,1,32]{2,1,0:T(1,128)} %param.24) | copy-start | bytes 388
  0.7 30.8 %copy-start.12 = (f32[1,1,3,512]{3,1,2,0:T(1,128)S(1)}, f32[1,1,3,512]{3,1,2,0:T(1,128)}, u32[]{:S(2)}) copy-start(f32[1,1,3,512]{3,1,2,0:T(1,128)} %param.25) | copy-start | bytes 18436
  0.7 31.0 %copy-start.15 = (s32[1,1,64,8]{2,3,1,0:T(8,128)S(1)}, s32[1,1,64,8]{2,3,1,0:T(8,128)}, u32[]{:S(2)}) copy-start(s32[1,1,64,8]{2,3,1,0:T(8,128)} %param.30) | copy-start | bytes 6148
  2.0 36.0 %copy-start.16 = (f32[1,1,128]{2,1,0:T(1,128)S(1)}, f32[1,1,128]{2,1,0:T(1,128)}, u32[]{:S(2)}) copy-start(f32[1,1,128]{2,1,0:T(1,128)} %param.28) | copy-start | bytes 1540
  2.0 64.5 %copy-start.11 = (s32[1,1,64,15]{2,1,3,0:T(1,128)S(1)}, s32[1,1,64,15]{2,1,3,0:T(1,128)}, u32[]{:S(2)}) copy-start(s32[1,1,64,15]{2,1,3,0:T(1,128)} %param.23) | copy-start | bytes 11524
  2.0 65.2 %copy-start.7 = (f32[1,1,3,8192]{3,1,2,0:T(1,128)S(1)}, f32[1,1,3,8192]{3,1,2,0:T(1,128)}, u32[]{:S(2)}) copy-start(f32[1,1,3,8192]{3,1,2,0:T(1,128)} %param.22) | copy-start | bytes 294916
  2.0 32.9 %collective-permute-start = (f32[1,1,8,8192]{3,1,2,0:T(1,128)S(1)}, f32[1,1,8,8192]{3,1,2,0:T(1,128)S(1)}, u32[]{:S(2)}, u32[]{:S(2)}) collective-permute-start(f32[1,1,8,8192]{3,1,2,0:T(1,128)S(1)} %pad_maximum_fusion.5), channel_id=1, source_target_pairs={{0,1},{1,2},{2,3},{4,5},{5,6},{6,7},{8,9},{9,10},{10,11},{12,13},{... | collective-permute-start | bytes 786440 | tf_op jit(solution)/shard_map/ppermute | solution.py:19
  6.8 28.2 %collective-permute-start.1 = (f32[1,1,8,8192]{3,1,2,0:T(1,128)S(1)}, f32[1,1,8,8192]{3,1,2,0:T(1,128)S(1)}, u32[]{:S(2)}, u32[]{:S(2)}) collective-permute-start(f32[1,1,8,8192]{3,1,2,0:T(1,128)S(1)} %pad_maximum_fusion.5), channel_id=1, source_target_pairs={{1,0},{2,1},{3,2},{5,4},{6,5},{7,6},{9,8},{10,9},{11,10},{13,12},{... | collective-permute-start | bytes 786440 | tf_op jit(solution)/shard_map/ppermute | solution.py:20
  16.6 64.3 %all-to-all-start = ((f32[3,64,8]{2,0,1:T(4,128)}), f32[3,64,8]{2,0,1:T(4,128)S(1)}, u32[]{:S(2)}, u32[]{:S(2)}) async-start(f32[3,64,8]{2,0,1:T(4,128)} %copy.193), calls=%async_computation | async-start | bytes 262144 | tf_op jit(solution)/shard_map/all_to_all | solution.py:113
  31.8 39.8 %copy-start.8 = (f32[1,1,3,8192]{3,1,2,0:T(1,128)S(1)}, f32[1,1,3,8192]{3,1,2,0:T(1,128)}, u32[]{:S(2)}) copy-start(f32[1,1,3,8192]{3,1,2,0:T(1,128)} %param.19) | copy-start | bytes 294916
  35.7 29.9 %collective-permute-start.2 = (f32[1,3,8,8192]{3,1,2,0:T(4,128)S(1)}, f32[1,3,8,8192]{3,1,2,0:T(4,128)}, u32[]{:S(2)}, u32[]{:S(2)}) collective-permute-start(f32[1,3,8,8192]{3,1,2,0:T(4,128)S(1)} %pad_maximum_fusion.1), channel_id=1, source_target_pairs={{0,4},{4,8},{8,12},{12,16},{16,20},{20,24},{24,28},{28,32},{32,36}... | collective-permute-start | bytes 2359304 | tf_op jit(solution)/shard_map/ppermute | solution.py:27
  38.9 66.5 %collective-permute-start.4 = (f32[1,3,8,8192]{3,1,2,0:T(4,128)S(1)}, f32[1,3,8,8192]{3,1,2,0:T(4,128)}, u32[]{:S(2)}, u32[]{:S(2)}) collective-permute-start(f32[1,3,8,8192]{3,1,2,0:T(4,128)S(1)} %pad_maximum_fusion.1), channel_id=1, source_target_pairs={{0,252},{4,0},{8,4},{12,8},{16,12},{20,16},{24,20},{28,24},{32,28}... | collective-permute-start | bytes 2359304 | tf_op jit(solution)/shard_map/ppermute | solution.py:27
  65.6 41.1 %collective-permute-start.3 = (f32[1,3,8,8192]{3,1,2,0:T(4,128)}, f32[1,3,8,8192]{3,1,2,0:T(4,128)}, u32[]{:S(2)}, u32[]{:S(2)}) collective-permute-start(f32[1,3,8,8192]{3,1,2,0:T(4,128)} %collective-permute-done.2), channel_id=1, source_target_pairs={{0,4},{4,8},{8,12},{12,16},{16,20},{20,24},{24,28},{28,32},{32,36}... | collective-permute-start | bytes 2359304 | tf_op jit(solution)/shard_map/ppermute | solution.py:27
  65.6 8.7 %copy-start.10 = (s32[512,1]{0,1:T(1,128)}, s32[512,1]{0,1:T(1,128)S(1)}, u32[]{:S(2)}) copy-start(s32[512,1]{0,1:T(1,128)S(1)} %compare_select_fusion.4) | copy-start | bytes 6148
  67.2 7.3 %copy-start.13 = (f32[1,1,3,512]{3,1,2,0:T(1,128)S(1)}, f32[1,1,3,512]{3,1,2,0:T(1,128)}, u32[]{:S(2)}) copy-start(f32[1,1,3,512]{3,1,2,0:T(1,128)} %param.26) | copy-start | bytes 18436
  82.5 21.5 %all-to-all-start.1 = ((f32[3,64,8]{2,0,1:T(4,128)}), f32[3,64,8]{2,0,1:T(4,128)}, u32[]{:S(2)}, u32[]{:S(2)}) async-start(f32[3,64,8]{2,0,1:T(4,128)} %copy.199), calls=%async_computation.1 | async-start | bytes 262144 | tf_op jit(solution)/shard_map/all_to_all | solution.py:116
  105.4 22.8 %collective-permute-start.5 = (f32[1,3,8,8192]{3,1,2,0:T(4,128)}, f32[1,3,8,8192]{3,1,2,0:T(4,128)S(1)}, u32[]{:S(2)}, u32[]{:S(2)}) collective-permute-start(f32[1,3,8,8192]{3,1,2,0:T(4,128)} %collective-permute-done.4), channel_id=1, source_target_pairs={{0,252},{4,0},{8,4},{12,8},{16,12},{20,16},{24,20},{28,24},{32,28}... | collective-permute-start | bytes 2359304 | tf_op jit(solution)/shard_map/ppermute | solution.py:27
  128.5 4.1 copy-start.6
where the time goes:
time: 466 us; the launch traced here: 461 us
  other arithmetic  246 us (53%)
  local copies, waits for them, and re-layouts  129 us (28%)
  waiting for transfers between devices  43.4 us (9%)
  starting transfers between devices  39.8 us (9%)
    reduce_sum x16, other arithmetic, pair_force(): now_sq = jnp.sum(bond_now * bond_now, axis=1)  104 us
    gather x16, local copies, waits for them, and re-layouts, fetch(): return window[name_row // tile_count, :, name_row % tile_count]  46.7 us
    mul x16, other arithmetic, pair_force(): bond_scale * stiffness * intact * jnp.exp(-ref_sq / horizon_sq) * strain  42 us
    reduce_sum x16, other arithmetic, pair_force(): return jnp.sum(coeff[:, None] * bond_now, axis=(0, 3))  41.3 us
    ppermute x4, waiting for transfers between devices, from_behind(): lax.ppermute(shard, axis, [(i, (i + by) % length) for i in range(length)])  36.8 us
    gather x16, local copies, waits for them, and re-layouts, tile_force(): return pair_force(own_field[:, tile_id], fetch(name_row), alive_row)  24.1 us
    unnamed x49, local copies, waits for them, and re-layouts  22.7 us
    all_to_all x1, starting transfers between devices, on_device(): lax.all_to_all(rim_values, 'blk', split_axis=1, concat_axis=1, tiled=True)  14 us
  transfers between devices with their start and end apart: 8, of which 3 were waited for; matrix products, arithmetic and copies ran while one was open for 9% of the time, Pallas kernels for 0%

commit v1 on v0

v1 whole, which is shorter than its diff:
```python
import math
import jax
import jax.numpy as jnp
from jax import lax
from jax.experimental import pallas as pl
from jax.experimental.pallas import tpu as pltpu
from jax.sharding import PartitionSpec as P

TILE = 128
log_scale = math.log2(math.e) / 9.0
force_scale = -0.125 * log_scale * math.exp(1.0 / 9.0)
f32 = jnp.float32
bf16 = jnp.bfloat16
UNROLL = 8
OWN_UNROLL = 1
spring = 0.5
time_step = 0.5


def split3(value):
    high = value.astype(bf16).astype(f32)
    rest = value - high
    middle = rest.astype(bf16).astype(f32)
    return high, middle, (rest - middle)


def point_terms(v):
    row = lax.broadcasted_iota(jnp.int32, v.shape, 0)
    disp = pltpu.roll(v, 5, 0)
    now = v + disp
    first = row < 3
    ref_norm = jnp.sum(jnp.where(first, v * v, 0.0), axis=0, keepdims=True)
    growth = jnp.sum(jnp.where(first, disp * (v + now), 0.0), axis=0, keepdims=True)
    return row, disp, now, ref_norm, growth


def own_kernel(field_ref, lhs_ref):
    def one_tile(tile, carry):
        v = field_ref[:, pl.ds(pl.multiple_of(tile * TILE, TILE), TILE)]
        row, disp, now, ref_norm, growth = point_terms(v)
        row16 = lax.broadcasted_iota(jnp.int32, (16, TILE), 0)
        coef_ref = jnp.where(row < 3, 2.0 * log_scale * v, jnp.where(row == 6, -log_scale, 0.0))
        coef_now = jnp.where(
            row < 3,
            -2.0 * disp,
            jnp.where(row < 6, -2.0 * pltpu.roll(now, 3, 0), jnp.where(row == 7, 1.0, 0.0)),
        )
        for place, coef, alone in (
            (0, coef_ref, -log_scale * (1.0 + ref_norm)),
            (1, coef_now, growth),
        ):
            high, middle, low = split3(coef)
            a, b, c = split3(alone)
            const = jnp.where(row16 == 0, a, jnp.where(row16 == 1, b, jnp.where(row16 == 2, c, 0.0)))
            rows = jnp.concatenate([high, high, middle, middle, high, low, const], axis=0)
            lhs_ref[tile, pl.ds(place * TILE, TILE), :] = rows.T.astype(bf16)
        return carry

    lax.fori_loop(0, field_ref.shape[1] // TILE, one_tile, 0, unroll=OWN_UNROLL)


def own_table(field):
    tiles = field.shape[1] // TILE
    return pl.pallas_call(
        own_kernel,
        out_shape=jax.ShapeDtypeStruct((tiles, 2 * TILE, 64), bf16),
        name="own_table",
        cost_estimate=pl.CostEstimate(flops=8_000_000_000, transcendentals=0, bytes_accessed=4_500_000),
    )(field)


def fill_table(field_ref, table_ref, place, chunk):
    def one(step, carry):
        lanes = pl.ds(pl.multiple_of(step * chunk, chunk), chunk)
        v = field_ref[:, lanes]
        row, disp, now, ref_norm, growth = point_terms(v)
        terms = jnp.where(row < 6, v, jnp.where(row == 6, ref_norm, growth))
        high, middle, low = split3(terms)
        table_ref[place, 0:16, lanes] = jnp.concatenate([high, middle], axis=0).astype(bf16)
        table_ref[place, 16:32, lanes] = jnp.concatenate([low, high], axis=0).astype(bf16)
        whole = 1.0 - v[6:7]
        stiff = v[7:8]
        spread = jnp.where(row < 3, now, jnp.where(row < 6, pltpu.roll(now, 3, 0), 1.0))
        weight = whole * jnp.where((row < 3) | (row == 6), 1.0, stiff)
        sums = spread * weight
        q_high = sums.astype(bf16).astype(f32)
        table_ref[place, 32:48, lanes] = jnp.concatenate([q_high, sums - q_high], axis=0).astype(bf16)
        return carry

    lax.fori_loop(0, field_ref.shape[1] // chunk, one, 0)


def make_stage_kernel(slots, first):
    count = len(slots)
    group = 2 if count % 2 == 0 else 3

    def kernel(names_ref, flags_ref, lhs_ref, *refs):
        block_refs = refs[:count]
        rest = refs[count:]
        if not first:
            before_ref, rest = rest[0], rest[1:]
        out_ref, table_ref = rest
        for place, ref in enumerate(block_refs):
            fill_table(ref, table_ref, place, 512)
        ones = jnp.ones((16, TILE), bf16)

        def one_tile(tile, carry):
            lhs = lhs_ref[tile]
            word = flags_ref[tile // 2]
            acc = None
            for start in range(0, count, group):
                rhs, sums = [], []
                for place in range(start, min(start + group, count)):
                    slot = slots[place]
                    name = names_ref[tile, slot]
                    where = (place // 3) * 3 + (name // 64) % 3
                    lanes = pl.ds(pl.multiple_of((name % 64) * TILE, TILE), TILE)
                    top = table_ref[where, 0:16, lanes]
                    low = table_ref[where, 16:32, lanes]
                    alive = 1 - (lax.shift_right_logical(word, (tile % 2) * 15 + slot) & 1)
                    rhs.append(jnp.concatenate([top, top, low, ones], axis=0))
                    q = table_ref[where, 32:48, lanes]
                    sums.append(jnp.where(alive == 1, q, jnp.zeros_like(q)))
                rhs = jnp.concatenate(rhs, axis=1)
                sums = jnp.concatenate(sums, axis=1)
                both = jnp.dot(lhs, rhs, preferred_element_type=f32)
                stretch = both[:TILE]
                pull = both[TILE:] * jnp.exp2(stretch) / stretch
                high = pull.astype(bf16)
                low = (pull - high.astype(f32)).astype(bf16)
                dims = (((1,), (1,)), ((), ()))
                part = lax.dot_general(sums, high, dims, preferred_element_type=f32)
                part += lax.dot_general(sums, low, dims, preferred_element_type=f32)
                acc = part if acc is None else acc + part
            acc = acc[0:8] + acc[8:16]
            lanes = pl.ds(pl.multiple_of(tile * TILE, TILE), TILE)
            if not first:
                acc += before_ref[:, lanes]
            out_ref[:, lanes] = acc
            return carry

        lax.fori_loop(0, lhs_ref.shape[0], one_tile, 0, unroll=UNROLL)

    return kernel


def stage(names, flags, lhs, blocks, before, slots):
    first = before is None
    points = blocks[0].shape[1]
    smem = pl.BlockSpec(memory_space=pltpu.SMEM)
    vmem = pl.BlockSpec(memory_space=pltpu.VMEM)
    args = [names, flags, lhs, *blocks] + ([] if first else [before])
    return pl.pallas_call(
        make_stage_kernel(slots, first),
        out_shape=jax.ShapeDtypeStruct((8, points), f32),
        in_specs=[smem, smem] + [vmem] * (len(args) - 2),
        out_specs=vmem,
        scratch_shapes=[pltpu.VMEM((len(blocks), 48, points), bf16)],
        name="bond_stage",
        cost_estimate=pl.CostEstimate(flops=20_000_000_000, transcendentals=0, bytes_accessed=6_000_000),
    )(*args)


def finish_force(sums, field):
    now = field[0:3] + field[3:6]
    whole = 1.0 - field[6:7]
    inner = sums[0:3] - now * sums[6:7]
    outer = sums[3:6] - now * sums[7:8]
    return force_scale * whole * (field[7:8] * inner + outer)


def shift_layer(value, by):
    size = lax.axis_size("layer")
    pairs = [(i, i + by) for i in range(size) if 0 <= i + by < size]
    return lax.ppermute(value, "layer", pairs)


def shift_sector(value, by):
    size = lax.axis_size("blk")
    return lax.ppermute(value, "blk", [(i, (i + by) % size) for i in range(size)])


def layered(value):
    return [shift_layer(value, 1), value, shift_layer(value, -1)]


def on_device(
    ref_pos,
    disk_disp,
    disk_vel,
    damage,
    modulus,
    body_load,
    nbr_tiles,
    break_flags,
    blade_disp,
    blade_vel,
    elem_nodes,
    elem_modulus,
    elem_stiff,
    root_nodes,
    rim_points,
):
    disk_now = disk_disp[0, 0]
    blade_now = blade_disp[0, 0]
    field = jnp.concatenate([ref_pos[0, 0], disk_now, damage[0], modulus[0]], axis=0)
    names = nbr_tiles[0, 0]
    flags = break_flags[0, 0]
    behind = shift_sector(field, 1)
    ahead = shift_sector(field, -1)
    near = layered(field)
    far_behind = shift_sector(behind, 1)
    far_ahead = shift_sector(ahead, -1)
    rim_flat = rim_points[0, 0].reshape(-1)
    root_flat = root_nodes[0, 0].reshape(-1)
    rim_values = disk_now[:, rim_flat]
    root_values = blade_now[:, root_flat]
    swapped = lax.all_to_all(
        jnp.concatenate([rim_values, root_values], axis=0), "blk", split_axis=1, concat_axis=1, tiled=True
    )
    middle = layered(behind) + layered(ahead)
    outer = layered(far_behind) + layered(far_ahead)
    lhs = own_table(field)
    sums = stage(names, flags, lhs, near, None, (6, 7, 8))
    sums = stage(names, flags, lhs, middle, sums, (3, 4, 5, 9, 10, 11))
    sums = stage(names, flags, lhs, outer, sums, (0, 1, 2, 12, 13, 14))
    bond_force = finish_force(sums, field)
    loads = spring * (swapped[0:3] - root_values)
    coupling = jnp.zeros_like(blade_now).at[:, root_flat].add(loads)
    returned = spring * (rim_values - swapped[3:6])
    reaction = jnp.zeros_like(disk_now).at[:, rim_flat].add(-returned)
    connect = elem_nodes[0, 0]
    elem_count = connect.shape[1]
    gathered = blade_now[:, connect].reshape(24, elem_count)
    elem_force = elem_modulus[0, 0][None, :] * jnp.dot(
        elem_stiff, gathered, precision=lax.Precision.HIGHEST, preferred_element_type=jnp.float32
    )
    internal = jnp.zeros_like(blade_now).at[:, connect.reshape(-1)].add(-elem_force.reshape(3, -1))
    disk_vel_new = disk_vel[0, 0] + time_step * (bond_force + body_load[0, 0] + reaction)
    disk_disp_new = disk_now + time_step * disk_vel_new
    blade_vel_new = blade_vel[0, 0] + time_step * (internal + coupling)
    blade_disp_new = blade_now + time_step * blade_vel_new
    return (
        disk_disp_new[None, None],
        disk_vel_new[None, None],
        blade_disp_new[None, None],
        blade_vel_new[None, None],
    )


def solution(mesh):
    in_specs = (
        P("blk", "layer", None, None),
        P("blk", "layer", None, None),
        P("blk", "layer", None, None),
        P("blk", "layer", None),
        P("blk", "layer", None),
        P("blk", "layer", None, None),
        P("blk", "layer", None, None),
        P("blk", "layer", None),
        P("blk", "layer", None, None),
        P("blk", "layer", None, None),
        P("blk", "layer", None, None),
        P("blk", "layer", None),
        P(),
        P("blk", "layer", None, None),
        P("blk", "layer", None, None),
    )
    out_specs = (
        P("blk", "layer", None, None),
        P("blk", "layer", None, None),
        P("blk", "layer", None, None),
        P("blk", "layer", None, None),
    )
    return jax.shard_map(
        on_device, mesh=mesh, in_specs=in_specs, out_specs=out_specs, check_vma=False
    )
```

time: 466 us -> 172 us (0.37); the launches traced: 461 us -> 172 us
  other arithmetic: 246 us -> 18.2 us
  local copies, waits for them, and re-layouts: 129 us -> 26.6 us
  Pallas kernels: 0 us -> 69.5 us
  waiting for transfers between devices: 43.4 us -> 0.04 us
  starting transfers between devices: 39.8 us -> 55.9 us
    reduce_sum x32 -> x0, other arithmetic: 146 us -> none  [the longest x16 104 us: pair_force(): now_sq = jnp.sum(bond_now * bond_now, axis=1)]
    gather x35 -> x2, local copies, waits for them, and re-layouts: 73.3 us -> 1.14 us  [on_device(): root_values = blade_now[:, root_flat]]
    pallas_call x0 -> x4, Pallas kernels: none -> 69.5 us  [the longest x3 59.3 us: stage(): pl.pallas_call(make_stage_kernel(slots, first), out_shape=jax.ShapeDtypeS...]
    mul x34 -> x1, other arithmetic: 42.9 us -> 0.04 us  [finish_force(): return force_scale * whole * (field[7:8] * inner + outer)]
    ppermute x6 -> x14, waiting for transfers between devices: 36.8 us -> 0.04 us  [the longest x10 0.03 us: shift_layer(): return lax.ppermute(value, 'layer', pairs)]
    ppermute x6 -> x14, starting transfers between devices: 15.3 us -> 46.5 us  [the longest x10 29.3 us: shift_layer(): return lax.ppermute(value, 'layer', pairs)]
    concatenate x35 -> x2, other arithmetic: 24.3 us -> 0.91 us  [the longest x1 0.9 us: on_device(): jnp.concatenate([ref_pos[0, 0], disk_now, damage[0], modulus[0]], axis=0)]
    unnamed x49 -> x66, local copies, waits for them, and re-layouts: 22.7 us -> 7.52 us
  transfers between devices with their start and end apart: 8 -> 15, of which waited for: 3 -> 0; matrix products, arithmetic and copies ran while one was open for 9% -> 14% of each run, Pallas kernels for 0% -> 28%
where the time goes in v1:
time: 172 us
  Pallas kernels  69.5 us (40%)
  starting transfers between devices  55.9 us (32%)
  local copies, waits for them, and re-layouts  26.6 us (15%)
  other arithmetic  18.2 us (11%)
    pallas_call x3, Pallas kernels, stage(): pl.pallas_call(make_stage_kernel(slots, first), out_shape=jax.ShapeDtypeS...  59.3 us
    ppermute x10, starting transfers between devices, shift_layer(): return lax.ppermute(value, 'layer', pairs)  29.3 us
    ppermute x4, starting transfers between devices, shift_sector(): lax.ppermute(value, 'blk', [(i, (i + by) % size) for i in range(size)])  17.2 us
    pallas_call x1, Pallas kernels, own_table(): pl.pallas_call(own_kernel, out_shape=jax.ShapeDtypeStruct((tiles, 2 * TIL...  10.2 us
    all_to_all x1, starting transfers between devices, on_device(): lax.all_to_all(jnp.concatenate([rim_values, root_values], axis=0), 'blk',...  9.46 us
    unnamed x66, local copies, waits for them, and re-layouts  7.52 us
    scatter-add x1, other arithmetic, on_device(): reaction = jnp.zeros_like(disk_now).at[:, rim_flat].add(-returned)  7.21 us
    scatter-add x1, other arithmetic, on_device(): jnp.zeros_like(blade_now).at[:, connect.reshape(-1)]  6.13 us
  transfers between devices with their start and end apart: 15, of which 0 were waited for; matrix products, arithmetic and copies ran while one was open for 14% of the time, Pallas kernels for 28%

profile of v1, /device:TPU:1, one launch (start us, length us, event | category | flops | bytes accessed | tf_op | source)
XLA Modules:
  0.0 171.8 jit_solution(3529878607102978593)
XLA Ops:
  0.7 1.1 copy_bitcast_fusion
  1.8 0.9 pad_maximum_fusion.field_ref.refs_1_
  2.7 5.1 %collective-permute-start.13 = (f32[8,8192]{1,0:T(8,128)S(1)}, f32[8,8192]{1,0:T(8,128)S(1)}, u32[]{:S(2)}, u32[]{:S(2)}) collective-permute-start(f32[8,8192]{1,0:T(8,128)S(1)} %pad_maximum_fusion.field_ref.refs_1_), channel_id=1, source_target_pairs={{1,0},{2,1},{3,2},{5,4},{6,5},{7,6},{9,8},{10,9},{11,10},{13,12},{... | collective-permute-start | bytes 786440 | tf_op jit(solution)/shard_map/ppermute | solution.py:175
  7.9 1.9 %collective-permute-start.12 = (f32[8,8192]{1,0:T(8,128)S(1)}, f32[8,8192]{1,0:T(8,128)}, u32[]{:S(2)}, u32[]{:S(2)}) collective-permute-start(f32[8,8192]{1,0:T(8,128)S(1)} %pad_maximum_fusion.field_ref.refs_1_), channel_id=1, source_target_pairs={{0,1},{1,2},{2,3},{4,5},{5,6},{6,7},{8,9},{9,10},{10,11},{12,13},{... | collective-permute-start | bytes 786440 | tf_op jit(solution)/shard_map/ppermute | solution.py:175
  9.8 9.8 %collective-permute-start.4 = (f32[8,8192]{1,0:T(8,128)S(1)}, f32[8,8192]{1,0:T(8,128)S(1)}, u32[]{:S(2)}, u32[]{:S(2)}) collective-permute-start(f32[8,8192]{1,0:T(8,128)S(1)} %pad_maximum_fusion.field_ref.refs_1_), channel_id=1, source_target_pairs={{0,252},{4,0},{8,4},{12,8},{16,12},{20,16},{24,20},{28,24},{32,28}... | collective-permute-start | bytes 786440 | tf_op jit(solution)/shard_map/ppermute | solution.py:180
  19.6 2.7 %copy.81 = f32[3,8192]{0,1:T(8,128)} copy(f32[3,8192]{1,0:T(4,128)S(1)} %get-tuple-element.33) | data formatting | bytes 196608 | tf_op jit(solution)/shard_map/squeeze | solution.py:204
  22.7 0.1 copy.82
  22.8 1.0 gather_fusion.1
  24.0 3.2 %gather_fusion = f32[512,3]{1,0:T(8,128)S(1)} fusion(f32[3,8192]{0,1:T(8,128)} %copy.81, s32[1024]{0:T(1024)S(1)} %pad_clamp_fusion.1), kind=kCustom, calls=%fused_computation | custom fusion | bytes 14336 | tf_op jit(solution)/shard_map/gather | solution.py:216
  27.5 0.8 copy.86
  28.3 9.5 %all-to-all-start = ((f32[6,64,8]{2,0,1:T(8,128)}), f32[6,64,8]{2,0,1:T(8,128)S(1)}, u32[]{:S(2)}, u32[]{:S(2)}) async-start(f32[6,64,8]{2,0,1:T(8,128)} %copy.86), calls=%async_computation | async-start | bytes 524288 | tf_op jit(solution)/shard_map/all_to_all | solution.py:218
  37.9 10.2 %own_table.1.lhs_ref = bf16[64,256,64]{2,1,0:T(8,128)(2,1)} custom-call(f32[8,8192]{1,0:T(8,128)} %copy-done.3), custom_call_target="tpu_custom_call" | custom-call | flops 8000000000 | bytes 4500000 | tf_op jit(solution)/shard_map/own_table/pallas_call | solution.py:64
  48.1 2.8 %gather_fusion.2 = f32[1024,3]{1,0:T(8,128)S(1)} fusion(f32[3,512]{0,1:T(8,128)S(1)} %bitcast.102, s32[1024]{0:T(1024)S(1)} %fusion.24), kind=kCustom, calls=%fused_computation.2 | custom fusion | bytes 28672 | tf_op jit(solution)/shard_map/gather | solution.py:234
  50.9 0.2 copy.91
  51.1 0.2 fusion.1
  51.3 0.7 copy.79
  52.0 0.1 copy.90
  52.2 0.2 copy.92
  52.4 6.1 %scatter_custom_fusion.1 = f32[3,512]{0,1:T(8,128)S(1)} fusion(s32[1024]{0:T(1024)S(1)} %bitcast.120, f32[3,1024]{0,1:T(8,128)S(1)} %copy.92, f32[]{:T(128)} %constant.0.clone.1), kind=kCustom, calls=%fused_computation.9 | custom fusion | flops 3072 | bytes 530436 | tf_op jit(solution)/shard_map/scatter-add | solution.py:238
  58.6 0.4 copy.93
  59.1 2.3 %scatter_custom_fusion.2 = f32[3,512]{0,1:T(8,128)S(1)} fusion(s32[512]{0:T(512)S(1)} %bitcast.119, f32[3,64,8]{0,2,1:T(8,128)S(1)} %copy.93, f32[]{:T(128)} %constant.0.clone.1, f32[]{:T(128)} %constant.12.clone.1, f32[512,3]{1,0:T(8,128)S(1)} %gather_fusion.1), kind=kCustom, calls=%fused_computation.12 | custom fusion | flops 4608 | bytes 530440 | tf_op jit(solution)/shard_map/scatter-add | solution.py:229
  61.5 2.8 %collective-permute-start.11 = (f32[8,8192]{1,0:T(8,128)S(1)}, f32[8,8192]{1,0:T(8,128)S(1)}, u32[]{:S(2)}, u32[]{:S(2)}) collective-permute-start(f32[8,8192]{1,0:T(8,128)S(1)} %collective-permute-done.4.refs_4_), channel_id=1, source_target_pairs={{1,0},{2,1},{3,2},{5,4},{6,5},{7,6},{9,8},{10,9},{11,10},{13,12},{... | collective-permute-start | bytes 786440 | tf_op jit(solution)/shard_map/ppermute | solution.py:175
  64.3 0.7 copy.97
  65.0 0.7 copy.96
  65.7 0.4 copy.87
  66.2 2.8 %collective-permute-start.10 = (f32[8,8192]{1,0:T(8,128)S(1)}, f32[8,8192]{1,0:T(8,128)S(1)}, u32[]{:S(2)}, u32[]{:S(2)}) collective-permute-start(f32[8,8192]{1,0:T(8,128)S(1)} %collective-permute-done.4.refs_4_), channel_id=1, source_target_pairs={{0,1},{1,2},{2,3},{4,5},{5,6},{6,7},{8,9},{9,10},{10,11},{12,13},{... | collective-permute-start | bytes 786440 | tf_op jit(solution)/shard_map/ppermute | solution.py:175
  69.0 7.1 %collective-permute-start.5 = (f32[8,8192]{1,0:T(8,128)S(1)}, f32[8,8192]{1,0:T(8,128)S(1)}, u32[]{:S(2)}, u32[]{:S(2)}) collective-permute-start(f32[8,8192]{1,0:T(8,128)S(1)} %collective-permute-done.4.refs_4_), channel_id=1, source_target_pairs={{0,252},{4,0},{8,4},{12,8},{16,12},{20,16},{24,20},{28,24},{32,28}... | collective-permute-start | bytes 786440 | tf_op jit(solution)/shard_map/ppermute | solution.py:180
  76.1 2.1 %collective-permute-start.9 = (f32[8,8192]{1,0:T(8,128)S(1)}, f32[8,8192]{1,0:T(8,128)S(1)}, u32[]{:S(2)}, u32[]{:S(2)}) collective-permute-start(f32[8,8192]{1,0:T(8,128)S(1)} %collective-permute-done.refs_1_), channel_id=1, source_target_pairs={{1,0},{2,1},{3,2},{5,4},{6,5},{7,6},{9,8},{10,9},{11,10},{13,12},{... | collective-permute-start | bytes 786440 | tf_op jit(solution)/shard_map/ppermute | solution.py:175
  78.2 3.4 %collective-permute-start.8 = (f32[8,8192]{1,0:T(8,128)S(1)}, f32[8,8192]{1,0:T(8,128)S(1)}, u32[]{:S(2)}, u32[]{:S(2)}) collective-permute-start(f32[8,8192]{1,0:T(8,128)S(1)} %collective-permute-done.refs_1_), channel_id=1, source_target_pairs={{0,1},{1,2},{2,3},{4,5},{5,6},{6,7},{8,9},{9,10},{10,11},{12,13},{... | collective-permute-start | bytes 786440 | tf_op jit(solution)/shard_map/ppermute | solution.py:175
  81.7 0.3 collective-permute-start.1
  82.0 16.2 %bond_stage.3.refs_6_ = f32[8,8192]{1,0:T(8,128)} custom-call(s32[64,15]{1,0:T(8,128)} %bitcast.112, s32[32]{0:T(128)} %bitcast.122, bf16[64,256,64]{2,1,0:T(8,128)(2,1)} %own_table.1.lhs_ref, f32[8,8192]{1,0:T(8,128)} %collective-permute-done.12.refs_0_, f32[8,8192]{1,0:T(8,128)} %copy-done.3, f32[8,8192]{1,0:T(8,128)} %copy-done.17), custom_call_target="tpu_custom_call" | custom-call | flops 20000000000 | bytes 6000000 | tf_op jit(solution)/shard_map/bond_stage/pallas_call | solution.py:153
  98.2 1.9 %collective-permute-start.7 = (f32[8,8192]{1,0:T(8,128)S(1)}, f32[8,8192]{1,0:T(8,128)S(1)}, u32[]{:S(2)}, u32[]{:S(2)}) collective-permute-start(f32[8,8192]{1,0:T(8,128)S(1)} %collective-permute-done.5.refs_4_), channel_id=1, source_target_pairs={{1,0},{2,1},{3,2},{5,4},{6,5},{7,6},{9,8},{10,9},{11,10},{13,12},{... | collective-permute-start | bytes 786440 | tf_op jit(solution)/shard_map/ppermute | solution.py:175
  100.2 3.6 %collective-permute-start.6 = (f32[8,8192]{1,0:T(8,128)S(1)}, f32[8,8192]{1,0:T(8,128)S(1)}, u32[]{:S(2)}, u32[]{:S(2)}) collective-permute-start(f32[8,8192]{1,0:T(8,128)S(1)} %collective-permute-done.5.refs_4_), channel_id=1, source_target_pairs={{0,1},{1,2},{2,3},{4,5},{5,6},{6,7},{8,9},{9,10},{10,11},{12,13},{... | collective-permute-start | bytes 786440 | tf_op jit(solution)/shard_map/ppermute | solution.py:175
  103.8 1.9 %collective-permute-start.3 = (f32[8,8192]{1,0:T(8,128)S(1)}, f32[8,8192]{1,0:T(8,128)S(1)}, u32[]{:S(2)}, u32[]{:S(2)}) collective-permute-start(f32[8,8192]{1,0:T(8,128)S(1)} %collective-permute-done.1.refs_1_), channel_id=1, source_target_pairs={{1,0},{2,1},{3,2},{5,4},{6,5},{7,6},{9,8},{10,9},{11,10},{13,12},{... | collective-permute-start | bytes 786440 | tf_op jit(solution)/shard_map/ppermute | solution.py:175
  105.8 3.6 %collective-permute-start.2 = (f32[8,8192]{1,0:T(8,128)S(1)}, f32[8,8192]{1,0:T(8,128)S(1)}, u32[]{:S(2)}, u32[]{:S(2)}) collective-permute-start(f32[8,8192]{1,0:T(8,128)S(1)} %collective-permute-done.1.refs_1_), channel_id=1, source_target_pairs={{0,1},{1,2},{2,3},{4,5},{5,6},{6,7},{8,9},{9,10},{10,11},{12,13},{... | collective-permute-start | bytes 786440 | tf_op jit(solution)/shard_map/ppermute | solution.py:175
  109.5 0.7 copy-done.24
  110.2 21.6 %bond_stage.4.refs_6_ = f32[8,8192]{1,0:T(8,128)} custom-call(s32[64,15]{1,0:T(8,128)} %bitcast.113, s32[32]{0:T(128)} %bitcast.123, bf16[64,256,64]{2,1,0:T(8,128)(2,1)} %own_table.1.lhs_ref, f32[8,8192]{1,0:T(8,128)} %copy-done.24, f32[8,8192]{1,0:T(8,128)} %copy-done.16, f32[8,8192]{1,0:T(8,128)} %copy-done.22, f32[8,8192]{1,0:T(8,128)} %copy-done.20, ...), custom_call_target="tpu_custom_call" | custom-call | flops 20000000000 | bytes 6000000 | tf_op jit(solution)/shard_map/bond_stage/pallas_call | solution.py:153
  131.9 0.6 copy-done.23
  132.7 0.7 copy-done.27
  133.4 21.5 %bond_stage.5 = f32[8,8192]{1,0:T(8,128)} custom-call(s32[64,15]{1,0:T(8,128)} %bitcast.114, s32[32]{0:T(128)} %bitcast.124, bf16[64,256,64]{2,1,0:T(8,128)(2,1)} %own_table.1.lhs_ref, f32[8,8192]{1,0:T(8,128)} %copy-done.27, f32[8,8192]{1,0:T(8,128)} %copy-done.21, f32[8,8192]{1,0:T(8,128)} %copy-done.26, f32[8,8192]{1,0:T(8,128)} %copy-done.25, ...), custom_call_target="tpu_custom_call" | custom-call | flops 20000000000 | bytes 6000000 | tf_op jit(solution)/shard_map/bond_stage/pallas_call | solution.py:153
  154.9 1.1 fusion.29
  156.1 1.3 fusion.15
  157.4 2.7 %copy.88 = f32[3,8192]{0,1:T(8,128)} copy(f32[3,8192]{1,0:T(4,128)S(1)} %fusion.15) | data formatting | bytes 196608 | tf_op jit(solution)/shard_map/add | solution.py:239
  160.0 7.2 %scatter_custom_fusion = f32[3,8192]{0,1:T(8,128)} fusion(f32[3,8192]{0,1:T(8,128)} %copy.88, s32[512]{0:T(512)S(1)} %bitcast.117, f32[3,64,8]{0,2,1:T(8,128)S(1)} %copy.87, f32[]{:T(128)} %constant.12.clone.1, f32[512,3]{1,0:T(8,128)S(1)} %gather_fusion), kind=kCustom, calls=%fused_computation.17 | custom fusion | flops 6144 | bytes 623104 | tf_op jit(solution)/shard_map/scatter-add | solution.py:231
  167.3 2.8 %copy.89 = f32[3,8192]{1,0:T(4,128)S(1)} copy(f32[3,8192]{0,1:T(8,128)} %scatter_custom_fusion) | data formatting | bytes 196608 | tf_op jit(solution)/shard_map/scatter-add | solution.py:231
  170.1 0.2 fusion.21
  170.3 0.7 copy.95
  171.0 0.7 copy.94
  (87 shorter events, 1.3 us)
Async XLA Ops:
  0.6 50.5 %copy-start = (f32[24,24]{1,0:T(8,128)S(1)}, f32[24,24]{1,0:T(8,128)}, u32[]{:S(2)}) copy-start(f32[24,24]{1,0:T(8,128)} %param.27) | copy-start | bytes 6916
  0.6 37.2 %copy-start.5 = (f32[1,1,8192]{2,1,0:T(1,128)S(1)}, f32[1,1,8192]{2,1,0:T(1,128)}, u32[]{:S(2)}) copy-start(f32[1,1,8192]{2,1,0:T(1,128)} %param.18) | copy-start | bytes 98308
  0.7 21.6 %copy-start.12 = (s32[1,1,64,8]{2,3,1,0:T(8,128)S(1)}, s32[1,1,64,8]{2,3,1,0:T(8,128)}, u32[]{:S(2)}) copy-start(s32[1,1,64,8]{2,3,1,0:T(8,128)} %param.28) | copy-start | bytes 6148
  0.7 21.8 %copy-start.13 = (s32[1,1,64,8]{2,3,1,0:T(8,128)S(1)}, s32[1,1,64,8]{2,3,1,0:T(8,128)}, u32[]{:S(2)}) copy-start(s32[1,1,64,8]{2,3,1,0:T(8,128)} %param.29) | copy-start | bytes 6148
  0.7 22.0 %copy-start.10 = (f32[1,1,3,512]{3,1,2,0:T(1,128)S(1)}, f32[1,1,3,512]{3,1,2,0:T(1,128)}, u32[]{:S(2)}) copy-start(f32[1,1,3,512]{3,1,2,0:T(1,128)} %param.23) | copy-start | bytes 18436
  2.7 35.2 %copy-start.3 = (f32[8,8192]{1,0:T(8,128)}, f32[8,8192]{1,0:T(8,128)S(1)}, u32[]{:S(2)}) copy-start(f32[8,8192]{1,0:T(8,128)S(1)} %pad_maximum_fusion.field_ref.refs_1_) | copy-start | bytes 786436
  2.7 66.2 %collective-permute-start.13 = (f32[8,8192]{1,0:T(8,128)S(1)}, f32[8,8192]{1,0:T(8,128)S(1)}, u32[]{:S(2)}, u32[]{:S(2)}) collective-permute-start(f32[8,8192]{1,0:T(8,128)S(1)} %pad_maximum_fusion.field_ref.refs_1_), channel_id=1, source_target_pairs={{1,0},{2,1},{3,2},{5,4},{6,5},{7,6},{9,8},{10,9},{11,10},{13,12},{... | collective-permute-start | bytes 786440 | tf_op jit(solution)/shard_map/ppermute | solution.py:175
  7.9 70.4 %collective-permute-start.12 = (f32[8,8192]{1,0:T(8,128)S(1)}, f32[8,8192]{1,0:T(8,128)}, u32[]{:S(2)}, u32[]{:S(2)}) collective-permute-start(f32[8,8192]{1,0:T(8,128)S(1)} %pad_maximum_fusion.field_ref.refs_1_), channel_id=1, source_target_pairs={{0,1},{1,2},{2,3},{4,5},{5,6},{6,7},{8,9},{9,10},{10,11},{12,13},{... | collective-permute-start | bytes 786440 | tf_op jit(solution)/shard_map/ppermute | solution.py:175
  9.8 51.6 %collective-permute-start.4 = (f32[8,8192]{1,0:T(8,128)S(1)}, f32[8,8192]{1,0:T(8,128)S(1)}, u32[]{:S(2)}, u32[]{:S(2)}) collective-permute-start(f32[8,8192]{1,0:T(8,128)S(1)} %pad_maximum_fusion.field_ref.refs_1_), channel_id=1, source_target_pairs={{0,252},{4,0},{8,4},{12,8},{16,12},{20,16},{24,20},{28,24},{32,28}... | collective-permute-start | bytes 786440 | tf_op jit(solution)/shard_map/ppermute | solution.py:180
  19.6 56.5 %collective-permute-start = (f32[8,8192]{1,0:T(8,128)S(1)}, f32[8,8192]{1,0:T(8,128)S(1)}, u32[]{:S(2)}, u32[]{:S(2)}) collective-permute-start(f32[8,8192]{1,0:T(8,128)S(1)} %pad_maximum_fusion.field_ref.refs_1_), channel_id=1, source_target_pairs={{0,4},{4,8},{8,12},{12,16},{16,20},{20,24},{24,28},{28,32},{32,36}... | collective-permute-start | bytes 786440 | tf_op jit(solution)/shard_map/ppermute | solution.py:180
  28.3 30.2 %all-to-all-start = ((f32[6,64,8]{2,0,1:T(8,128)}), f32[6,64,8]{2,0,1:T(8,128)S(1)}, u32[]{:S(2)}, u32[]{:S(2)}) async-start(f32[6,64,8]{2,0,1:T(8,128)} %copy.86), calls=%async_computation | async-start | bytes 524288 | tf_op jit(solution)/shard_map/all_to_all | solution.py:218
  37.9 10.2 %copy-start.8 = (s32[1,1,8,128]{3,2,1,0:T(8,128)S(1)}, s32[1,1,8,128]{3,2,1,0:T(8,128)}, u32[]{:S(2)}) copy-start(s32[1,1,8,128]{3,2,1,0:T(8,128)} %param.25) | copy-start | bytes 12292
  37.9 13.2 %copy-start.14 = (f32[1,1,128]{2,1,0:T(1,128)S(1)}, f32[1,1,128]{2,1,0:T(1,128)}, u32[]{:S(2)}) copy-start(f32[1,1,128]{2,1,0:T(1,128)} %param.26) | copy-start | bytes 1540
  37.9 13.4 %copy-start.9 = (s32[1,1,64,15]{2,1,3,0:T(1,128)S(1)}, s32[1,1,64,15]{2,1,3,0:T(1,128)}, u32[]{:S(2)}) copy-start(s32[1,1,64,15]{2,1,3,0:T(1,128)} %param.21) | copy-start | bytes 11524
  37.9 14.1 %copy-start.11 = (f32[1,1,3,512]{3,1,2,0:T(1,128)S(1)}, f32[1,1,3,512]{3,1,2,0:T(1,128)}, u32[]{:S(2)}) copy-start(f32[1,1,3,512]{3,1,2,0:T(1,128)} %param.24) | copy-start | bytes 18436
  61.4 36.8 %copy-start.15 = (f32[8,8192]{1,0:T(8,128)}, f32[8,8192]{1,0:T(8,128)S(1)}, u32[]{:S(2)}) copy-start(f32[8,8192]{1,0:T(8,128)S(1)} %collective-permute-done.4.refs_4_) | copy-start | bytes 786436
  61.5 20.2 %collective-permute-start.11 = (f32[8,8192]{1,0:T(8,128)S(1)}, f32[8,8192]{1,0:T(8,128)S(1)}, u32[]{:S(2)}, u32[]{:S(2)}) collective-permute-start(f32[8,8192]{1,0:T(8,128)S(1)} %collective-permute-done.4.refs_4_), channel_id=1, source_target_pairs={{1,0},{2,1},{3,2},{5,4},{6,5},{7,6},{9,8},{10,9},{11,10},{13,12},{... | collective-permute-start | bytes 786440 | tf_op jit(solution)/shard_map/ppermute | solution.py:175
  66.2 34.0 %collective-permute-start.10 = (f32[8,8192]{1,0:T(8,128)S(1)}, f32[8,8192]{1,0:T(8,128)S(1)}, u32[]{:S(2)}, u32[]{:S(2)}) collective-permute-start(f32[8,8192]{1,0:T(8,128)S(1)} %collective-permute-done.4.refs_4_), channel_id=1, source_target_pairs={{0,1},{1,2},{2,3},{4,5},{5,6},{6,7},{8,9},{9,10},{10,11},{12,13},{... | collective-permute-start | bytes 786440 | tf_op jit(solution)/shard_map/ppermute | solution.py:175
  69.0 13.0 %copy-start.17 = (f32[8,8192]{1,0:T(8,128)}, f32[8,8192]{1,0:T(8,128)S(1)}, u32[]{:S(2)}) copy-start(f32[8,8192]{1,0:T(8,128)S(1)} %collective-permute-done.13.refs_2_) | copy-start | bytes 786436
  69.0 29.2 %collective-permute-start.5 = (f32[8,8192]{1,0:T(8,128)S(1)}, f32[8,8192]{1,0:T(8,128)S(1)}, u32[]{:S(2)}, u32[]{:S(2)}) collective-permute-start(f32[8,8192]{1,0:T(8,128)S(1)} %collective-permute-done.4.refs_4_), channel_id=1, source_target_pairs={{0,252},{4,0},{8,4},{12,8},{16,12},{20,16},{24,20},{28,24},{32,28}... | collective-permute-start | bytes 786440 | tf_op jit(solution)/shard_map/ppermute | solution.py:180
  76.1 22.1 %copy-start.16 = (f32[8,8192]{1,0:T(8,128)}, f32[8,8192]{1,0:T(8,128)S(1)}, u32[]{:S(2)}) copy-start(f32[8,8192]{1,0:T(8,128)S(1)} %collective-permute-done.refs_1_) | copy-start | bytes 786436
  76.1 29.7 %collective-permute-start.9 = (f32[8,8192]{1,0:T(8,128)S(1)}, f32[8,8192]{1,0:T(8,128)S(1)}, u32[]{:S(2)}, u32[]{:S(2)}) collective-permute-start(f32[8,8192]{1,0:T(8,128)S(1)} %collective-permute-done.refs_1_), channel_id=1, source_target_pairs={{1,0},{2,1},{3,2},{5,4},{6,5},{7,6},{9,8},{10,9},{11,10},{13,12},{... | collective-permute-start | bytes 786440 | tf_op jit(solution)/shard_map/ppermute | solution.py:175
  78.2 31.2 %collective-permute-start.8 = (f32[8,8192]{1,0:T(8,128)S(1)}, f32[8,8192]{1,0:T(8,128)S(1)}, u32[]{:S(2)}, u32[]{:S(2)}) collective-permute-start(f32[8,8192]{1,0:T(8,128)S(1)} %collective-permute-done.refs_1_), channel_id=1, source_target_pairs={{0,1},{1,2},{2,3},{4,5},{5,6},{6,7},{8,9},{9,10},{10,11},{12,13},{... | collective-permute-start | bytes 786440 | tf_op jit(solution)/shard_map/ppermute | solution.py:175
  81.7 16.5 %copy-start.18 = (f32[8,8192]{1,0:T(8,128)}, f32[8,8192]{1,0:T(8,128)S(1)}, u32[]{:S(2)}) copy-start(f32[8,8192]{1,0:T(8,128)S(1)} %collective-permute-done.11.refs_5_) | copy-start | bytes 786436
  81.7 22.1 %collective-permute-start.1 = (f32[8,8192]{1,0:T(8,128)S(1)}, f32[8,8192]{1,0:T(8,128)S(1)}, u32[]{:S(2)}, u32[]{:S(2)}) collective-permute-start(f32[8,8192]{1,0:T(8,128)S(1)} %collective-permute-done.refs_1_), channel_id=1, source_target_pairs={{0,4},{4,8},{8,12},{12,16},{16,20},{20,24},{24,28},{28,32},{32,36}... | collective-permute-start | bytes 786440 | tf_op jit(solution)/shard_map/ppermute | solution.py:180
  98.2 33.5 %copy-start.19 = (f32[8,8192]{1,0:T(8,128)}, f32[8,8192]{1,0:T(8,128)S(1)}, u32[]{:S(2)}) copy-start(f32[8,8192]{1,0:T(8,128)S(1)} %collective-permute-done.5.refs_4_) | copy-start | bytes 786436
  98.2 33.6 %collective-permute-start.7 = (f32[8,8192]{1,0:T(8,128)S(1)}, f32[8,8192]{1,0:T(8,128)S(1)}, u32[]{:S(2)}, u32[]{:S(2)}) collective-permute-start(f32[8,8192]{1,0:T(8,128)S(1)} %collective-permute-done.5.refs_4_), channel_id=1, source_target_pairs={{1,0},{2,1},{3,2},{5,4},{6,5},{7,6},{9,8},{10,9},{11,10},{13,12},{... | collective-permute-start | bytes 786440 | tf_op jit(solution)/shard_map/ppermute | solution.py:175
  100.2 9.3 %copy-start.20 = (f32[8,8192]{1,0:T(8,128)}, f32[8,8192]{1,0:T(8,128)S(1)}, u32[]{:S(2)}) copy-start(f32[8,8192]{1,0:T(8,128)S(1)} %collective-permute-done.10.refs_3_) | copy-start | bytes 786436
  100.2 31.6 %collective-permute-start.6 = (f32[8,8192]{1,0:T(8,128)S(1)}, f32[8,8192]{1,0:T(8,128)S(1)}, u32[]{:S(2)}, u32[]{:S(2)}) collective-permute-start(f32[8,8192]{1,0:T(8,128)S(1)} %collective-permute-done.5.refs_4_), channel_id=1, source_target_pairs={{0,1},{1,2},{2,3},{4,5},{5,6},{6,7},{8,9},{9,10},{10,11},{12,13},{... | collective-permute-start | bytes 786440 | tf_op jit(solution)/shard_map/ppermute | solution.py:175
  103.8 27.9 %copy-start.21 = (f32[8,8192]{1,0:T(8,128)}, f32[8,8192]{1,0:T(8,128)S(1)}, u32[]{:S(2)}) copy-start(f32[8,8192]{1,0:T(8,128)S(1)} %collective-permute-done.1.refs_1_) | copy-start | bytes 786436
  103.8 28.0 %collective-permute-start.3 = (f32[8,8192]{1,0:T(8,128)S(1)}, f32[8,8192]{1,0:T(8,128)S(1)}, u32[]{:S(2)}, u32[]{:S(2)}) collective-permute-start(f32[8,8192]{1,0:T(8,128)S(1)} %collective-permute-done.1.refs_1_), channel_id=1, source_target_pairs={{1,0},{2,1},{3,2},{5,4},{6,5},{7,6},{9,8},{10,9},{11,10},{13,12},{... | collective-permute-start | bytes 786440 | tf_op jit(solution)/shard_map/ppermute | solution.py:175
  105.8 3.7 %copy-start.22 = (f32[8,8192]{1,0:T(8,128)}, f32[8,8192]{1,0:T(8,128)S(1)}, u32[]{:S(2)}) copy-start(f32[8,8192]{1,0:T(8,128)S(1)} %collective-permute-done.9.refs_2_) | copy-start | bytes 786436
  105.8 26.1 %collective-permute-start.2 = (f32[8,8192]{1,0:T(8,128)S(1)}, f32[8,8192]{1,0:T(8,128)S(1)}, u32[]{:S(2)}, u32[]{:S(2)}) collective-permute-start(f32[8,8192]{1,0:T(8,128)S(1)} %collective-permute-done.1.refs_1_), channel_id=1, source_target_pairs={{0,1},{1,2},{2,3},{4,5},{5,6},{6,7},{8,9},{9,10},{10,11},{12,13},{... | collective-permute-start | bytes 786440 | tf_op jit(solution)/shard_map/ppermute | solution.py:175
  109.5 0.7 copy-start.24
  131.8 24.3 %copy-start.1 = (f32[1,1,3,8192]{3,1,2,0:T(1,128)S(1)}, f32[1,1,3,8192]{3,1,2,0:T(1,128)}, u32[]{:S(2)}) copy-start(f32[1,1,3,8192]{3,1,2,0:T(1,128)} %param.16) | copy-start | bytes 294916
  131.8 24.3 %copy-start.2 = (f32[1,1,3,8192]{3,1,2,0:T(1,128)S(1)}, f32[1,1,3,8192]{3,1,2,0:T(1,128)}, u32[]{:S(2)}) copy-start(f32[1,1,3,8192]{3,1,2,0:T(1,128)} %param.15) | copy-start | bytes 294916
  131.8 24.3 %copy-start.4 = (f32[1,1,8192]{2,1,0:T(1,128)S(1)}, f32[1,1,8192]{2,1,0:T(1,128)}, u32[]{:S(2)}) copy-start(f32[1,1,8192]{2,1,0:T(1,128)} %param.19) | copy-start | bytes 98308
  131.8 24.3 %copy-start.6 = (f32[1,1,3,8192]{3,1,2,0:T(1,128)S(1)}, f32[1,1,3,8192]{3,1,2,0:T(1,128)}, u32[]{:S(2)}) copy-start(f32[1,1,3,8192]{3,1,2,0:T(1,128)} %param.20) | copy-start | bytes 294916
  131.8 0.7 copy-start.23
  131.8 0.8 copy-start.25
  131.9 0.8 copy-start.26
  132.7 0.7 copy-start.27
  160.0 10.1 %copy-start.7 = (f32[1,1,3,8192]{3,1,2,0:T(1,128)S(1)}, f32[1,1,3,8192]{3,1,2,0:T(1,128)}, u32[]{:S(2)}) copy-start(f32[1,1,3,8192]{3,1,2,0:T(1,128)} %param.17) | copy-start | bytes 294916

commit v2 on v1

v2 whole, which is shorter than its diff:
```python
import math
import jax
import jax.numpy as jnp
from jax import lax
from jax.experimental import pallas as pl
from jax.experimental.pallas import tpu as pltpu
from jax.sharding import PartitionSpec as P

TILE = 128
log_scale = math.log2(math.e) / 9.0
force_scale = -0.125 * log_scale * math.exp(1.0 / 9.0)
f32 = jnp.float32
bf16 = jnp.bfloat16
UNROLL = 8
UNROLL_OTHER = 8
OWN_GROUP = 2
own_slots = (1, 4, 7, 10, 13)
other_slots = (0, 2, 3, 5, 6, 8, 9, 11, 12, 14)
OWN_UNROLL = 4
spring = 0.5
time_step = 0.5


def split3(value):
    high = value.astype(bf16).astype(f32)
    rest = value - high
    middle = rest.astype(bf16).astype(f32)
    return high, middle, (rest - middle)


def point_terms(v):
    row = lax.broadcasted_iota(jnp.int32, v.shape, 0)
    disp = pltpu.roll(v, 5, 0)
    now = v + disp
    first = row < 3
    ref_norm = jnp.sum(jnp.where(first, v * v, 0.0), axis=0, keepdims=True)
    growth = jnp.sum(jnp.where(first, disp * (v + now), 0.0), axis=0, keepdims=True)
    return row, disp, now, ref_norm, growth


def own_kernel(field_ref, lhs_ref):
    def one_tile(tile, carry):
        v = field_ref[:, pl.ds(pl.multiple_of(tile * TILE, TILE), TILE)]
        row, disp, now, ref_norm, growth = point_terms(v)
        row16 = lax.broadcasted_iota(jnp.int32, (16, TILE), 0)
        coef_ref = jnp.where(row < 3, 2.0 * log_scale * v, jnp.where(row == 6, -log_scale, 0.0))
        coef_now = jnp.where(
            row < 3,
            -2.0 * disp,
            jnp.where(row < 6, -2.0 * pltpu.roll(now, 3, 0), jnp.where(row == 7, 1.0, 0.0)),
        )
        for place, coef, alone in (
            (0, coef_ref, -log_scale * (1.0 + ref_norm)),
            (1, coef_now, growth),
        ):
            high, middle, low = split3(coef)
            a, b, c = split3(alone)
            const = jnp.where(row16 == 0, a, jnp.where(row16 == 1, b, jnp.where(row16 == 2, c, 0.0)))
            rows = jnp.concatenate([high, high, middle, middle, high, low, const], axis=0)
            lhs_ref[tile, pl.ds(place * TILE, TILE), :] = rows.T.astype(bf16)
        return carry

    lax.fori_loop(0, field_ref.shape[1] // TILE, one_tile, 0, unroll=OWN_UNROLL)


def own_table(field):
    tiles = field.shape[1] // TILE
    return pl.pallas_call(
        own_kernel,
        out_shape=jax.ShapeDtypeStruct((tiles, 2 * TILE, 64), bf16),
        name="own_table",
        cost_estimate=pl.CostEstimate(flops=8_000_000_000, transcendentals=0, bytes_accessed=4_500_000),
    )(field)


def fill_table(field_ref, table_ref, row_start, place, chunk):
    def one(step, carry):
        lanes = pl.ds(pl.multiple_of(step * chunk, chunk), chunk)
        v = field_ref[row_start : row_start + 8, lanes]
        row, disp, now, ref_norm, growth = point_terms(v)
        terms = jnp.where(row < 6, v, jnp.where(row == 6, ref_norm, growth))
        high, middle, low = split3(terms)
        table_ref[place, 0:16, lanes] = jnp.concatenate([high, middle], axis=0).astype(bf16)
        table_ref[place, 16:32, lanes] = jnp.concatenate([low, high], axis=0).astype(bf16)
        whole = 1.0 - v[6:7]
        stiff = v[7:8]
        spread = jnp.where(row < 3, now, jnp.where(row < 6, pltpu.roll(now, 3, 0), 1.0))
        weight = whole * jnp.where((row < 3) | (row == 6), 1.0, stiff)
        sums = spread * weight
        q_high = sums.astype(bf16).astype(f32)
        table_ref[place, 32:48, lanes] = jnp.concatenate([q_high, sums - q_high], axis=0).astype(bf16)
        return carry

    lax.fori_loop(0, field_ref.shape[1] // chunk, one, 0)


def pair_sums(tile, slots, table_ref, names_ref, word, lhs, group):
    ones = jnp.ones((16, TILE), bf16)
    acc = None
    for start in range(0, len(slots), group):
        rhs, sums = [], []
        for place in range(start, min(start + group, len(slots))):
            slot = slots[place]
            name = names_ref[tile, slot]
            lanes = pl.ds(pl.multiple_of((name % 64) * TILE, TILE), TILE)
            top = table_ref[place, 0:16, lanes]
            low = table_ref[place, 16:32, lanes]
            alive = 1 - (lax.shift_right_logical(word, (tile % 2) * 15 + slot) & 1)
            rhs.append(jnp.concatenate([top, top, low, ones], axis=0))
            q = table_ref[place, 32:48, lanes]
            sums.append(jnp.where(alive == 1, q, jnp.zeros_like(q)))
        while len(rhs) < group:
            rhs.append(rhs[-1])
            sums.append(jnp.zeros_like(sums[-1]))
        rhs = jnp.concatenate(rhs, axis=1)
        sums = jnp.concatenate(sums, axis=1)
        both = jnp.dot(lhs, rhs, preferred_element_type=f32)
        stretch = both[:TILE]
        pull = both[TILE:] * jnp.exp2(stretch) / stretch
        high = pull.astype(bf16)
        low = (pull - high.astype(f32)).astype(bf16)
        dims = (((1,), (1,)), ((), ()))
        part = lax.dot_general(sums, high, dims, preferred_element_type=f32)
        part += lax.dot_general(sums, low, dims, preferred_element_type=f32)
        acc = part if acc is None else acc + part
    return acc[0:8] + acc[8:16]


def own_layer_kernel(names_ref, flags_ref, lhs_ref, *refs):
    out_ref, table_ref = refs[-2:]
    for place, ref in enumerate(refs[:-2]):
        fill_table(ref, table_ref, 0, place, 512)

    def one_tile(tile, carry):
        lanes = pl.ds(pl.multiple_of(tile * TILE, TILE), TILE)
        word = flags_ref[tile // 2]
        out_ref[:, lanes] = pair_sums(
            tile, own_slots, table_ref, names_ref, word, lhs_ref[tile], OWN_GROUP
        )
        return carry

    lax.fori_loop(0, lhs_ref.shape[0], one_tile, 0, unroll=UNROLL)


def other_layer_kernel(
    names_ref, flags_ref, layer_ref, lhs_ref, below_ref, own_ref, above_ref,
    sums_ref, vel_ref, body_ref, react_ref, disp_out_ref, vel_out_ref, table_ref,
):
    layer = layer_ref[0]
    for side, ref, edge in ((0, below_ref, 0), (1, above_ref, 3)):

        @pl.when(layer == edge)
        def _():
            for sector in range(5):
                fill_table(own_ref, table_ref, sector * 8, sector * 2 + side, 512)

        @pl.when(layer != edge)
        def _():
            for sector in range(5):
                fill_table(ref, table_ref, sector * 8, sector * 2 + side, 512)

    def one_tile(tile, carry):
        lanes = pl.ds(pl.multiple_of(tile * TILE, TILE), TILE)
        word = flags_ref[tile // 2]
        acc = pair_sums(tile, other_slots, table_ref, names_ref, word, lhs_ref[tile], 2)
        acc += sums_ref[:, lanes]
        own = own_ref[16:24, lanes]
        disp = own[3:6]
        now = own[0:3] + disp
        whole = 1.0 - own[6:7]
        inner = acc[0:3] - now * acc[6:7]
        outer = acc[3:6] - now * acc[7:8]
        force = force_scale * whole * (own[7:8] * inner + outer)
        vel = vel_ref[:, lanes] + time_step * (force + body_ref[:, lanes] + react_ref[:, lanes])
        vel_out_ref[:, lanes] = vel
        disp_out_ref[:, lanes] = disp + time_step * vel
        return carry

    lax.fori_loop(0, lhs_ref.shape[0], one_tile, 0, unroll=UNROLL_OTHER)


def cost(flops):
    return pl.CostEstimate(flops=flops, transcendentals=0, bytes_accessed=6_000_000)


smem = pl.BlockSpec(memory_space=pltpu.SMEM)
vmem = pl.BlockSpec(memory_space=pltpu.VMEM)


def own_layer_sums(names, flags, lhs, blocks):
    points = blocks[0].shape[1]
    return pl.pallas_call(
        own_layer_kernel,
        out_shape=jax.ShapeDtypeStruct((8, points), f32),
        in_specs=[smem, smem] + [vmem] * (1 + len(blocks)),
        out_specs=vmem,
        scratch_shapes=[pltpu.VMEM((len(blocks), 48, points), bf16)],
        name="own_layer",
        cost_estimate=cost(18_000_000_000),
    )(names, flags, lhs, *blocks)


def other_layer_update(names, flags, layer, lhs, below, own, above, sums, vel, body, react):
    points = own.shape[1]
    shape = jax.ShapeDtypeStruct((3, points), f32)
    return pl.pallas_call(
        other_layer_kernel,
        out_shape=(shape, shape),
        in_specs=[smem] * 3 + [vmem] * 8,
        out_specs=(vmem, vmem),
        scratch_shapes=[pltpu.VMEM((10, 48, points), bf16)],
        name="other_layer",
        cost_estimate=cost(36_000_000_000),
    )(names, flags, layer, lhs, below, own, above, sums, vel, body, react)


def parts32(value):
    high, middle, low = split3(value)
    return jnp.concatenate([high, middle, low, jnp.zeros_like(low)], axis=0)


def join32(value):
    return value[0:8] + value[8:16] + value[16:24]


def one_hot(index, count):
    row = lax.broadcasted_iota(jnp.int32, (count, index.shape[1]), 0)
    return jnp.where(row == index, 1.0, 0.0).astype(bf16)


across = (((1,), (1,)), ((), ()))


def values_kernel(field_ref, blade_ref, rim_ref, root_ref, out_ref, pad_ref):
    rim = rim_ref[...]
    tile_of = lax.shift_right_logical(rim, 7)
    lane_hot = one_hot(rim & 127, TILE)

    def one_batch(step, acc):
        rows = []
        for inner in range(8):
            start = pl.multiple_of(step * (8 * TILE) + inner * TILE, TILE)
            rows.append(parts32(field_ref[:, pl.ds(start, TILE)]))
        found = jnp.dot(jnp.concatenate(rows, axis=0).astype(bf16), lane_hot, preferred_element_type=f32)
        for inner in range(8):
            acc = acc + jnp.where(tile_of == step * 8 + inner, found[inner * 32 : inner * 32 + 24], 0.0)
        return acc

    acc = lax.fori_loop(0, field_ref.shape[1] // (8 * TILE), one_batch, jnp.zeros((24, rim.shape[1]), f32))
    out_ref[0:3] = join32(acc)[3:6]
    pad_ref[...] = jnp.zeros_like(pad_ref)
    pad_ref[0:3] = blade_ref[...]
    found = jnp.dot(
        parts32(pad_ref[...]).astype(bf16), one_hot(root_ref[...], blade_ref.shape[1]), preferred_element_type=f32
    )
    out_ref[3:6] = join32(found)[0:3]


def coupling_values(field, blade, rim, root):
    return pl.pallas_call(
        values_kernel,
        out_shape=jax.ShapeDtypeStruct((6, rim.shape[1]), f32),
        scratch_shapes=[pltpu.VMEM((8, blade.shape[1]), f32)],
        name="coupling_values",
        cost_estimate=cost(3_000_000_000),
    )(field, blade, rim, root)


def coupling_kernel(
    swapped_ref, sent_ref, rim_ref, root_ref, nodes_ref, scale_ref, stiff_ref, blade_ref, vel_ref,
    react_ref, disp_out_ref, vel_out_ref, pad_ref, elem_ref,
):
    nodes = blade_ref.shape[1]
    rim = rim_ref[...]
    tile_of = lax.shift_right_logical(rim, 7)
    lane_hot = one_hot(rim & 127, TILE)
    pad_ref[...] = jnp.zeros_like(pad_ref)
    pad_ref[0:3] = spring * (swapped_ref[3:6] - sent_ref[0:3])
    back = parts32(pad_ref[...])

    def one_batch(step, carry):
        rows = jnp.concatenate(
            [jnp.where(tile_of == step * 8 + inner, back, 0.0) for inner in range(8)], axis=0
        )
        put = lax.dot_general(rows.astype(bf16), lane_hot, across, preferred_element_type=f32)
        for inner in range(8):
            start = pl.multiple_of(step * (8 * TILE) + inner * TILE, TILE)
            react_ref[:, pl.ds(start, TILE)] = join32(put[inner * 32 : inner * 32 + 32])[0:3]
        return carry

    lax.fori_loop(0, react_ref.shape[1] // (8 * TILE), one_batch, 0)
    pad_ref[0:3] = spring * (swapped_ref[0:3] - sent_ref[3:6])
    loads = parts32(pad_ref[...]).astype(bf16)
    coupling = join32(
        lax.dot_general(loads, one_hot(root_ref[...], nodes), across, preferred_element_type=f32)
    )
    pad_ref[0:3] = blade_ref[...]
    blade = parts32(pad_ref[...]).astype(bf16)
    hots = []
    for q in range(8):
        hot = one_hot(nodes_ref[q : q + 1], nodes)
        hots.append(hot)
        taken = join32(jnp.dot(blade, hot, preferred_element_type=f32))
        for a in range(3):
            elem_ref[8 * a + q : 8 * a + q + 1, :] = taken[a : a + 1]
    force = scale_ref[...] * jnp.dot(
        stiff_ref[...], elem_ref[...], precision=lax.Precision.HIGHEST, preferred_element_type=f32
    )
    high, middle, low = split3(force)
    force = jnp.concatenate([high, middle, low, jnp.zeros((8, force.shape[1]), f32)], axis=0).astype(bf16)
    row = lax.broadcasted_iota(jnp.int32, (24, nodes), 0)
    total = jnp.zeros((24, nodes), f32)
    for q in range(8):
        put = lax.dot_general(force, hots[q], across, preferred_element_type=f32)
        total = total + jnp.where(row % 8 == q, put[0:24] + put[24:48] + put[48:72], 0.0)
    for a in range(3):
        internal = -jnp.sum(total[8 * a : 8 * a + 8], axis=0, keepdims=True)
        vel = vel_ref[a : a + 1] + time_step * (internal + coupling[a : a + 1])
        vel_out_ref[a : a + 1] = vel
        disp_out_ref[a : a + 1] = blade_ref[a : a + 1] + time_step * vel


def coupling_update(swapped, sent, rim, root, nodes, scale, stiff, blade, vel, points):
    small = jax.ShapeDtypeStruct(blade.shape, f32)
    return pl.pallas_call(
        coupling_kernel,
        out_shape=(jax.ShapeDtypeStruct((3, points), f32), small, small),
        scratch_shapes=[
            pltpu.VMEM((8, blade.shape[1]), f32),
            pltpu.VMEM((24, nodes.shape[1]), f32),
        ],
        name="coupling_update",
        cost_estimate=cost(4_000_000_000),
    )(swapped, sent, rim, root, nodes, scale, stiff, blade, vel)


def shift_layer(value, by):
    size = lax.axis_size("layer")
    pairs = [(i, i + by) for i in range(size) if 0 <= i + by < size]
    return lax.ppermute(value, "layer", pairs)


def shift_sector(value, by):
    size = lax.axis_size("blk")
    return lax.ppermute(value, "blk", [(i, (i + by) % size) for i in range(size)])


def on_device(
    ref_pos,
    disk_disp,
    disk_vel,
    damage,
    modulus,
    body_load,
    nbr_tiles,
    break_flags,
    blade_disp,
    blade_vel,
    elem_nodes,
    elem_modulus,
    elem_stiff,
    root_nodes,
    rim_points,
):
    disk_now = disk_disp[0, 0]
    blade_now = blade_disp[0, 0]
    field = jnp.concatenate([ref_pos[0, 0], disk_now, damage[0], modulus[0]], axis=0)
    names = nbr_tiles[0, 0]
    flags = break_flags[0, 0]
    far_behind = shift_sector(field, 2)
    behind = shift_sector(field, 1)
    ahead = shift_sector(field, -1)
    far_ahead = shift_sector(field, -2)
    rim = rim_points[0, 0].reshape(1, -1)
    root = root_nodes[0, 0].reshape(1, -1)
    sent = coupling_values(field, blade_now, rim, root)
    swapped = lax.all_to_all(sent, "blk", split_axis=1, concat_axis=1, tiled=True)
    lhs = own_table(field)
    blocks = [far_behind, behind, field, ahead, far_ahead]
    own = jnp.concatenate(blocks, axis=0)
    below = shift_layer(own, 1)
    above = shift_layer(own, -1)
    sums = own_layer_sums(names, flags, lhs, blocks)
    reaction, blade_disp_new, blade_vel_new = coupling_update(
        swapped, sent, rim, root, elem_nodes[0, 0], elem_modulus[0], elem_stiff, blade_now,
        blade_vel[0, 0], field.shape[1],
    )
    layer = lax.axis_index("layer").reshape(1).astype(jnp.int32)
    disk_disp_new, disk_vel_new = other_layer_update(
        names, flags, layer, lhs, below, own, above, sums, disk_vel[0, 0], body_load[0, 0], reaction
    )
    return (
        disk_disp_new[None, None],
        disk_vel_new[None, None],
        blade_disp_new[None, None],
        blade_vel_new[None, None],
    )


def solution(mesh):
    in_specs = (
        P("blk", "layer", None, None),
        P("blk", "layer", None, None),
        P("blk", "layer", None, None),
        P("blk", "layer", None),
        P("blk", "layer", None),
        P("blk", "layer", None, None),
        P("blk", "layer", None, None),
        P("blk", "layer", None),
        P("blk", "layer", None, None),
        P("blk", "layer", None, None),
        P("blk", "layer", None, None),
        P("blk", "layer", None),
        P(),
        P("blk", "layer", None, None),
        P("blk", "layer", None, None),
    )
    out_specs = (
        P("blk", "layer", None, None),
        P("blk", "layer", None, None),
        P("blk", "layer", None, None),
        P("blk", "layer", None, None),
    )
    return jax.shard_map(
        on_device, mesh=mesh, in_specs=in_specs, out_specs=out_specs, check_vma=False
    )
```

time: 172 us -> 122 us (0.71)
  starting transfers between devices: 55.9 us -> 30.9 us
  other arithmetic: 18.2 us -> 0.9 us
  local copies, waits for them, and re-layouts: 26.6 us -> 16.6 us
  waiting for transfers between devices: 0.04 us -> 4.8 us
  Pallas kernels: 69.5 us -> 67.5 us
    ppermute x10 -> x2, starting transfers between devices: 29.3 us -> 7.93 us  [shift_layer(): return lax.ppermute(value, 'layer', pairs)]
    scatter-add x3 -> x0, other arithmetic: 15.7 us -> none  [the longest x1 7.21 us: on_device(): reaction = jnp.zeros_like(disk_now).at[:, rim_flat].add(-returned)]
    gather x6 -> x0, local copies, waits for them, and re-layouts: 7.48 us -> none  [the longest x2 3.34 us: on_device(): rim_values = disk_now[:, rim_flat]]
    unnamed x66 -> x35, local copies, waits for them, and re-layouts: 7.52 us -> 12.6 us
    pallas_call x1, Pallas kernels: 10.2 us -> 5.27 us  [own_table(): pl.pallas_call(own_kernel, out_shape=jax.ShapeDtypeStruct((tiles, 2 * TIL...]
    all_to_all x1, waiting for transfers between devices: 0.01 us -> 4.78 us  [on_device(): lax.all_to_all(sent, 'blk', split_axis=1, concat_axis=1, tiled=True)]
    ppermute x4, starting transfers between devices: 17.2 us -> 13.7 us  [shift_sector(): lax.ppermute(value, 'blk', [(i, (i + by) % size) for i in range(size)])]
    pallas_call x3 -> x4, Pallas kernels: 59.3 us -> 62.3 us  [the longest x1 33.2 us: other_layer_update(): pl.pallas_call(other_layer_kernel, out_shape=(shape, shape), in_specs=[sm...]
  transfers between devices with their start and end apart: 15 -> 7, of which waited for: 0 -> 1; matrix products, arithmetic and copies ran while one was open for 14% -> 8% of each run, Pallas kernels for 28% -> 28%
where the time goes in v2:
time: 122 us
  Pallas kernels  67.5 us (55%)
  starting transfers between devices  30.9 us (25%)
  local copies, waits for them, and re-layouts  16.6 us (14%)
  waiting for transfers between devices  4.8 us (4%)
    pallas_call x1, Pallas kernels, other_layer_update(): pl.pallas_call(other_layer_kernel, out_shape=(shape, shape), in_specs=[sm...  33.2 us
    pallas_call x1, Pallas kernels, own_layer_sums(): pl.pallas_call(own_layer_kernel, out_shape=jax.ShapeDtypeStruct((8, point...  20.9 us
    ppermute x4, starting transfers between devices, shift_sector(): lax.ppermute(value, 'blk', [(i, (i + by) % size) for i in range(size)])  13.7 us
    unnamed x35, local copies, waits for them, and re-layouts  12.6 us
    all_to_all x1, starting transfers between devices, on_device(): lax.all_to_all(sent, 'blk', split_axis=1, concat_axis=1, tiled=True)  9.28 us
    ppermute x2, starting transfers between devices, shift_layer(): return lax.ppermute(value, 'layer', pairs)  7.93 us
    pallas_call x1, Pallas kernels, own_table(): pl.pallas_call(own_kernel, out_shape=jax.ShapeDtypeStruct((tiles, 2 * TIL...  5.27 us
    all_to_all x1, waiting for transfers between devices, on_device(): lax.all_to_all(sent, 'blk', split_axis=1, concat_axis=1, tiled=True)  4.78 us
  transfers between devices with their start and end apart: 7, of which 1 were waited for; matrix products, arithmetic and copies ran while one was open for 8% of the time, Pallas kernels for 28%

profile of v2, /device:TPU:1, one launch (start us, length us, event | category | flops | bytes accessed | tf_op | source)
XLA Modules:
  0.0 121.6 jit_solution(12651180187414397140)
XLA Ops:
  0.6 1.1 copy_bitcast_fusion.2
  1.7 0.9 pad_maximum_fusion.field_ref.refs_2_
  2.6 0.0 copy-start.1
  2.6 3.7 %collective-permute-start = (f32[8,8192]{1,0:T(8,128)S(1)}, f32[8,8192]{1,0:T(8,128)S(1)}, u32[]{:S(2)}, u32[]{:S(2)}) collective-permute-start(f32[8,8192]{1,0:T(8,128)S(1)} %pad_maximum_fusion.field_ref.refs_2_), channel_id=1, source_target_pairs={{0,8},{4,12},{8,16},{12,20},{16,24},{20,28},{24,32},{28,36},{32,40... | collective-permute-start | bytes 786440 | tf_op jit(solution)/shard_map/ppermute | solution.py:345
  6.3 0.3 collective-permute-start.1
  6.6 7.5 %collective-permute-start.2 = (f32[8,8192]{1,0:T(8,128)S(1)}, f32[8,8192]{1,0:T(8,128)S(1)}, u32[]{:S(2)}, u32[]{:S(2)}) collective-permute-start(f32[8,8192]{1,0:T(8,128)S(1)} %pad_maximum_fusion.field_ref.refs_2_), channel_id=1, source_target_pairs={{0,252},{4,0},{8,4},{12,8},{16,12},{20,16},{24,20},{28,24},{32,28}... | collective-permute-start | bytes 786440 | tf_op jit(solution)/shard_map/ppermute | solution.py:345
  14.1 2.2 %collective-permute-start.3 = (f32[8,8192]{1,0:T(8,128)S(1)}, f32[8,8192]{1,0:T(8,128)S(1)}, u32[]{:S(2)}, u32[]{:S(2)}) collective-permute-start(f32[8,8192]{1,0:T(8,128)S(1)} %pad_maximum_fusion.field_ref.refs_2_), channel_id=1, source_target_pairs={{0,248},{4,252},{8,0},{12,4},{16,8},{20,12},{24,16},{28,20},{32,24... | collective-permute-start | bytes 786440 | tf_op jit(solution)/shard_map/ppermute | solution.py:345
  16.3 0.8 copy.34
  17.1 0.7 reshape_squeeze.6.rim_ref
  17.7 0.8 copy.35
  18.5 0.7 reshape_squeeze.7.root_ref
  19.2 1.3 %copy.55 = f32[1,1,3,512]{3,2,1,0:T(4,128)} copy(f32[1,1,3,512]{3,1,2,0:T(1,128)} %param.23) | data formatting | bytes 12288
  20.5 0.0 copy-done.1
  20.5 3.6 %coupling_values.1.sent_ref = f32[6,512]{1,0:T(8,128)} custom-call(f32[8,8192]{1,0:T(8,128)} %copy-done.1, f32[3,512]{1,0:T(4,128)} %bitcast.37, s32[1,512]{1,0:T(1,128)} %reshape_squeeze.6.rim_ref, s32[1,512]{1,0:T(1,128)} %reshape_squeeze.7.root_ref), custom_call_target="tpu_custom_call" | custom-call | flops 3000000000 | bytes 6000000 | tf_op jit(solution)/shard_map/coupling_values/pallas_call | solution.py:260
  24.1 0.8 all_to_all.7
  24.9 0.8 copy.36
  25.8 9.3 %all-to-all-start = ((f32[6,64,8]{2,0,1:T(8,128)}), f32[6,64,8]{2,0,1:T(8,128)S(1)}, u32[]{:S(2)}, u32[]{:S(2)}) async-start(f32[6,64,8]{2,0,1:T(8,128)} %copy.36), calls=%async_computation | async-start | bytes 524288 | tf_op jit(solution)/shard_map/all_to_all | solution.py:377
  35.0 0.0 copy-done.8
  35.0 0.0 copy-done.9
  35.1 0.8 copy_bitcast_fusion
  35.9 5.3 %own_table.1.lhs_ref = bf16[64,256,64]{2,1,0:T(8,128)(2,1)} custom-call(f32[8,8192]{1,0:T(8,128)} %copy-done.1), custom_call_target="tpu_custom_call" | custom-call | flops 8000000000 | bytes 4500000 | tf_op jit(solution)/shard_map/own_table/pallas_call | solution.py:68
  41.2 0.0 copy-done.10
  41.2 0.7 copy.33
  41.9 0.0 copy-done.11
  41.9 0.6 copy.54
  42.5 4.8 %all-to-all-done = f32[6,64,8]{2,0,1:T(8,128)S(1)} async-done(((f32[6,64,8]{2,0,1:T(8,128)}), f32[6,64,8]{2,0,1:T(8,128)S(1)}, u32[]{:S(2)}, u32[]{:S(2)}) %all-to-all-start) | async-done | bytes 12320 | tf_op jit(solution)/shard_map/all_to_all | solution.py:377
  47.3 0.7 all_to_all.9.swapped_ref
  48.0 4.6 %coupling_update.1 = (f32[3,8192]{1,0:T(4,128)}, f32[3,512]{1,0:T(4,128)}, f32[3,512]{1,0:T(4,128)}) custom-call(f32[6,512]{1,0:T(8,128)} %all_to_all.9.swapped_ref, f32[6,512]{1,0:T(8,128)} %coupling_values.1.sent_ref, s32[1,512]{1,0:T(1,128)} %reshape_squeeze.6.rim_ref, s32[1,512]{1,0:T(1,128)} %reshape_squeeze.7.root_ref, s32[8,128]{1,0:T(8,128)} %bitcast.42, ...), custom_call_target="tpu_custom_call" | custom-call | flops 4000000000 | bytes 6000000 | tf_op jit(solution)/shard_map/coupling_update/pallas_call | solution.py:325
  52.6 1.3 %copy.40 = f32[1,1,3,512]{3,1,2,0:T(1,128)} copy(f32[1,1,3,512]{3,2,1,0:T(4,128)} %bitcast.41) | data formatting | bytes 12288
  53.9 1.3 %copy.41 = f32[1,1,3,512]{3,1,2,0:T(1,128)} copy(f32[1,1,3,512]{3,2,1,0:T(4,128)} %bitcast.40) | data formatting | bytes 12288
  55.2 0.0 collective-permute-done.refs_0_
  55.2 0.0 collective-permute-done.1.refs_1_
  55.3 0.0 collective-permute-done.2.refs_3_
  55.3 0.0 collective-permute-done.3.refs_4_
  55.3 0.3 concatenate.8.own_ref
  55.6 0.4 copy-done.2
  56.0 0.1 copy-done.3
  56.1 0.1 copy-done.4
  56.2 0.1 copy-done.5
  56.2 5.8 %collective-permute-start.4 = (f32[40,8192]{1,0:T(8,128)S(1)}, f32[40,8192]{1,0:T(8,128)}, u32[]{:S(2)}, u32[]{:S(2)}) collective-permute-start(f32[40,8192]{1,0:T(8,128)S(1)} %concatenate.8.own_ref), channel_id=1, source_target_pairs={{0,1},{1,2},{2,3},{4,5},{5,6},{6,7},{8,9},{9,10},{10,11},{12,13},{... | collective-permute-start | bytes 3932168 | tf_op jit(solution)/shard_map/ppermute | solution.py:340
  62.1 2.1 %collective-permute-start.5 = (f32[40,8192]{1,0:T(8,128)S(1)}, f32[40,8192]{1,0:T(8,128)}, u32[]{:S(2)}, u32[]{:S(2)}) collective-permute-start(f32[40,8192]{1,0:T(8,128)S(1)} %concatenate.8.own_ref), channel_id=1, source_target_pairs={{1,0},{2,1},{3,2},{5,4},{6,5},{7,6},{9,8},{10,9},{11,10},{13,12},{... | collective-permute-start | bytes 3932168 | tf_op jit(solution)/shard_map/ppermute | solution.py:340
  64.2 20.9 %own_layer.1.sums_ref = f32[8,8192]{1,0:T(8,128)} custom-call(s32[64,15]{1,0:T(8,128)} %bitcast.35, s32[32]{0:T(128)} %bitcast.44, bf16[64,256,64]{2,1,0:T(8,128)(2,1)} %own_table.1.lhs_ref, f32[8,8192]{1,0:T(8,128)} %copy-done.2, f32[8,8192]{1,0:T(8,128)} %copy-done.3, f32[8,8192]{1,0:T(8,128)} %copy-done.1, f32[8,8192]{1,0:T(8,128)} %copy-done.4, ...), custom_call_target="tpu_custom_call" | custom-call | flops 17999998976 | bytes 6000000 | tf_op jit(solution)/shard_map/own_layer/pallas_call | solution.py:192
  85.1 0.0 copy-done
  85.1 0.0 collective-permute-done.4.below_ref
  85.1 0.0 collective-permute-done.5.above_ref
  85.1 33.2 %other_layer.1 = (f32[3,8192]{1,0:T(4,128)}, f32[3,8192]{1,0:T(4,128)}) custom-call(s32[64,15]{1,0:T(8,128)} %bitcast.36, s32[32]{0:T(128)} %bitcast.45, s32[1]{0:T(128)} %bitcast.2.layer_ref, bf16[64,256,64]{2,1,0:T(8,128)(2,1)} %own_table.1.lhs_ref, f32[40,8192]{1,0:T(8,128)} %collective-permute-done.4.below_ref, f32[40,8192]{1,0:T(8,128)} %copy-done, ...), custom_call_target="tpu_custom_call" | custom-call | flops 35999997952 | bytes 6000000 | tf_op jit(solution)/shard_map/other_layer/pallas_call | solution.py:206
  118.3 1.6 %copy.38 = f32[1,1,3,8192]{3,1,2,0:T(1,128)} copy(f32[1,1,3,8192]{3,2,1,0:T(4,128)} %bitcast.34) | data formatting | bytes 196608
  119.9 1.6 %copy.39 = f32[1,1,3,8192]{3,1,2,0:T(1,128)} copy(f32[1,1,3,8192]{3,2,1,0:T(4,128)} %bitcast.33) | data formatting | bytes 196608
  (14 shorter events, 0.1 us)
Async XLA Ops:
  2.6 17.9 %copy-start.1 = (f32[8,8192]{1,0:T(8,128)}, f32[8,8192]{1,0:T(8,128)S(1)}, u32[]{:S(2)}) copy-start(f32[8,8192]{1,0:T(8,128)S(1)} %pad_maximum_fusion.field_ref.refs_2_) | copy-start | bytes 786436
  2.6 52.6 %collective-permute-start = (f32[8,8192]{1,0:T(8,128)S(1)}, f32[8,8192]{1,0:T(8,128)S(1)}, u32[]{:S(2)}, u32[]{:S(2)}) collective-permute-start(f32[8,8192]{1,0:T(8,128)S(1)} %pad_maximum_fusion.field_ref.refs_2_), channel_id=1, source_target_pairs={{0,8},{4,12},{8,16},{12,20},{16,24},{20,28},{24,32},{28,36},{32,40... | collective-permute-start | bytes 786440 | tf_op jit(solution)/shard_map/ppermute | solution.py:345
  6.3 49.0 %collective-permute-start.1 = (f32[8,8192]{1,0:T(8,128)S(1)}, f32[8,8192]{1,0:T(8,128)S(1)}, u32[]{:S(2)}, u32[]{:S(2)}) collective-permute-start(f32[8,8192]{1,0:T(8,128)S(1)} %pad_maximum_fusion.field_ref.refs_2_), channel_id=1, source_target_pairs={{0,4},{4,8},{8,12},{12,16},{16,20},{20,24},{24,28},{28,32},{32,36}... | collective-permute-start | bytes 786440 | tf_op jit(solution)/shard_map/ppermute | solution.py:345
  6.6 48.7 %collective-permute-start.2 = (f32[8,8192]{1,0:T(8,128)S(1)}, f32[8,8192]{1,0:T(8,128)S(1)}, u32[]{:S(2)}, u32[]{:S(2)}) collective-permute-start(f32[8,8192]{1,0:T(8,128)S(1)} %pad_maximum_fusion.field_ref.refs_2_), channel_id=1, source_target_pairs={{0,252},{4,0},{8,4},{12,8},{16,12},{20,16},{24,20},{28,24},{32,28}... | collective-permute-start | bytes 786440 | tf_op jit(solution)/shard_map/ppermute | solution.py:345
  14.1 41.2 %collective-permute-start.3 = (f32[8,8192]{1,0:T(8,128)S(1)}, f32[8,8192]{1,0:T(8,128)S(1)}, u32[]{:S(2)}, u32[]{:S(2)}) collective-permute-start(f32[8,8192]{1,0:T(8,128)S(1)} %pad_maximum_fusion.field_ref.refs_2_), channel_id=1, source_target_pairs={{0,248},{4,252},{8,0},{12,4},{16,8},{20,12},{24,16},{28,20},{32,24... | collective-permute-start | bytes 786440 | tf_op jit(solution)/shard_map/ppermute | solution.py:345
  20.5 14.6 %copy-start.8 = (f32[1,1,3,8192]{3,1,2,0:T(1,128)S(1)}, f32[1,1,3,8192]{3,1,2,0:T(1,128)}, u32[]{:S(2)}) copy-start(f32[1,1,3,8192]{3,1,2,0:T(1,128)} %param.20) | copy-start | bytes 294916
  20.5 14.6 %copy-start.9 = (f32[1,1,3,8192]{3,1,2,0:T(1,128)S(1)}, f32[1,1,3,8192]{3,1,2,0:T(1,128)}, u32[]{:S(2)}) copy-start(f32[1,1,3,8192]{3,1,2,0:T(1,128)} %param.17) | copy-start | bytes 294916
  25.8 21.5 %all-to-all-start = ((f32[6,64,8]{2,0,1:T(8,128)}), f32[6,64,8]{2,0,1:T(8,128)S(1)}, u32[]{:S(2)}, u32[]{:S(2)}) async-start(f32[6,64,8]{2,0,1:T(8,128)} %copy.36), calls=%async_computation | async-start | bytes 524288 | tf_op jit(solution)/shard_map/all_to_all | solution.py:377
  35.9 5.3 %copy-start.10 = (s32[1,1,64,15]{2,1,3,0:T(1,128)S(1)}, s32[1,1,64,15]{2,1,3,0:T(1,128)}, u32[]{:S(2)}) copy-start(s32[1,1,64,15]{2,1,3,0:T(1,128)} %param.21) | copy-start | bytes 11524
  35.9 6.0 %copy-start.11 = (f32[1,1,3,512]{3,1,2,0:T(1,128)S(1)}, f32[1,1,3,512]{3,1,2,0:T(1,128)}, u32[]{:S(2)}) copy-start(f32[1,1,3,512]{3,1,2,0:T(1,128)} %param.24) | copy-start | bytes 18436
  48.0 7.3 %copy-start.6 = (f32[1,1,8192]{2,1,0:T(1,128)S(1)}, f32[1,1,8192]{2,1,0:T(1,128)}, u32[]{:S(2)}) copy-start(f32[1,1,8192]{2,1,0:T(1,128)} %param.19) | copy-start | bytes 98308
  48.0 7.3 %copy-start.7 = (f32[1,1,8192]{2,1,0:T(1,128)S(1)}, f32[1,1,8192]{2,1,0:T(1,128)}, u32[]{:S(2)}) copy-start(f32[1,1,8192]{2,1,0:T(1,128)} %param.18) | copy-start | bytes 98308
  55.2 0.7 copy-start.2
  55.3 0.8 copy-start.3
  55.3 0.9 copy-start.4
  55.3 0.9 copy-start.5
  56.2 28.9 %copy-start = (f32[40,8192]{1,0:T(8,128)}, f32[40,8192]{1,0:T(8,128)S(1)}, u32[]{:S(2)}) copy-start(f32[40,8192]{1,0:T(8,128)S(1)} %concatenate.8.own_ref) | copy-start | bytes 3932164
  56.2 28.9 %collective-permute-start.4 = (f32[40,8192]{1,0:T(8,128)S(1)}, f32[40,8192]{1,0:T(8,128)}, u32[]{:S(2)}, u32[]{:S(2)}) collective-permute-start(f32[40,8192]{1,0:T(8,128)S(1)} %concatenate.8.own_ref), channel_id=1, source_target_pairs={{0,1},{1,2},{2,3},{4,5},{5,6},{6,7},{8,9},{9,10},{10,11},{12,13},{... | collective-permute-start | bytes 3932168 | tf_op jit(solution)/shard_map/ppermute | solution.py:340
  62.1 23.0 %collective-permute-start.5 = (f32[40,8192]{1,0:T(8,128)S(1)}, f32[40,8192]{1,0:T(8,128)}, u32[]{:S(2)}, u32[]{:S(2)}) collective-permute-start(f32[40,8192]{1,0:T(8,128)S(1)} %concatenate.8.own_ref), channel_id=1, source_target_pairs={{1,0},{2,1},{3,2},{5,4},{6,5},{7,6},{9,8},{10,9},{11,10},{13,12},{... | collective-permute-start | bytes 3932168 | tf_op jit(solution)/shard_map/ppermute | solution.py:340

commit v3 on v2

--- a/solution.py
+++ b/solution.py
@@ -11,7 +11,7 @@
 force_scale = -0.125 * log_scale * math.exp(1.0 / 9.0)
 f32 = jnp.float32
 bf16 = jnp.bfloat16
-UNROLL = 8
+UNROLL = 16
 UNROLL_OTHER = 8
 OWN_GROUP = 2
 own_slots = (1, 4, 7, 10, 13)
@@ -101,7 +101,7 @@
         rhs, sums = [], []
         for place in range(start, min(start + group, len(slots))):
             slot = slots[place]
-            name = names_ref[tile, slot]
+            name = names_ref[slot, tile]
             lanes = pl.ds(pl.multiple_of((name % 64) * TILE, TILE), TILE)
             top = table_ref[place, 0:16, lanes]
             low = table_ref[place, 16:32, lanes]
@@ -171,9 +171,12 @@
         inner = acc[0:3] - now * acc[6:7]
         outer = acc[3:6] - now * acc[7:8]
         force = force_scale * whole * (own[7:8] * inner + outer)
-        vel = vel_ref[:, lanes] + time_step * (force + body_ref[:, lanes] + react_ref[:, lanes])
-        vel_out_ref[:, lanes] = vel
-        disp_out_ref[:, lanes] = disp + time_step * vel
+        force += react_ref[:, lanes]
+        for c in range(3):
+            load = force[c : c + 1] + body_ref[c, :, lanes]
+            vel = vel_ref[c, :, lanes] + time_step * load
+            vel_out_ref[c, :, lanes] = vel
+            disp_out_ref[c, :, lanes] = disp[c : c + 1] + time_step * vel
         return carry
 
     lax.fori_loop(0, lhs_ref.shape[0], one_tile, 0, unroll=UNROLL_OTHER)
@@ -202,7 +205,7 @@
 
 def other_layer_update(names, flags, layer, lhs, below, own, above, sums, vel, body, react):
     points = own.shape[1]
-    shape = jax.ShapeDtypeStruct((3, points), f32)
+    shape = jax.ShapeDtypeStruct((3, 1, points), f32)
     return pl.pallas_call(
         other_layer_kernel,
         out_shape=(shape, shape),
@@ -228,11 +231,16 @@
     return jnp.where(row == index, 1.0, 0.0).astype(bf16)
 
 
+def slot_row(index_ref):
+    return jnp.concatenate([index_ref[c : c + 1, :] for c in range(index_ref.shape[0])], axis=1)
+
+
 across = (((1,), (1,)), ((), ()))
 
 
 def values_kernel(field_ref, blade_ref, rim_ref, root_ref, out_ref, pad_ref):
-    rim = rim_ref[...]
+    rim = slot_row(rim_ref)
+    root = slot_row(root_ref)
     tile_of = lax.shift_right_logical(rim, 7)
     lane_hot = one_hot(rim & 127, TILE)
 
@@ -249,9 +257,10 @@
     acc = lax.fori_loop(0, field_ref.shape[1] // (8 * TILE), one_batch, jnp.zeros((24, rim.shape[1]), f32))
     out_ref[0:3] = join32(acc)[3:6]
     pad_ref[...] = jnp.zeros_like(pad_ref)
-    pad_ref[0:3] = blade_ref[...]
+    for c in range(3):
+        pad_ref[c : c + 1] = blade_ref[c]
     found = jnp.dot(
-        parts32(pad_ref[...]).astype(bf16), one_hot(root_ref[...], blade_ref.shape[1]), preferred_element_type=f32
+        parts32(pad_ref[...]).astype(bf16), one_hot(root, blade_ref.shape[2]), preferred_element_type=f32
     )
     out_ref[3:6] = join32(found)[0:3]
 
@@ -259,8 +268,8 @@
 def coupling_values(field, blade, rim, root):
     return pl.pallas_call(
         values_kernel,
-        out_shape=jax.ShapeDtypeStruct((6, rim.shape[1]), f32),
-        scratch_shapes=[pltpu.VMEM((8, blade.shape[1]), f32)],
+        out_shape=jax.ShapeDtypeStruct((6, rim.shape[0] * rim.shape[1]), f32),
+        scratch_shapes=[pltpu.VMEM((8, blade.shape[2]), f32)],
         name="coupling_values",
         cost_estimate=cost(3_000_000_000),
     )(field, blade, rim, root)
@@ -268,10 +277,11 @@
 
 def coupling_kernel(
     swapped_ref, sent_ref, rim_ref, root_ref, nodes_ref, scale_ref, stiff_ref, blade_ref, vel_ref,
-    react_ref, disp_out_ref, vel_out_ref, pad_ref, elem_ref,
+    after_ref, react_ref, disp_out_ref, vel_out_ref, pad_ref, elem_ref,
 ):
-    nodes = blade_ref.shape[1]
-    rim = rim_ref[...]
+    nodes = blade_ref.shape[2]
+    rim = slot_row(rim_ref)
+    root = slot_row(root_ref)
     tile_of = lax.shift_right_logical(rim, 7)
     lane_hot = one_hot(rim & 127, TILE)
     pad_ref[...] = jnp.zeros_like(pad_ref)
@@ -292,9 +302,10 @@
     pad_ref[0:3] = spring * (swapped_ref[0:3] - sent_ref[3:6])
     loads = parts32(pad_ref[...]).astype(bf16)
     coupling = join32(
-        lax.dot_general(loads, one_hot(root_ref[...], nodes), across, preferred_element_type=f32)
-    )
-    pad_ref[0:3] = blade_ref[...]
+        lax.dot_general(loads, one_hot(root, nodes), across, preferred_element_type=f32)
+    )
+    for c in range(3):
+        pad_ref[c : c + 1] = blade_ref[c]
     blade = parts32(pad_ref[...]).astype(bf16)
     hots = []
     for q in range(8):
@@ -315,23 +326,24 @@
         total = total + jnp.where(row % 8 == q, put[0:24] + put[24:48] + put[48:72], 0.0)
     for a in range(3):
         internal = -jnp.sum(total[8 * a : 8 * a + 8], axis=0, keepdims=True)
-        vel = vel_ref[a : a + 1] + time_step * (internal + coupling[a : a + 1])
-        vel_out_ref[a : a + 1] = vel
-        disp_out_ref[a : a + 1] = blade_ref[a : a + 1] + time_step * vel
-
-
-def coupling_update(swapped, sent, rim, root, nodes, scale, stiff, blade, vel, points):
+        vel = vel_ref[a] + time_step * (internal + coupling[a : a + 1])
+        vel_out_ref[a] = vel
+        disp_out_ref[a] = blade_ref[a] + time_step * vel
+
+
+def coupling_update(swapped, sent, rim, root, nodes, scale, stiff, blade, vel, after, points):
     small = jax.ShapeDtypeStruct(blade.shape, f32)
     return pl.pallas_call(
         coupling_kernel,
         out_shape=(jax.ShapeDtypeStruct((3, points), f32), small, small),
         scratch_shapes=[
-            pltpu.VMEM((8, blade.shape[1]), f32),
+            pltpu.VMEM((8, blade.shape[2]), f32),
             pltpu.VMEM((24, nodes.shape[1]), f32),
         ],
+        in_specs=[vmem] * 9 + [pl.BlockSpec(memory_space=pl.ANY)],
         name="coupling_update",
         cost_estimate=cost(4_000_000_000),
-    )(swapped, sent, rim, root, nodes, scale, stiff, blade, vel)
+    )(swapped, sent, rim, root, nodes, scale, stiff, blade, vel, after)
 
 
 def shift_layer(value, by):
@@ -363,37 +375,42 @@
     rim_points,
 ):
     disk_now = disk_disp[0, 0]
-    blade_now = blade_disp[0, 0]
     field = jnp.concatenate([ref_pos[0, 0], disk_now, damage[0], modulus[0]], axis=0)
-    names = nbr_tiles[0, 0]
+    names = nbr_tiles[0, 0].T
     flags = break_flags[0, 0]
     far_behind = shift_sector(field, 2)
     behind = shift_sector(field, 1)
     ahead = shift_sector(field, -1)
     far_ahead = shift_sector(field, -2)
-    rim = rim_points[0, 0].reshape(1, -1)
-    root = root_nodes[0, 0].reshape(1, -1)
-    sent = coupling_values(field, blade_now, rim, root)
-    swapped = lax.all_to_all(sent, "blk", split_axis=1, concat_axis=1, tiled=True)
+    rim = rim_points[0, 0].T
+    root = root_nodes[0, 0].T
+    blade_rows = blade_disp.reshape(3, 1, -1)
+    sent = coupling_values(field, blade_rows, rim, root)
+    swapped = lax.all_to_all(
+        sent.reshape(6, rim.shape[0], rim.shape[1]), "blk", split_axis=2, concat_axis=2, tiled=True
+    )
     lhs = own_table(field)
     blocks = [far_behind, behind, field, ahead, far_ahead]
     own = jnp.concatenate(blocks, axis=0)
     below = shift_layer(own, 1)
     above = shift_layer(own, -1)
     sums = own_layer_sums(names, flags, lhs, blocks)
+    swapped, sums = lax.optimization_barrier((swapped, sums))
+    swapped = swapped.reshape(sent.shape)
     reaction, blade_disp_new, blade_vel_new = coupling_update(
-        swapped, sent, rim, root, elem_nodes[0, 0], elem_modulus[0], elem_stiff, blade_now,
-        blade_vel[0, 0], field.shape[1],
+        swapped, sent, rim, root, elem_nodes[0, 0], elem_modulus[0], elem_stiff, blade_rows,
+        blade_vel.reshape(3, 1, -1), sums, field.shape[1],
     )
     layer = lax.axis_index("layer").reshape(1).astype(jnp.int32)
     disk_disp_new, disk_vel_new = other_layer_update(
-        names, flags, layer, lhs, below, own, above, sums, disk_vel[0, 0], body_load[0, 0], reaction
+        names, flags, layer, lhs, below, own, above, sums, disk_vel.reshape(3, 1, -1),
+        body_load.reshape(3, 1, -1), reaction
     )
     return (
-        disk_disp_new[None, None],
-        disk_vel_new[None, None],
-        blade_disp_new[None, None],
-        blade_vel_new[None, None],
+        disk_disp_new.reshape(disk_disp.shape),
+        disk_vel_new.reshape(disk_vel.shape),
+        blade_disp_new.reshape(blade_disp.shape),
+        blade_vel_new.reshape(blade_vel.shape),
     )
 
 

time: 122 us -> 104 us (0.85)
  local copies, waits for them, and re-layouts: 16.6 us -> 6.13 us
  waiting for transfers between devices: 4.8 us -> 0.02 us
  starting transfers between devices: 30.9 us -> 29.3 us
    unnamed x35 -> x22, local copies, waits for them, and re-layouts: 12.6 us -> 3.41 us
    all_to_all x1, waiting for transfers between devices: 4.78 us -> 0.01 us  [on_device(): lax.all_to_all(sent.reshape(6, rim.shape[0], rim.shape[1]), 'blk', split_...]
    all_to_all x4 -> x0, local copies, waits for them, and re-layouts: 2.44 us -> none  [on_device(): lax.all_to_all(sent, 'blk', split_axis=1, concat_axis=1, tiled=True)]
    reshape x0 -> x3, local copies, waits for them, and re-layouts: none -> 2.33 us  [the longest x2 1.64 us: on_device(): sent.reshape(6, rim.shape[0], rim.shape[1])]
    ppermute x2, starting transfers between devices: 7.93 us -> 6.36 us  [shift_layer(): return lax.ppermute(value, 'layer', pairs)]
    another operation x2 -> x0, local copies, waits for them, and re-layouts: 1.34 us -> none  [the longest x1 0.67 us: on_device(): root = root_nodes[0, 0].reshape(1, -1)]
  transfers between devices with their start and end apart: 7 -> 7, of which waited for: 1 -> 0; matrix products, arithmetic and copies ran while one was open for 8% -> 3% of each run, Pallas kernels for 28% -> 32%
where the time goes in v3:
time: 104 us
  Pallas kernels  66.5 us (64%)
  starting transfers between devices  29.3 us (28%)
  local copies, waits for them, and re-layouts  6.13 us (6%)
    pallas_call x1, Pallas kernels, other_layer_update(): pl.pallas_call(other_layer_kernel, out_shape=(shape, shape), in_specs=[sm...  33.1 us
    pallas_call x1, Pallas kernels, own_layer_sums(): pl.pallas_call(own_layer_kernel, out_shape=jax.ShapeDtypeStruct((8, point...  19.8 us
    ppermute x4, starting transfers between devices, shift_sector(): lax.ppermute(value, 'blk', [(i, (i + by) % size) for i in range(size)])  13.7 us
    all_to_all x1, starting transfers between devices, on_device(): lax.all_to_all(sent.reshape(6, rim.shape[0], rim.shape[1]), 'blk', split_...  9.28 us
    ppermute x2, starting transfers between devices, shift_layer(): return lax.ppermute(value, 'layer', pairs)  6.36 us
    pallas_call x1, Pallas kernels, own_table(): pl.pallas_call(own_kernel, out_shape=jax.ShapeDtypeStruct((tiles, 2 * TIL...  5.27 us
    pallas_call x1, Pallas kernels, coupling_update(): pl.pallas_call(coupling_kernel, out_shape=(jax.ShapeDtypeStruct((3, point...  4.68 us
    pallas_call x1, Pallas kernels, coupling_values(): pl.pallas_call(values_kernel, out_shape=jax.ShapeDtypeStruct((6, rim.shap...  3.62 us
  transfers between devices with their start and end apart: 7, of which 0 were waited for; matrix products, arithmetic and copies ran while one was open for 3% of the time, Pallas kernels for 32%

profile of v3, /device:TPU:1, one launch (start us, length us, event | category | flops | bytes accessed | tf_op | source)
XLA Modules:
  0.0 103.6 jit_solution(6990918834515293504)
XLA Ops:
  0.6 1.1 %copy_bitcast_fusion = (f32[3,8192]{1,0:T(4,128)S(1)}, f32[3,8192]{1,0:T(4,128)S(1)}) fusion(f32[1,1,3,8192]{3,1,2,0:T(1,128)} %param.16, f32[1,1,3,8192]{3,1,2,0:T(1,128)} %param.15), kind=kLoop, calls=%fused_computation.1 | loop fusion | bytes 393216
  1.7 0.9 pad_maximum_fusion.field_ref.refs_2_
  2.6 0.0 copy-start.1
  2.6 3.7 %collective-permute-start = (f32[8,8192]{1,0:T(8,128)S(1)}, f32[8,8192]{1,0:T(8,128)S(1)}, u32[]{:S(2)}, u32[]{:S(2)}) collective-permute-start(f32[8,8192]{1,0:T(8,128)S(1)} %pad_maximum_fusion.field_ref.refs_2_), channel_id=1, source_target_pairs={{0,8},{4,12},{8,16},{12,20},{16,24},{20,28},{24,32},{28,36},{32,40... | collective-permute-start | bytes 786440 | tf_op jit(solution)/shard_map/ppermute | solution.py:357
  6.3 0.3 collective-permute-start.1
  6.6 7.5 %collective-permute-start.2 = (f32[8,8192]{1,0:T(8,128)S(1)}, f32[8,8192]{1,0:T(8,128)S(1)}, u32[]{:S(2)}, u32[]{:S(2)}) collective-permute-start(f32[8,8192]{1,0:T(8,128)S(1)} %pad_maximum_fusion.field_ref.refs_2_), channel_id=1, source_target_pairs={{0,252},{4,0},{8,4},{12,8},{16,12},{20,16},{24,20},{28,24},{32,28}... | collective-permute-start | bytes 786440 | tf_op jit(solution)/shard_map/ppermute | solution.py:357
  14.1 2.2 %collective-permute-start.3 = (f32[8,8192]{1,0:T(8,128)S(1)}, f32[8,8192]{1,0:T(8,128)S(1)}, u32[]{:S(2)}, u32[]{:S(2)}) collective-permute-start(f32[8,8192]{1,0:T(8,128)S(1)} %pad_maximum_fusion.field_ref.refs_2_), channel_id=1, source_target_pairs={{0,248},{4,252},{8,0},{12,4},{16,8},{20,12},{24,16},{28,20},{32,24... | collective-permute-start | bytes 786440 | tf_op jit(solution)/shard_map/ppermute | solution.py:357
  16.3 0.0 copy-done.1
  16.3 3.6 %coupling_values.1.sent_ref = f32[6,512]{1,0:T(8,128)} custom-call(f32[8,8192]{1,0:T(8,128)} %copy-done.1, f32[3,1,512]{2,1,0:T(1,128)} %bitcast.45, s32[8,64]{1,0:T(8,128)} %bitcast.48, s32[8,64]{1,0:T(8,128)} %bitcast.50), custom_call_target="tpu_custom_call" | custom-call | flops 3000000000 | bytes 6000000 | tf_op jit(solution)/shard_map/coupling_values/pallas_call | solution.py:269
  19.9 0.8 reshape.43
  20.7 0.8 copy.23
  21.6 9.3 %all-to-all-start = ((f32[6,8,64]{1,0,2:T(8,128)}), f32[6,8,64]{1,0,2:T(8,128)S(1)}, u32[]{:S(2)}, u32[]{:S(2)}) async-start(f32[6,8,64]{1,0,2:T(8,128)} %copy.23), calls=%async_computation | async-start | bytes 524288 | tf_op jit(solution)/shard_map/all_to_all | solution.py:389
  30.9 0.0 copy-start.8
  30.9 0.0 copy-start.6
  30.9 0.0 copy-start.7
  30.9 5.3 %own_table.1.lhs_ref = bf16[64,256,64]{2,1,0:T(8,128)(2,1)} custom-call(f32[8,8192]{1,0:T(8,128)} %copy-done.1), custom_call_target="tpu_custom_call" | custom-call | flops 8000000000 | bytes 4500000 | tf_op jit(solution)/shard_map/own_table/pallas_call | solution.py:68
  36.2 0.0 copy-done.8
  36.2 0.6 copy.35
  36.8 0.0 collective-permute-done.refs_0_
  36.8 0.0 copy-start.2
  36.8 0.0 collective-permute-done.1.refs_1_
  36.8 0.0 copy-start.3
  36.8 0.0 collective-permute-done.2.refs_3_
  36.8 0.0 copy-start.4
  36.8 0.0 collective-permute-done.3.refs_4_
  36.8 0.0 copy-done.6
  36.8 0.0 copy-done.7
  36.8 0.0 copy-start.5
  36.8 0.3 concatenate.8.own_ref
  37.1 0.3 copy-done.2
  37.5 0.1 copy-done.3
  37.6 0.1 copy-done.4
  37.7 0.1 copy-done.5
  37.8 0.0 copy-start
  37.8 4.3 %collective-permute-start.4 = (f32[40,8192]{1,0:T(8,128)S(1)}, f32[40,8192]{1,0:T(8,128)}, u32[]{:S(2)}, u32[]{:S(2)}) collective-permute-start(f32[40,8192]{1,0:T(8,128)S(1)} %concatenate.8.own_ref), channel_id=1, source_target_pairs={{0,1},{1,2},{2,3},{4,5},{5,6},{6,7},{8,9},{9,10},{10,11},{12,13},{... | collective-permute-start | bytes 3932168 | tf_op jit(solution)/shard_map/ppermute | solution.py:352
  42.0 2.1 %collective-permute-start.5 = (f32[40,8192]{1,0:T(8,128)S(1)}, f32[40,8192]{1,0:T(8,128)S(1)}, u32[]{:S(2)}, u32[]{:S(2)}) collective-permute-start(f32[40,8192]{1,0:T(8,128)S(1)} %concatenate.8.own_ref), channel_id=1, source_target_pairs={{1,0},{2,1},{3,2},{5,4},{6,5},{7,6},{9,8},{10,9},{11,10},{13,12},{... | collective-permute-start | bytes 3932168 | tf_op jit(solution)/shard_map/ppermute | solution.py:352
  44.1 19.8 %own_layer.1.after_ref.sums_ref = f32[8,8192]{1,0:T(8,128)} custom-call(s32[15,64]{1,0:T(8,128)} %bitcast.41, s32[32]{0:T(128)} %bitcast.54, bf16[64,256,64]{2,1,0:T(8,128)(2,1)} %own_table.1.lhs_ref, f32[8,8192]{1,0:T(8,128)} %copy-done.2, f32[8,8192]{1,0:T(8,128)} %copy-done.3, f32[8,8192]{1,0:T(8,128)} %copy-done.1, f32[8,8192]{1,0:T(8,128)} %copy-done.4, ...), custom_call_target="tpu_custom_call" | custom-call | flops 17999998976 | bytes 6000000 | tf_op jit(solution)/shard_map/own_layer/pallas_call | solution.py:195
  63.9 0.0 copy-done
  63.9 0.0 all-to-all-done
  63.9 0.1 copy.24
  64.0 0.7 reshape.46.swapped_ref
  64.7 4.7 %coupling_update.1 = (f32[3,8192]{1,0:T(4,128)}, f32[3,1,512]{2,1,0:T(1,128)}, f32[3,1,512]{2,1,0:T(1,128)}) custom-call(f32[6,512]{1,0:T(8,128)} %reshape.46.swapped_ref, f32[6,512]{1,0:T(8,128)} %coupling_values.1.sent_ref, s32[8,64]{1,0:T(8,128)} %bitcast.49, s32[8,64]{1,0:T(8,128)} %bitcast.51, s32[8,128]{1,0:T(8,128)} %bitcast.52, f32[1,128]{1,0:T(1,128)} %bitcast.53, ...), custom_call_target="tpu_custom_call" | custom-call | flops 4000000000 | bytes 6000000 | tf_op jit(solution)/shard_map/coupling_update/pallas_call | solution.py:336
  69.4 0.0 collective-permute-done.4.below_ref
  69.4 0.0 collective-permute-done.5.above_ref
  69.4 0.0 copy-start.9
  69.4 1.1 %copy-done.9 = f32[40,8192]{1,0:T(8,128)} copy-done((f32[40,8192]{1,0:T(8,128)}, f32[40,8192]{1,0:T(8,128)S(1)}, u32[]{:S(2)}) %copy-start.9) | copy-done | bytes 1310744
  70.5 33.1 %other_layer.1 = (f32[3,1,8192]{2,1,0:T(1,128)}, f32[3,1,8192]{2,1,0:T(1,128)}) custom-call(s32[15,64]{1,0:T(8,128)} %bitcast.42, s32[32]{0:T(128)} %bitcast.55, s32[1]{0:T(128)} %bitcast.2.layer_ref, bf16[64,256,64]{2,1,0:T(8,128)(2,1)} %own_table.1.lhs_ref, f32[40,8192]{1,0:T(8,128)} %collective-permute-done.4.below_ref, f32[40,8192]{1,0:T(8,128)} %copy-done, ...), custom_call_target="tpu_custom_call" | custom-call | flops 35999997952 | bytes 6000000 | tf_op jit(solution)/shard_map/other_layer/pallas_call | solution.py:209
Async XLA Ops:
  2.6 13.7 %copy-start.1 = (f32[8,8192]{1,0:T(8,128)}, f32[8,8192]{1,0:T(8,128)S(1)}, u32[]{:S(2)}) copy-start(f32[8,8192]{1,0:T(8,128)S(1)} %pad_maximum_fusion.field_ref.refs_2_) | copy-start | bytes 786436
  2.6 34.1 %collective-permute-start = (f32[8,8192]{1,0:T(8,128)S(1)}, f32[8,8192]{1,0:T(8,128)S(1)}, u32[]{:S(2)}, u32[]{:S(2)}) collective-permute-start(f32[8,8192]{1,0:T(8,128)S(1)} %pad_maximum_fusion.field_ref.refs_2_), channel_id=1, source_target_pairs={{0,8},{4,12},{8,16},{12,20},{16,24},{20,28},{24,32},{28,36},{32,40... | collective-permute-start | bytes 786440 | tf_op jit(solution)/shard_map/ppermute | solution.py:357
  6.3 30.5 %collective-permute-start.1 = (f32[8,8192]{1,0:T(8,128)S(1)}, f32[8,8192]{1,0:T(8,128)S(1)}, u32[]{:S(2)}, u32[]{:S(2)}) collective-permute-start(f32[8,8192]{1,0:T(8,128)S(1)} %pad_maximum_fusion.field_ref.refs_2_), channel_id=1, source_target_pairs={{0,4},{4,8},{8,12},{12,16},{16,20},{20,24},{24,28},{28,32},{32,36}... | collective-permute-start | bytes 786440 | tf_op jit(solution)/shard_map/ppermute | solution.py:357
  6.6 30.2 %collective-permute-start.2 = (f32[8,8192]{1,0:T(8,128)S(1)}, f32[8,8192]{1,0:T(8,128)S(1)}, u32[]{:S(2)}, u32[]{:S(2)}) collective-permute-start(f32[8,8192]{1,0:T(8,128)S(1)} %pad_maximum_fusion.field_ref.refs_2_), channel_id=1, source_target_pairs={{0,252},{4,0},{8,4},{12,8},{16,12},{20,16},{24,20},{28,24},{32,28}... | collective-permute-start | bytes 786440 | tf_op jit(solution)/shard_map/ppermute | solution.py:357
  14.1 22.7 %collective-permute-start.3 = (f32[8,8192]{1,0:T(8,128)S(1)}, f32[8,8192]{1,0:T(8,128)S(1)}, u32[]{:S(2)}, u32[]{:S(2)}) collective-permute-start(f32[8,8192]{1,0:T(8,128)S(1)} %pad_maximum_fusion.field_ref.refs_2_), channel_id=1, source_target_pairs={{0,248},{4,252},{8,0},{12,4},{16,8},{20,12},{24,16},{28,20},{32,24... | collective-permute-start | bytes 786440 | tf_op jit(solution)/shard_map/ppermute | solution.py:357
  21.6 42.4 %all-to-all-start = ((f32[6,8,64]{1,0,2:T(8,128)}), f32[6,8,64]{1,0,2:T(8,128)S(1)}, u32[]{:S(2)}, u32[]{:S(2)}) async-start(f32[6,8,64]{1,0,2:T(8,128)} %copy.23), calls=%async_computation | async-start | bytes 524288 | tf_op jit(solution)/shard_map/all_to_all | solution.py:389
  30.9 5.3 %copy-start.8 = (s32[1,1,64,15]{2,1,3,0:T(1,128)S(1)}, s32[1,1,64,15]{2,1,3,0:T(1,128)}, u32[]{:S(2)}) copy-start(s32[1,1,64,15]{2,1,3,0:T(1,128)} %param.21) | copy-start | bytes 11524
  30.9 5.9 %copy-start.6 = (f32[1,1,8192]{2,1,0:T(1,128)S(1)}, f32[1,1,8192]{2,1,0:T(1,128)}, u32[]{:S(2)}) copy-start(f32[1,1,8192]{2,1,0:T(1,128)} %param.19) | copy-start | bytes 98308
  30.9 5.9 %copy-start.7 = (f32[1,1,8192]{2,1,0:T(1,128)S(1)}, f32[1,1,8192]{2,1,0:T(1,128)}, u32[]{:S(2)}) copy-start(f32[1,1,8192]{2,1,0:T(1,128)} %param.18) | copy-start | bytes 98308
  36.8 0.7 copy-start.2
  36.8 0.8 copy-start.3
  36.8 0.9 copy-start.4
  36.8 0.9 copy-start.5
  37.8 26.2 %copy-start = (f32[40,8192]{1,0:T(8,128)}, f32[40,8192]{1,0:T(8,128)S(1)}, u32[]{:S(2)}) copy-start(f32[40,8192]{1,0:T(8,128)S(1)} %concatenate.8.own_ref) | copy-start | bytes 3932164
  37.8 31.6 %collective-permute-start.4 = (f32[40,8192]{1,0:T(8,128)S(1)}, f32[40,8192]{1,0:T(8,128)}, u32[]{:S(2)}, u32[]{:S(2)}) collective-permute-start(f32[40,8192]{1,0:T(8,128)S(1)} %concatenate.8.own_ref), channel_id=1, source_target_pairs={{0,1},{1,2},{2,3},{4,5},{5,6},{6,7},{8,9},{9,10},{10,11},{12,13},{... | collective-permute-start | bytes 3932168 | tf_op jit(solution)/shard_map/ppermute | solution.py:352
  42.0 27.4 %collective-permute-start.5 = (f32[40,8192]{1,0:T(8,128)S(1)}, f32[40,8192]{1,0:T(8,128)S(1)}, u32[]{:S(2)}, u32[]{:S(2)}) collective-permute-start(f32[40,8192]{1,0:T(8,128)S(1)} %concatenate.8.own_ref), channel_id=1, source_target_pairs={{1,0},{2,1},{3,2},{5,4},{6,5},{7,6},{9,8},{10,9},{11,10},{13,12},{... | collective-permute-start | bytes 3932168 | tf_op jit(solution)/shard_map/ppermute | solution.py:352
  69.4 1.1 %copy-start.9 = (f32[40,8192]{1,0:T(8,128)}, f32[40,8192]{1,0:T(8,128)S(1)}, u32[]{:S(2)}) copy-start(f32[40,8192]{1,0:T(8,128)S(1)} %collective-permute-done.5.above_ref) | copy-start | bytes 3932164

commit v4 on v3

--- a/solution.py
+++ b/solution.py
@@ -10,13 +10,13 @@
 log_scale = math.log2(math.e) / 9.0
 force_scale = -0.125 * log_scale * math.exp(1.0 / 9.0)
 f32 = jnp.float32
+across = (((1,), (1,)), ((), ()))
 bf16 = jnp.bfloat16
 UNROLL = 16
 UNROLL_OTHER = 8
-OWN_GROUP = 2
 own_slots = (1, 4, 7, 10, 13)
 other_slots = (0, 2, 3, 5, 6, 8, 9, 11, 12, 14)
-OWN_UNROLL = 4
+OWN_UNROLL = 8
 spring = 0.5
 time_step = 0.5
 
@@ -77,8 +77,11 @@
     def one(step, carry):
         lanes = pl.ds(pl.multiple_of(step * chunk, chunk), chunk)
         v = field_ref[row_start : row_start + 8, lanes]
-        row, disp, now, ref_norm, growth = point_terms(v)
-        terms = jnp.where(row < 6, v, jnp.where(row == 6, ref_norm, growth))
+        row = lax.broadcasted_iota(jnp.int32, v.shape, 0)
+        now = v + pltpu.roll(v, 5, 0)
+        grown = v * (v + jnp.where(row < 3, 0.0, 2.0 * pltpu.roll(v, 3, 0)))
+        summed = grown + pltpu.roll(grown, 7, 0) + pltpu.roll(grown, 6, 0)
+        terms = jnp.where(row < 6, v, jnp.where(row == 6, pltpu.roll(summed, 6, 0), pltpu.roll(summed, 4, 0)))
         high, middle, low = split3(terms)
         table_ref[place, 0:16, lanes] = jnp.concatenate([high, middle], axis=0).astype(bf16)
         table_ref[place, 16:32, lanes] = jnp.concatenate([low, high], axis=0).astype(bf16)
@@ -94,36 +97,40 @@
     lax.fori_loop(0, field_ref.shape[1] // chunk, one, 0)
 
 
-def pair_sums(tile, slots, table_ref, names_ref, word, lhs, group):
-    ones = jnp.ones((16, TILE), bf16)
+def slot_terms(tile, slot, place, table_ref, names_ref, word):
+    name = names_ref[slot, tile]
+    lanes = pl.ds(pl.multiple_of((name % 64) * TILE, TILE), TILE)
+    top = table_ref[place, 0:16, lanes]
+    low = table_ref[place, 16:32, lanes]
+    alive = 1 - (lax.shift_right_logical(word, (tile % 2) * 15 + slot) & 1)
+    q = table_ref[place, 32:48, lanes]
+    rhs = jnp.concatenate([top, top, low, jnp.ones((16, TILE), bf16)], axis=0)
+    return rhs, jnp.where(alive == 1, q, jnp.zeros_like(q))
+
+
+def pull_sums(lhs, rhs, sums):
+    both = jnp.dot(lhs, rhs, preferred_element_type=f32)
+    stretch = both[:TILE]
+    pull = both[TILE:] * jnp.exp2(stretch) / stretch
+    high = pull.astype(bf16)
+    low = (pull - high.astype(f32)).astype(bf16)
+    part = lax.dot_general(sums, high, across, preferred_element_type=f32)
+    return part + lax.dot_general(sums, low, across, preferred_element_type=f32)
+
+
+def pair_sums(tile, slots, table_ref, names_ref, word, lhs):
     acc = None
-    for start in range(0, len(slots), group):
-        rhs, sums = [], []
-        for place in range(start, min(start + group, len(slots))):
-            slot = slots[place]
-            name = names_ref[slot, tile]
-            lanes = pl.ds(pl.multiple_of((name % 64) * TILE, TILE), TILE)
-            top = table_ref[place, 0:16, lanes]
-            low = table_ref[place, 16:32, lanes]
-            alive = 1 - (lax.shift_right_logical(word, (tile % 2) * 15 + slot) & 1)
-            rhs.append(jnp.concatenate([top, top, low, ones], axis=0))
-            q = table_ref[place, 32:48, lanes]
-            sums.append(jnp.where(alive == 1, q, jnp.zeros_like(q)))
-        while len(rhs) < group:
-            rhs.append(rhs[-1])
-            sums.append(jnp.zeros_like(sums[-1]))
-        rhs = jnp.concatenate(rhs, axis=1)
-        sums = jnp.concatenate(sums, axis=1)
-        both = jnp.dot(lhs, rhs, preferred_element_type=f32)
-        stretch = both[:TILE]
-        pull = both[TILE:] * jnp.exp2(stretch) / stretch
-        high = pull.astype(bf16)
-        low = (pull - high.astype(f32)).astype(bf16)
-        dims = (((1,), (1,)), ((), ()))
-        part = lax.dot_general(sums, high, dims, preferred_element_type=f32)
-        part += lax.dot_general(sums, low, dims, preferred_element_type=f32)
+    for start in range(0, len(slots), 2):
+        terms = [
+            slot_terms(tile, slots[place], place, table_ref, names_ref, word) for place in (start, start + 1)
+        ]
+        part = pull_sums(
+            lhs,
+            jnp.concatenate([terms[0][0], terms[1][0]], axis=1),
+            jnp.concatenate([terms[0][1], terms[1][1]], axis=1),
+        )
         acc = part if acc is None else acc + part
-    return acc[0:8] + acc[8:16]
+    return acc
 
 
 def own_layer_kernel(names_ref, flags_ref, lhs_ref, *refs):
@@ -131,15 +138,38 @@
     for place, ref in enumerate(refs[:-2]):
         fill_table(ref, table_ref, 0, place, 512)
 
-    def one_tile(tile, carry):
-        lanes = pl.ds(pl.multiple_of(tile * TILE, TILE), TILE)
-        word = flags_ref[tile // 2]
-        out_ref[:, lanes] = pair_sums(
-            tile, own_slots, table_ref, names_ref, word, lhs_ref[tile], OWN_GROUP
+    last = len(own_slots) - 1
+
+    def two_tiles(pair, carry):
+        word = flags_ref[pair]
+        tiles = (2 * pair, 2 * pair + 1)
+        accs = [
+            pair_sums(tile, own_slots[:last], table_ref, names_ref, word, lhs_ref[tile]) for tile in tiles
+        ]
+        terms = [slot_terms(tile, own_slots[last], last, table_ref, names_ref, word) for tile in tiles]
+        none_rhs, none_sums = (jnp.zeros_like(part) for part in terms[0])
+        rhs = jnp.concatenate(
+            [
+                jnp.concatenate([terms[0][0], none_rhs], axis=1),
+                jnp.concatenate([none_rhs, terms[1][0]], axis=1),
+            ],
+            axis=0,
         )
+        sums = jnp.concatenate(
+            [
+                jnp.concatenate([terms[0][1], none_sums], axis=1),
+                jnp.concatenate([none_sums, terms[1][1]], axis=1),
+            ],
+            axis=0,
+        )
+        lhs = jnp.concatenate([lhs_ref[tiles[0]], lhs_ref[tiles[1]]], axis=1)
+        shared = pull_sums(lhs, rhs, sums)
+        for side, tile in enumerate(tiles):
+            acc = accs[side] + shared[16 * side : 16 * side + 16]
+            out_ref[:, pl.ds(pl.multiple_of(tile * TILE, TILE), TILE)] = acc[0:8] + acc[8:16]
         return carry
 
-    lax.fori_loop(0, lhs_ref.shape[0], one_tile, 0, unroll=UNROLL)
+    lax.fori_loop(0, lhs_ref.shape[0] // 2, two_tiles, 0, unroll=UNROLL // 2)
 
 
 def other_layer_kernel(
@@ -162,8 +192,8 @@
     def one_tile(tile, carry):
         lanes = pl.ds(pl.multiple_of(tile * TILE, TILE), TILE)
         word = flags_ref[tile // 2]
-        acc = pair_sums(tile, other_slots, table_ref, names_ref, word, lhs_ref[tile], 2)
-        acc += sums_ref[:, lanes]
+        acc = pair_sums(tile, other_slots, table_ref, names_ref, word, lhs_ref[tile])
+        acc = acc[0:8] + acc[8:16] + sums_ref[:, lanes]
         own = own_ref[16:24, lanes]
         disp = own[3:6]
         now = own[0:3] + disp
@@ -222,6 +252,16 @@
     return jnp.concatenate([high, middle, low, jnp.zeros_like(low)], axis=0)
 
 
+def parts16(value):
+    row = lax.broadcasted_iota(jnp.int32, value.shape, 0)
+    high, middle, low = split3(value)
+    return jnp.concatenate([jnp.where(row < 3, pltpu.roll(middle, 5, 0), high), low], axis=0)
+
+
+def join16(value):
+    return value[3:6] + value[0:3] + value[11:14]
+
+
 def join32(value):
     return value[0:8] + value[8:16] + value[16:24]
 
@@ -233,9 +273,6 @@
 
 def slot_row(index_ref):
     return jnp.concatenate([index_ref[c : c + 1, :] for c in range(index_ref.shape[0])], axis=1)
-
-
-across = (((1,), (1,)), ((), ()))
 
 
 def values_kernel(field_ref, blade_ref, rim_ref, root_ref, out_ref, pad_ref):
@@ -248,14 +285,14 @@
         rows = []
         for inner in range(8):
             start = pl.multiple_of(step * (8 * TILE) + inner * TILE, TILE)
-            rows.append(parts32(field_ref[:, pl.ds(start, TILE)]))
+            rows.append(parts16(field_ref[:, pl.ds(start, TILE)]))
         found = jnp.dot(jnp.concatenate(rows, axis=0).astype(bf16), lane_hot, preferred_element_type=f32)
         for inner in range(8):
-            acc = acc + jnp.where(tile_of == step * 8 + inner, found[inner * 32 : inner * 32 + 24], 0.0)
+            acc = acc + jnp.where(tile_of == step * 8 + inner, found[inner * 16 : inner * 16 + 16], 0.0)
         return acc
 
-    acc = lax.fori_loop(0, field_ref.shape[1] // (8 * TILE), one_batch, jnp.zeros((24, rim.shape[1]), f32))
-    out_ref[0:3] = join32(acc)[3:6]
+    acc = lax.fori_loop(0, field_ref.shape[1] // (8 * TILE), one_batch, jnp.zeros((16, rim.shape[1]), f32))
+    out_ref[0:3] = join16(acc)
     pad_ref[...] = jnp.zeros_like(pad_ref)
     for c in range(3):
         pad_ref[c : c + 1] = blade_ref[c]
@@ -285,8 +322,9 @@
     tile_of = lax.shift_right_logical(rim, 7)
     lane_hot = one_hot(rim & 127, TILE)
     pad_ref[...] = jnp.zeros_like(pad_ref)
-    pad_ref[0:3] = spring * (swapped_ref[3:6] - sent_ref[0:3])
-    back = parts32(pad_ref[...])
+    pad_ref[3:6] = spring * (swapped_ref[3:6] - sent_ref[0:3])
+    back = parts16(pad_ref[...])
+    pad_ref[...] = jnp.zeros_like(pad_ref)
 
     def one_batch(step, carry):
         rows = jnp.concatenate(
@@ -295,7 +333,7 @@
         put = lax.dot_general(rows.astype(bf16), lane_hot, across, preferred_element_type=f32)
         for inner in range(8):
             start = pl.multiple_of(step * (8 * TILE) + inner * TILE, TILE)
-            react_ref[:, pl.ds(start, TILE)] = join32(put[inner * 32 : inner * 32 + 32])[0:3]
+            react_ref[:, pl.ds(start, TILE)] = join16(put[inner * 16 : inner * 16 + 16])
         return carry
 
     lax.fori_loop(0, react_ref.shape[1] // (8 * TILE), one_batch, 0)
@@ -380,12 +418,13 @@
     flags = break_flags[0, 0]
     far_behind = shift_sector(field, 2)
     behind = shift_sector(field, 1)
-    ahead = shift_sector(field, -1)
-    far_ahead = shift_sector(field, -2)
     rim = rim_points[0, 0].T
     root = root_nodes[0, 0].T
     blade_rows = blade_disp.reshape(3, 1, -1)
     sent = coupling_values(field, blade_rows, rim, root)
+    later, sent = lax.optimization_barrier((field, sent))
+    ahead = shift_sector(later, -1)
+    far_ahead = shift_sector(later, -2)
     swapped = lax.all_to_all(
         sent.reshape(6, rim.shape[0], rim.shape[1]), "blk", split_axis=2, concat_axis=2, tiled=True
     )

time: 104 us -> 103 us (level)
  Pallas kernels: 66.5 us -> 62.2 us
  waiting for transfers between devices: 0.02 us -> 1.31 us
    pallas_call x1, Pallas kernels: 19.8 us -> 17.3 us  [own_layer_sums(): pl.pallas_call(own_layer_kernel, out_shape=jax.ShapeDtypeStruct((8, point...]
    ppermute x4, waiting for transfers between devices: 0.01 us -> 1.3 us  [shift_sector(): lax.ppermute(value, 'blk', [(i, (i + by) % size) for i in range(size)])]
  transfers between devices with their start and end apart: 7 -> 7, of which waited for: 0 -> 1; matrix products, arithmetic and copies ran while one was open for 3% -> 3% of each run, Pallas kernels for 32% -> 26%
where the time goes in v4:
time: 103 us; the launch traced here: 102 us
  Pallas kernels  62.2 us (60%)
  starting transfers between devices  29.9 us (29%)
  local copies, waits for them, and re-layouts  5.89 us (6%)
  other arithmetic  1.61 us (2%)
  waiting for transfers between devices  1.31 us (1%)
    pallas_call x1, Pallas kernels, other_layer_update(): pl.pallas_call(other_layer_kernel, out_shape=(shape, shape), in_specs=[sm...  32.5 us
    pallas_call x1, Pallas kernels, own_layer_sums(): pl.pallas_call(own_layer_kernel, out_shape=jax.ShapeDtypeStruct((8, point...  17.3 us
    ppermute x4, starting transfers between devices, shift_sector(): lax.ppermute(value, 'blk', [(i, (i + by) % size) for i in range(size)])  14.2 us
    all_to_all x1, starting transfers between devices, on_device(): lax.all_to_all(sent.reshape(6, rim.shape[0], rim.shape[1]), 'blk', split_...  9.47 us
    ppermute x2, starting transfers between devices, shift_layer(): return lax.ppermute(value, 'layer', pairs)  6.27 us
    pallas_call x1, Pallas kernels, own_table(): pl.pallas_call(own_kernel, out_shape=jax.ShapeDtypeStruct((tiles, 2 * TIL...  4.67 us
    pallas_call x1, Pallas kernels, coupling_update(): pl.pallas_call(coupling_kernel, out_shape=(jax.ShapeDtypeStruct((3, point...  4.37 us
    pallas_call x1, Pallas kernels, coupling_values(): pl.pallas_call(values_kernel, out_shape=jax.ShapeDtypeStruct((6, rim.shap...  3.36 us
  transfers between devices with their start and end apart: 7, of which 1 were waited for; matrix products, arithmetic and copies ran while one was open for 3% of the time, Pallas kernels for 26%

profile of v4, /device:TPU:1, one launch (start us, length us, event | category | flops | bytes accessed | tf_op | source)
XLA Modules:
  0.0 101.8 jit_solution(9068659879403818889)
XLA Ops:
  0.6 1.1 %copy_bitcast_fusion = (f32[3,8192]{1,0:T(4,128)S(1)}, f32[3,8192]{1,0:T(4,128)S(1)}) fusion(f32[1,1,3,8192]{3,1,2,0:T(1,128)} %param.16, f32[1,1,3,8192]{3,1,2,0:T(1,128)} %param.15), kind=kLoop, calls=%fused_computation.1 | loop fusion | bytes 393216
  1.7 1.6 %pad_maximum_fusion.field_ref.refs_2_ = f32[8,8192]{1,0:T(8,128)} fusion(f32[1,8192]{1,0:T(1,128)} %bitcast.37, f32[1,8192]{1,0:T(1,128)} %bitcast.39, f32[3,8192]{1,0:T(4,128)S(1)} %get-tuple-element.30, f32[3,8192]{1,0:T(4,128)S(1)} %get-tuple-element.31), kind=kLoop, calls=%fused_computation | loop fusion | flops 196608 | bytes 524288 | tf_op jit(solution)/shard_map/concatenate | solution.py:416
  3.3 0.0 copy-start.1
  3.3 3.4 %coupling_values.1.sent_ref = f32[6,512]{1,0:T(8,128)} custom-call(f32[8,8192]{1,0:T(8,128)} %pad_maximum_fusion.field_ref.refs_2_, f32[3,1,512]{2,1,0:T(1,128)} %bitcast.45, s32[8,64]{1,0:T(8,128)} %bitcast.48, s32[8,64]{1,0:T(8,128)} %bitcast.50), custom_call_target="tpu_custom_call" | custom-call | flops 3000000000 | bytes 6000000 | tf_op jit(solution)/shard_map/coupling_values/pallas_call | solution.py:306
  6.7 0.0 copy-done.1
  6.7 11.2 %collective-permute-start.2 = (f32[8,8192]{1,0:T(8,128)S(1)}, f32[8,8192]{1,0:T(8,128)S(1)}, u32[]{:S(2)}, u32[]{:S(2)}) collective-permute-start(f32[8,8192]{1,0:T(8,128)S(1)} %copy-done.1), channel_id=1, source_target_pairs={{0,252},{4,0},{8,4},{12,8},{16,12},{20,16},{24,20},{28,24},{32,28}... | collective-permute-start | bytes 786440 | tf_op jit(solution)/shard_map/ppermute | solution.py:395
  17.9 0.5 collective-permute-start.3
  18.4 2.5 %collective-permute-start = (f32[8,8192]{1,0:T(8,128)S(1)}, f32[8,8192]{1,0:T(8,128)S(1)}, u32[]{:S(2)}, u32[]{:S(2)}) collective-permute-start(f32[8,8192]{1,0:T(8,128)S(1)} %copy-done.1), channel_id=1, source_target_pairs={{0,8},{4,12},{8,16},{12,20},{16,24},{20,28},{24,32},{28,36},{32,40... | collective-permute-start | bytes 786440 | tf_op jit(solution)/shard_map/ppermute | solution.py:395
  20.9 0.0 collective-permute-start.1
  20.9 0.8 reshape.43
  21.7 0.8 copy.23
  22.5 9.5 %all-to-all-start = ((f32[6,8,64]{1,0,2:T(8,128)}), f32[6,8,64]{1,0,2:T(8,128)S(1)}, u32[]{:S(2)}, u32[]{:S(2)}) async-start(f32[6,8,64]{1,0,2:T(8,128)} %copy.23), calls=%async_computation | async-start | bytes 524288 | tf_op jit(solution)/shard_map/all_to_all | solution.py:428
  32.0 0.0 copy-start.8
  32.0 0.0 copy-start.6
  32.0 0.0 copy-start.7
  32.0 4.7 %own_table.1.lhs_ref = bf16[64,256,64]{2,1,0:T(8,128)(2,1)} custom-call(f32[8,8192]{1,0:T(8,128)} %pad_maximum_fusion.field_ref.refs_2_), custom_call_target="tpu_custom_call" | custom-call | flops 8000000000 | bytes 4500000 | tf_op jit(solution)/shard_map/own_table/pallas_call | solution.py:68
  36.7 0.0 copy-done.8
  36.7 0.6 copy.35
  37.3 0.0 collective-permute-done.2.refs_3_
  37.3 0.0 copy-start.2
  37.3 0.0 collective-permute-done.3.refs_4_
  37.3 0.0 copy-start.3
  37.3 0.0 collective-permute-done.refs_0_
  37.3 0.0 copy-start.4
  37.4 1.3 %collective-permute-done.1.refs_1_ = f32[8,8192]{1,0:T(8,128)S(1)} collective-permute-done((f32[8,8192]{1,0:T(8,128)S(1)}, f32[8,8192]{1,0:T(8,128)S(1)}, u32[]{:S(2)}, u32[]{:S(2)}) %collective-permute-start.1) | collective-permute-done | bytes 262176 | tf_op jit(solution)/shard_map/ppermute | solution.py:395
  38.7 0.0 copy-done.6
  38.7 0.0 copy-done.7
  38.7 0.0 copy-start.5
  38.7 0.3 concatenate.8.own_ref
  38.9 0.0 copy-done.2
  39.0 0.0 copy-done.3
  39.0 0.0 copy-done.4
  39.0 0.4 copy-done.5
  39.4 0.0 copy-start
  39.4 4.3 %collective-permute-start.4 = (f32[40,8192]{1,0:T(8,128)S(1)}, f32[40,8192]{1,0:T(8,128)}, u32[]{:S(2)}, u32[]{:S(2)}) collective-permute-start(f32[40,8192]{1,0:T(8,128)S(1)} %concatenate.8.own_ref), channel_id=1, source_target_pairs={{0,1},{1,2},{2,3},{4,5},{5,6},{6,7},{8,9},{9,10},{10,11},{12,13},{... | collective-permute-start | bytes 3932168 | tf_op jit(solution)/shard_map/ppermute | solution.py:390
  43.7 1.9 %collective-permute-start.5 = (f32[40,8192]{1,0:T(8,128)S(1)}, f32[40,8192]{1,0:T(8,128)S(1)}, u32[]{:S(2)}, u32[]{:S(2)}) collective-permute-start(f32[40,8192]{1,0:T(8,128)S(1)} %concatenate.8.own_ref), channel_id=1, source_target_pairs={{1,0},{2,1},{3,2},{5,4},{6,5},{7,6},{9,8},{10,9},{11,10},{13,12},{... | collective-permute-start | bytes 3932168 | tf_op jit(solution)/shard_map/ppermute | solution.py:390
  45.7 17.3 %own_layer.1.after_ref.sums_ref = f32[8,8192]{1,0:T(8,128)} custom-call(s32[15,64]{1,0:T(8,128)} %bitcast.41, s32[32]{0:T(128)} %bitcast.54, bf16[64,256,64]{2,1,0:T(8,128)(2,1)} %own_table.1.lhs_ref, f32[8,8192]{1,0:T(8,128)} %copy-done.4, f32[8,8192]{1,0:T(8,128)} %copy-done.5, f32[8,8192]{1,0:T(8,128)} %pad_maximum_fusion.field_ref.refs_2_, ...), custom_call_target="tpu_custom_call" | custom-call | flops 17999998976 | bytes 6000000 | tf_op jit(solution)/shard_map/own_layer/pallas_call | solution.py:225
  63.0 0.0 copy-done
  63.0 0.0 all-to-all-done
  63.0 0.1 copy.24
  63.1 0.7 reshape.46.swapped_ref
  63.8 4.4 %coupling_update.1 = (f32[3,8192]{1,0:T(4,128)}, f32[3,1,512]{2,1,0:T(1,128)}, f32[3,1,512]{2,1,0:T(1,128)}) custom-call(f32[6,512]{1,0:T(8,128)} %reshape.46.swapped_ref, f32[6,512]{1,0:T(8,128)} %coupling_values.1.sent_ref, s32[8,64]{1,0:T(8,128)} %bitcast.49, s32[8,64]{1,0:T(8,128)} %bitcast.51, s32[8,128]{1,0:T(8,128)} %bitcast.52, f32[1,128]{1,0:T(1,128)} %bitcast.53, ...), custom_call_target="tpu_custom_call" | custom-call | flops 4000000000 | bytes 6000000 | tf_op jit(solution)/shard_map/coupling_update/pallas_call | solution.py:374
  68.2 0.0 collective-permute-done.4.below_ref
  68.2 0.0 collective-permute-done.5.above_ref
  68.2 0.0 copy-start.9
  68.2 1.1 %copy-done.9 = f32[40,8192]{1,0:T(8,128)} copy-done((f32[40,8192]{1,0:T(8,128)}, f32[40,8192]{1,0:T(8,128)S(1)}, u32[]{:S(2)}) %copy-start.9) | copy-done | bytes 1310744
  69.2 32.5 %other_layer.1 = (f32[3,1,8192]{2,1,0:T(1,128)}, f32[3,1,8192]{2,1,0:T(1,128)}) custom-call(s32[15,64]{1,0:T(8,128)} %bitcast.42, s32[32]{0:T(128)} %bitcast.55, s32[1]{0:T(128)} %bitcast.2.layer_ref, bf16[64,256,64]{2,1,0:T(8,128)(2,1)} %own_table.1.lhs_ref, f32[40,8192]{1,0:T(8,128)} %collective-permute-done.4.below_ref, f32[40,8192]{1,0:T(8,128)} %copy-done, ...), custom_call_target="tpu_custom_call" | custom-call | flops 35999997952 | bytes 6000000 | tf_op jit(solution)/shard_map/other_layer/pallas_call | solution.py:239
Async XLA Ops:
  3.3 3.4 %copy-start.1 = (f32[8,8192]{1,0:T(8,128)S(1)}, f32[8,8192]{1,0:T(8,128)}, u32[]{:S(2)}) copy-start(f32[8,8192]{1,0:T(8,128)} %pad_maximum_fusion.field_ref.refs_2_) | copy-start | bytes 786436
  6.7 30.6 %collective-permute-start.2 = (f32[8,8192]{1,0:T(8,128)S(1)}, f32[8,8192]{1,0:T(8,128)S(1)}, u32[]{:S(2)}, u32[]{:S(2)}) collective-permute-start(f32[8,8192]{1,0:T(8,128)S(1)} %copy-done.1), channel_id=1, source_target_pairs={{0,252},{4,0},{8,4},{12,8},{16,12},{20,16},{24,20},{28,24},{32,28}... | collective-permute-start | bytes 786440 | tf_op jit(solution)/shard_map/ppermute | solution.py:395
  17.9 19.4 %collective-permute-start.3 = (f32[8,8192]{1,0:T(8,128)S(1)}, f32[8,8192]{1,0:T(8,128)S(1)}, u32[]{:S(2)}, u32[]{:S(2)}) collective-permute-start(f32[8,8192]{1,0:T(8,128)S(1)} %copy-done.1), channel_id=1, source_target_pairs={{0,248},{4,252},{8,0},{12,4},{16,8},{20,12},{24,16},{28,20},{32,24... | collective-permute-start | bytes 786440 | tf_op jit(solution)/shard_map/ppermute | solution.py:395
  18.4 18.9 %collective-permute-start = (f32[8,8192]{1,0:T(8,128)S(1)}, f32[8,8192]{1,0:T(8,128)S(1)}, u32[]{:S(2)}, u32[]{:S(2)}) collective-permute-start(f32[8,8192]{1,0:T(8,128)S(1)} %copy-done.1), channel_id=1, source_target_pairs={{0,8},{4,12},{8,16},{12,20},{16,24},{20,28},{24,32},{28,36},{32,40... | collective-permute-start | bytes 786440 | tf_op jit(solution)/shard_map/ppermute | solution.py:395
  20.9 17.8 %collective-permute-start.1 = (f32[8,8192]{1,0:T(8,128)S(1)}, f32[8,8192]{1,0:T(8,128)S(1)}, u32[]{:S(2)}, u32[]{:S(2)}) collective-permute-start(f32[8,8192]{1,0:T(8,128)S(1)} %copy-done.1), channel_id=1, source_target_pairs={{0,4},{4,8},{8,12},{12,16},{16,20},{20,24},{24,28},{28,32},{32,36}... | collective-permute-start | bytes 786440 | tf_op jit(solution)/shard_map/ppermute | solution.py:395
  22.5 40.4 %all-to-all-start = ((f32[6,8,64]{1,0,2:T(8,128)}), f32[6,8,64]{1,0,2:T(8,128)S(1)}, u32[]{:S(2)}, u32[]{:S(2)}) async-start(f32[6,8,64]{1,0,2:T(8,128)} %copy.23), calls=%async_computation | async-start | bytes 524288 | tf_op jit(solution)/shard_map/all_to_all | solution.py:428
  32.0 4.7 %copy-start.8 = (s32[1,1,64,15]{2,1,3,0:T(1,128)S(1)}, s32[1,1,64,15]{2,1,3,0:T(1,128)}, u32[]{:S(2)}) copy-start(s32[1,1,64,15]{2,1,3,0:T(1,128)} %param.21) | copy-start | bytes 11524
  32.0 6.6 %copy-start.6 = (f32[1,1,8192]{2,1,0:T(1,128)S(1)}, f32[1,1,8192]{2,1,0:T(1,128)}, u32[]{:S(2)}) copy-start(f32[1,1,8192]{2,1,0:T(1,128)} %param.19) | copy-start | bytes 98308
  32.0 6.6 %copy-start.7 = (f32[1,1,8192]{2,1,0:T(1,128)S(1)}, f32[1,1,8192]{2,1,0:T(1,128)}, u32[]{:S(2)}) copy-start(f32[1,1,8192]{2,1,0:T(1,128)} %param.18) | copy-start | bytes 98308
  37.3 1.6 %copy-start.2 = (f32[8,8192]{1,0:T(8,128)}, f32[8,8192]{1,0:T(8,128)S(1)}, u32[]{:S(2)}) copy-start(f32[8,8192]{1,0:T(8,128)S(1)} %collective-permute-done.2.refs_3_) | copy-start | bytes 786436
  37.3 1.6 %copy-start.3 = (f32[8,8192]{1,0:T(8,128)}, f32[8,8192]{1,0:T(8,128)S(1)}, u32[]{:S(2)}) copy-start(f32[8,8192]{1,0:T(8,128)S(1)} %collective-permute-done.3.refs_4_) | copy-start | bytes 786436
  37.3 1.6 %copy-start.4 = (f32[8,8192]{1,0:T(8,128)}, f32[8,8192]{1,0:T(8,128)S(1)}, u32[]{:S(2)}) copy-start(f32[8,8192]{1,0:T(8,128)S(1)} %collective-permute-done.refs_0_) | copy-start | bytes 786436
  38.7 0.7 copy-start.5
  39.4 23.6 %copy-start = (f32[40,8192]{1,0:T(8,128)}, f32[40,8192]{1,0:T(8,128)S(1)}, u32[]{:S(2)}) copy-start(f32[40,8192]{1,0:T(8,128)S(1)} %concatenate.8.own_ref) | copy-start | bytes 3932164
  39.4 28.8 %collective-permute-start.4 = (f32[40,8192]{1,0:T(8,128)S(1)}, f32[40,8192]{1,0:T(8,128)}, u32[]{:S(2)}, u32[]{:S(2)}) collective-permute-start(f32[40,8192]{1,0:T(8,128)S(1)} %concatenate.8.own_ref), channel_id=1, source_target_pairs={{0,1},{1,2},{2,3},{4,5},{5,6},{6,7},{8,9},{9,10},{10,11},{12,13},{... | collective-permute-start | bytes 3932168 | tf_op jit(solution)/shard_map/ppermute | solution.py:390
  43.7 24.4 %collective-permute-start.5 = (f32[40,8192]{1,0:T(8,128)S(1)}, f32[40,8192]{1,0:T(8,128)S(1)}, u32[]{:S(2)}, u32[]{:S(2)}) collective-permute-start(f32[40,8192]{1,0:T(8,128)S(1)} %concatenate.8.own_ref), channel_id=1, source_target_pairs={{1,0},{2,1},{3,2},{5,4},{6,5},{7,6},{9,8},{10,9},{11,10},{13,12},{... | collective-permute-start | bytes 3932168 | tf_op jit(solution)/shard_map/ppermute | solution.py:390
  68.2 1.1 %copy-start.9 = (f32[40,8192]{1,0:T(8,128)}, f32[40,8192]{1,0:T(8,128)S(1)}, u32[]{:S(2)}) copy-start(f32[40,8192]{1,0:T(8,128)S(1)} %collective-permute-done.5.above_ref) | copy-start | bytes 3932164

commit v5 on v4

--- a/solution.py
+++ b/solution.py
@@ -275,7 +275,14 @@
     return jnp.concatenate([index_ref[c : c + 1, :] for c in range(index_ref.shape[0])], axis=1)
 
 
-def values_kernel(field_ref, blade_ref, rim_ref, root_ref, out_ref, pad_ref):
+def values_kernel(
+    pos_ref, disp_ref, damage_ref, modulus_ref, blade_ref, rim_ref, root_ref, field_ref, out_ref, pad_ref
+):
+    for c in range(3):
+        field_ref[c : c + 1, :] = pos_ref[c]
+        field_ref[3 + c : 4 + c, :] = disp_ref[c]
+    field_ref[6:7, :] = damage_ref[...]
+    field_ref[7:8, :] = modulus_ref[...]
     rim = slot_row(rim_ref)
     root = slot_row(root_ref)
     tile_of = lax.shift_right_logical(rim, 7)
@@ -292,24 +299,34 @@
         return acc
 
     acc = lax.fori_loop(0, field_ref.shape[1] // (8 * TILE), one_batch, jnp.zeros((16, rim.shape[1]), f32))
-    out_ref[0:3] = join16(acc)
+    at_rim = join16(acc)
     pad_ref[...] = jnp.zeros_like(pad_ref)
     for c in range(3):
         pad_ref[c : c + 1] = blade_ref[c]
     found = jnp.dot(
         parts32(pad_ref[...]).astype(bf16), one_hot(root, blade_ref.shape[2]), preferred_element_type=f32
     )
-    out_ref[3:6] = join32(found)[0:3]
-
-
-def coupling_values(field, blade, rim, root):
+    values = jnp.concatenate([at_rim, join32(found)[0:3]], axis=0)
+    width = rim_ref.shape[1]
+    for c in range(rim_ref.shape[0]):
+        out_ref[:, c, :] = values[:, c * width : (c + 1) * width]
+
+
+def coupling_values(pos, disp, damage, modulus, blade, rim, root):
     return pl.pallas_call(
         values_kernel,
-        out_shape=jax.ShapeDtypeStruct((6, rim.shape[0] * rim.shape[1]), f32),
+        out_shape=(
+            jax.ShapeDtypeStruct((8, pos.shape[2]), f32),
+            jax.ShapeDtypeStruct((6, *rim.shape), f32),
+        ),
         scratch_shapes=[pltpu.VMEM((8, blade.shape[2]), f32)],
         name="coupling_values",
         cost_estimate=cost(3_000_000_000),
-    )(field, blade, rim, root)
+    )(pos, disp, damage, modulus, blade, rim, root)
+
+
+def slot_values(values_ref):
+    return jnp.concatenate([values_ref[:, c, :] for c in range(values_ref.shape[1])], axis=1)
 
 
 def coupling_kernel(
@@ -322,7 +339,9 @@
     tile_of = lax.shift_right_logical(rim, 7)
     lane_hot = one_hot(rim & 127, TILE)
     pad_ref[...] = jnp.zeros_like(pad_ref)
-    pad_ref[3:6] = spring * (swapped_ref[3:6] - sent_ref[0:3])
+    swapped = slot_values(swapped_ref)
+    sent = slot_values(sent_ref)
+    pad_ref[3:6] = spring * (swapped[3:6] - sent[0:3])
     back = parts16(pad_ref[...])
     pad_ref[...] = jnp.zeros_like(pad_ref)
 
@@ -337,7 +356,7 @@
         return carry
 
     lax.fori_loop(0, react_ref.shape[1] // (8 * TILE), one_batch, 0)
-    pad_ref[0:3] = spring * (swapped_ref[0:3] - sent_ref[3:6])
+    pad_ref[0:3] = spring * (swapped[0:3] - sent[3:6])
     loads = parts32(pad_ref[...]).astype(bf16)
     coupling = join32(
         lax.dot_general(loads, one_hot(root, nodes), across, preferred_element_type=f32)
@@ -382,6 +401,29 @@
         name="coupling_update",
         cost_estimate=cost(4_000_000_000),
     )(swapped, sent, rim, root, nodes, scale, stiff, blade, vel, after)
+
+
+def stack_kernel(*refs):
+    out_ref, sems = refs[-2:]
+    copies = []
+    for place, ref in enumerate(refs[:-2]):
+        copies.append(pltpu.make_async_copy(ref, out_ref.at[pl.ds(8 * place, 8), :], sems.at[place]))
+    for copy in copies:
+        copy.start()
+    for copy in copies:
+        copy.wait()
+
+
+def stacked(blocks):
+    raw = pl.BlockSpec(memory_space=pl.ANY)
+    return pl.pallas_call(
+        stack_kernel,
+        out_shape=jax.ShapeDtypeStruct((8 * len(blocks), blocks[0].shape[1]), f32),
+        in_specs=[raw] * len(blocks),
+        out_specs=raw,
+        scratch_shapes=[pltpu.SemaphoreType.DMA((len(blocks),))],
+        name="stacked",
+    )(*blocks)
 
 
 def shift_layer(value, by):
@@ -412,30 +454,26 @@
     root_nodes,
     rim_points,
 ):
-    disk_now = disk_disp[0, 0]
-    field = jnp.concatenate([ref_pos[0, 0], disk_now, damage[0], modulus[0]], axis=0)
     names = nbr_tiles[0, 0].T
     flags = break_flags[0, 0]
-    far_behind = shift_sector(field, 2)
-    behind = shift_sector(field, 1)
     rim = rim_points[0, 0].T
     root = root_nodes[0, 0].T
     blade_rows = blade_disp.reshape(3, 1, -1)
-    sent = coupling_values(field, blade_rows, rim, root)
-    later, sent = lax.optimization_barrier((field, sent))
-    ahead = shift_sector(later, -1)
-    far_ahead = shift_sector(later, -2)
-    swapped = lax.all_to_all(
-        sent.reshape(6, rim.shape[0], rim.shape[1]), "blk", split_axis=2, concat_axis=2, tiled=True
-    )
+    field, sent = coupling_values(
+        ref_pos.reshape(3, 1, -1), disk_disp.reshape(3, 1, -1), damage[0], modulus[0], blade_rows, rim, root
+    )
+    ahead = shift_sector(field, -1)
+    far_ahead = shift_sector(field, -2)
+    far_behind = shift_sector(field, 2)
+    behind = shift_sector(field, 1)
+    swapped = lax.all_to_all(sent, "blk", split_axis=2, concat_axis=2, tiled=True)
     lhs = own_table(field)
     blocks = [far_behind, behind, field, ahead, far_ahead]
-    own = jnp.concatenate(blocks, axis=0)
+    own = stacked(blocks)
     below = shift_layer(own, 1)
     above = shift_layer(own, -1)
     sums = own_layer_sums(names, flags, lhs, blocks)
     swapped, sums = lax.optimization_barrier((swapped, sums))
-    swapped = swapped.reshape(sent.shape)
     reaction, blade_disp_new, blade_vel_new = coupling_update(
         swapped, sent, rim, root, elem_nodes[0, 0], elem_modulus[0], elem_stiff, blade_rows,
         blade_vel.reshape(3, 1, -1), sums, field.shape[1],

time: 103 us -> 139 us (1.35)
  Pallas kernels: 62.2 us -> 103 us
  other arithmetic: 1.61 us -> 0 us
    pallas_call x1 -> x2, Pallas kernels: 3.36 us -> 44.3 us  [the longest x1 40.8 us: stacked(): pl.pallas_call(stack_kernel, out_shape=jax.ShapeDtypeStruct((8 * len(bloc...]
    reshape x3 -> x0, local copies, waits for them, and re-layouts: 2.33 us -> none  [the longest x2 1.64 us: on_device(): sent.reshape(6, rim.shape[0], rim.shape[1])]
    concatenate x1 -> x0, other arithmetic: 1.61 us -> none  [on_device(): jnp.concatenate([ref_pos[0, 0], disk_now, damage[0], modulus[0]], axis=0)]
    pallas_call x0 -> x1, local copies, waits for them, and re-layouts: none -> 1.58 us  [coupling_values(): pl.pallas_call(values_kernel, out_shape=(jax.ShapeDtypeStruct((8, pos.sha...]
    unnamed x22 -> x15, local copies, waits for them, and re-layouts: 3.17 us -> 3.63 us
  transfers between devices with their start and end apart: 7 -> 7, of which waited for: 1 -> 0; matrix products, arithmetic and copies ran while one was open for 3% -> 2% of each run, Pallas kernels for 26% -> 48%
where the time goes in v5:
time: 139 us
  Pallas kernels  103 us (74%)
  starting transfers between devices  29.1 us (21%)
  local copies, waits for them, and re-layouts  5.95 us (4%)
    pallas_call x1, Pallas kernels, stacked(): pl.pallas_call(stack_kernel, out_shape=jax.ShapeDtypeStruct((8 * len(bloc...  40.8 us
    pallas_call x1, Pallas kernels, other_layer_update(): pl.pallas_call(other_layer_kernel, out_shape=(shape, shape), in_specs=[sm...  32.5 us
    pallas_call x1, Pallas kernels, own_layer_sums(): pl.pallas_call(own_layer_kernel, out_shape=jax.ShapeDtypeStruct((8, point...  17.3 us
    ppermute x4, starting transfers between devices, shift_sector(): lax.ppermute(value, 'blk', [(i, (i + by) % size) for i in range(size)])  13.6 us
    all_to_all x1, starting transfers between devices, on_device(): lax.all_to_all(sent, 'blk', split_axis=2, concat_axis=2, tiled=True)  9.27 us
    ppermute x2, starting transfers between devices, shift_layer(): return lax.ppermute(value, 'layer', pairs)  6.19 us
    pallas_call x1, Pallas kernels, own_table(): pl.pallas_call(own_kernel, out_shape=jax.ShapeDtypeStruct((tiles, 2 * TIL...  4.68 us
    pallas_call x1, Pallas kernels, coupling_update(): pl.pallas_call(coupling_kernel, out_shape=(jax.ShapeDtypeStruct((3, point...  4.39 us
  transfers between devices with their start and end apart: 7, of which 0 were waited for; matrix products, arithmetic and copies ran while one was open for 2% of the time, Pallas kernels for 48%

profile of v5, /device:TPU:1, one launch (start us, length us, event | category | flops | bytes accessed | tf_op | source)
XLA Modules:
  0.0 139.0 jit_solution(14706732429470015212)
XLA Ops:
  0.6 3.5 %coupling_values.1 = (f32[8,8192]{1,0:T(8,128)}, f32[6,8,64]{2,1,0:T(8,128)}) custom-call(f32[3,1,8192]{2,1,0:T(1,128)} %bitcast.37, f32[3,1,8192]{2,1,0:T(1,128)} %bitcast.38, f32[1,8192]{1,0:T(1,128)} %bitcast.41, f32[1,8192]{1,0:T(1,128)} %bitcast.42, f32[3,1,512]{2,1,0:T(1,128)} %bitcast.43, s32[8,64]{1,0:T(8,128)} %bitcast.46, s32[8,64]{1,0:T(8,128)} %bitcast.48), custom_call_target="tpu_custom_call" | custom-call | flops 3000000000 | bytes 6000000 | tf_op jit(solution)/shard_map/coupling_values/pallas_call | solution.py:316
  4.1 3.6 %collective-permute-start = (f32[8,8192]{1,0:T(8,128)}, f32[8,8192]{1,0:T(8,128)S(1)}, u32[]{:S(2)}, u32[]{:S(2)}) collective-permute-start(f32[8,8192]{1,0:T(8,128)} %get-tuple-element.13.field_ref.refs_2_), channel_id=1, source_target_pairs={{0,8},{4,12},{8,16},{12,20},{16,24},{20,28},{24,32},{28,36},{32,40... | collective-permute-start | bytes 786440 | tf_op jit(solution)/shard_map/ppermute | solution.py:437
  7.7 0.3 collective-permute-start.1
  8.0 7.4 %collective-permute-start.2 = (f32[8,8192]{1,0:T(8,128)}, f32[8,8192]{1,0:T(8,128)S(1)}, u32[]{:S(2)}, u32[]{:S(2)}) collective-permute-start(f32[8,8192]{1,0:T(8,128)} %get-tuple-element.13.field_ref.refs_2_), channel_id=1, source_target_pairs={{0,252},{4,0},{8,4},{12,8},{16,12},{20,16},{24,20},{28,24},{32,28}... | collective-permute-start | bytes 786440 | tf_op jit(solution)/shard_map/ppermute | solution.py:437
  15.4 2.3 %collective-permute-start.3 = (f32[8,8192]{1,0:T(8,128)}, f32[8,8192]{1,0:T(8,128)S(1)}, u32[]{:S(2)}, u32[]{:S(2)}) collective-permute-start(f32[8,8192]{1,0:T(8,128)} %get-tuple-element.13.field_ref.refs_2_), channel_id=1, source_target_pairs={{0,248},{4,252},{8,0},{12,4},{16,8},{20,12},{24,16},{28,20},{32,24... | collective-permute-start | bytes 786440 | tf_op jit(solution)/shard_map/ppermute | solution.py:437
  17.7 1.6 %copy.23 = f32[6,8,64]{1,0,2:T(8,128)} copy(f32[6,8,64]{2,1,0:T(8,128)} %get-tuple-element.14.sent_ref) | data formatting | bytes 24576 | tf_op jit(solution)/shard_map/coupling_values/pallas_call | solution.py:316
  19.3 9.3 %all-to-all-start = ((f32[6,8,64]{1,0,2:T(8,128)}), f32[6,8,64]{1,0,2:T(8,128)S(1)}, u32[]{:S(2)}, u32[]{:S(2)}) async-start(f32[6,8,64]{1,0,2:T(8,128)} %copy.23), calls=%async_computation | async-start | bytes 524288 | tf_op jit(solution)/shard_map/all_to_all | solution.py:469
  28.6 0.0 copy-start.4
  28.6 4.7 %own_table.1.lhs_ref = bf16[64,256,64]{2,1,0:T(8,128)(2,1)} custom-call(f32[8,8192]{1,0:T(8,128)} %get-tuple-element.13.field_ref.refs_2_), custom_call_target="tpu_custom_call" | custom-call | flops 8000000000 | bytes 4500000 | tf_op jit(solution)/shard_map/own_table/pallas_call | solution.py:68
  33.3 0.0 copy-done.4
  33.3 0.6 copy.31
  33.9 0.0 collective-permute-done.refs_0_
  33.9 0.0 copy-start
  33.9 0.0 collective-permute-done.1.refs_1_
  33.9 0.0 copy-start.1
  33.9 0.0 collective-permute-done.2.refs_3_
  33.9 0.0 copy-start.2
  33.9 0.0 collective-permute-done.3.refs_4_
  33.9 0.7 copy-done
  34.6 0.1 copy-done.1
  34.7 0.1 copy-done.2
  34.7 0.0 copy-start.3
  34.7 0.7 copy-done.3
  35.5 40.8 %stacked.1.own_ref = f32[40,8192]{1,0:T(8,128)} custom-call(f32[8,8192]{1,0:T(8,128)} %copy-done, f32[8,8192]{1,0:T(8,128)} %copy-done.1, f32[8,8192]{1,0:T(8,128)} %get-tuple-element.13.field_ref.refs_2_, f32[8,8192]{1,0:T(8,128)} %copy-done.2, f32[8,8192]{1,0:T(8,128)} %copy-done.3), custom_call_target="tpu_custom_call" | custom-call | tf_op jit(solution)/shard_map/stacked/pallas_call | solution.py:419
  76.3 4.3 %collective-permute-start.4 = (f32[40,8192]{1,0:T(8,128)}, f32[40,8192]{1,0:T(8,128)S(1)}, u32[]{:S(2)}, u32[]{:S(2)}) collective-permute-start(f32[40,8192]{1,0:T(8,128)} %stacked.1.own_ref), channel_id=1, source_target_pairs={{0,1},{1,2},{2,3},{4,5},{5,6},{6,7},{8,9},{9,10},{10,11},{12,13},{... | collective-permute-start | bytes 3932168 | tf_op jit(solution)/shard_map/ppermute | solution.py:432
  80.6 1.9 %collective-permute-start.5 = (f32[40,8192]{1,0:T(8,128)}, f32[40,8192]{1,0:T(8,128)S(1)}, u32[]{:S(2)}, u32[]{:S(2)}) collective-permute-start(f32[40,8192]{1,0:T(8,128)} %stacked.1.own_ref), channel_id=1, source_target_pairs={{1,0},{2,1},{3,2},{5,4},{6,5},{7,6},{9,8},{10,9},{11,10},{13,12},{... | collective-permute-start | bytes 3932168 | tf_op jit(solution)/shard_map/ppermute | solution.py:432
  82.5 17.3 %own_layer.1.after_ref.sums_ref = f32[8,8192]{1,0:T(8,128)} custom-call(s32[15,64]{1,0:T(8,128)} %bitcast.35, s32[32]{0:T(128)} %bitcast.52, bf16[64,256,64]{2,1,0:T(8,128)(2,1)} %own_table.1.lhs_ref, f32[8,8192]{1,0:T(8,128)} %copy-done, f32[8,8192]{1,0:T(8,128)} %copy-done.1, f32[8,8192]{1,0:T(8,128)} %get-tuple-element.13.field_ref.refs_2_, ...), custom_call_target="tpu_custom_call" | custom-call | flops 17999998976 | bytes 6000000 | tf_op jit(solution)/shard_map/own_layer/pallas_call | solution.py:225
  99.8 0.0 all-to-all-done
  99.9 0.7 copy.24.swapped_ref
  100.6 4.4 %coupling_update.1 = (f32[3,8192]{1,0:T(4,128)}, f32[3,1,512]{2,1,0:T(1,128)}, f32[3,1,512]{2,1,0:T(1,128)}) custom-call(f32[6,8,64]{2,1,0:T(8,128)} %copy.24.swapped_ref, f32[6,8,64]{2,1,0:T(8,128)} %get-tuple-element.14.sent_ref, s32[8,64]{1,0:T(8,128)} %bitcast.47, s32[8,64]{1,0:T(8,128)} %bitcast.49, s32[8,128]{1,0:T(8,128)} %bitcast.50, ...), custom_call_target="tpu_custom_call" | custom-call | flops 4000000000 | bytes 6000000 | tf_op jit(solution)/shard_map/coupling_update/pallas_call | solution.py:393
  105.0 0.0 collective-permute-done.4.below_ref
  105.0 0.0 copy-start.5
  105.0 0.0 collective-permute-done.5.above_ref
  105.0 0.0 copy-start.6
  105.0 1.0 copy-done.5
  106.0 0.4 copy-done.6
  106.5 32.5 %other_layer.1 = (f32[3,1,8192]{2,1,0:T(1,128)}, f32[3,1,8192]{2,1,0:T(1,128)}) custom-call(s32[15,64]{1,0:T(8,128)} %bitcast.36, s32[32]{0:T(128)} %bitcast.53, s32[1]{0:T(128)} %bitcast.2.layer_ref, bf16[64,256,64]{2,1,0:T(8,128)(2,1)} %own_table.1.lhs_ref, f32[40,8192]{1,0:T(8,128)} %copy-done.5, f32[40,8192]{1,0:T(8,128)} %stacked.1.own_ref, ...), custom_call_target="tpu_custom_call" | custom-call | flops 35999997952 | bytes 6000000 | tf_op jit(solution)/shard_map/other_layer/pallas_call | solution.py:239
Async XLA Ops:
  4.1 29.8 %collective-permute-start = (f32[8,8192]{1,0:T(8,128)}, f32[8,8192]{1,0:T(8,128)S(1)}, u32[]{:S(2)}, u32[]{:S(2)}) collective-permute-start(f32[8,8192]{1,0:T(8,128)} %get-tuple-element.13.field_ref.refs_2_), channel_id=1, source_target_pairs={{0,8},{4,12},{8,16},{12,20},{16,24},{20,28},{24,32},{28,36},{32,40... | collective-permute-start | bytes 786440 | tf_op jit(solution)/shard_map/ppermute | solution.py:437
  7.7 26.2 %collective-permute-start.1 = (f32[8,8192]{1,0:T(8,128)}, f32[8,8192]{1,0:T(8,128)S(1)}, u32[]{:S(2)}, u32[]{:S(2)}) collective-permute-start(f32[8,8192]{1,0:T(8,128)} %get-tuple-element.13.field_ref.refs_2_), channel_id=1, source_target_pairs={{0,4},{4,8},{8,12},{12,16},{16,20},{20,24},{24,28},{28,32},{32,36}... | collective-permute-start | bytes 786440 | tf_op jit(solution)/shard_map/ppermute | solution.py:437
  8.0 25.9 %collective-permute-start.2 = (f32[8,8192]{1,0:T(8,128)}, f32[8,8192]{1,0:T(8,128)S(1)}, u32[]{:S(2)}, u32[]{:S(2)}) collective-permute-start(f32[8,8192]{1,0:T(8,128)} %get-tuple-element.13.field_ref.refs_2_), channel_id=1, source_target_pairs={{0,252},{4,0},{8,4},{12,8},{16,12},{20,16},{24,20},{28,24},{32,28}... | collective-permute-start | bytes 786440 | tf_op jit(solution)/shard_map/ppermute | solution.py:437
  15.4 18.5 %collective-permute-start.3 = (f32[8,8192]{1,0:T(8,128)}, f32[8,8192]{1,0:T(8,128)S(1)}, u32[]{:S(2)}, u32[]{:S(2)}) collective-permute-start(f32[8,8192]{1,0:T(8,128)} %get-tuple-element.13.field_ref.refs_2_), channel_id=1, source_target_pairs={{0,248},{4,252},{8,0},{12,4},{16,8},{20,12},{24,16},{28,20},{32,24... | collective-permute-start | bytes 786440 | tf_op jit(solution)/shard_map/ppermute | solution.py:437
  19.3 80.6 %all-to-all-start = ((f32[6,8,64]{1,0,2:T(8,128)}), f32[6,8,64]{1,0,2:T(8,128)S(1)}, u32[]{:S(2)}, u32[]{:S(2)}) async-start(f32[6,8,64]{1,0,2:T(8,128)} %copy.23), calls=%async_computation | async-start | bytes 524288 | tf_op jit(solution)/shard_map/all_to_all | solution.py:469
  28.6 4.7 %copy-start.4 = (s32[1,1,64,15]{2,1,3,0:T(1,128)S(1)}, s32[1,1,64,15]{2,1,3,0:T(1,128)}, u32[]{:S(2)}) copy-start(s32[1,1,64,15]{2,1,3,0:T(1,128)} %param.21) | copy-start | bytes 11524
  33.9 0.7 copy-start
  33.9 0.8 copy-start.1
  33.9 0.9 copy-start.2
  34.7 0.7 copy-start.3
  76.3 28.6 %collective-permute-start.4 = (f32[40,8192]{1,0:T(8,128)}, f32[40,8192]{1,0:T(8,128)S(1)}, u32[]{:S(2)}, u32[]{:S(2)}) collective-permute-start(f32[40,8192]{1,0:T(8,128)} %stacked.1.own_ref), channel_id=1, source_target_pairs={{0,1},{1,2},{2,3},{4,5},{5,6},{6,7},{8,9},{9,10},{10,11},{12,13},{... | collective-permute-start | bytes 3932168 | tf_op jit(solution)/shard_map/ppermute | solution.py:432
  80.6 24.4 %collective-permute-start.5 = (f32[40,8192]{1,0:T(8,128)}, f32[40,8192]{1,0:T(8,128)S(1)}, u32[]{:S(2)}, u32[]{:S(2)}) collective-permute-start(f32[40,8192]{1,0:T(8,128)} %stacked.1.own_ref), channel_id=1, source_target_pairs={{1,0},{2,1},{3,2},{5,4},{6,5},{7,6},{9,8},{10,9},{11,10},{13,12},{... | collective-permute-start | bytes 3932168 | tf_op jit(solution)/shard_map/ppermute | solution.py:432
  105.0 1.1 copy-start.5
  105.0 1.5 %copy-start.6 = (f32[40,8192]{1,0:T(8,128)}, f32[40,8192]{1,0:T(8,128)S(1)}, u32[]{:S(2)}) copy-start(f32[40,8192]{1,0:T(8,128)S(1)} %collective-permute-done.5.above_ref) | copy-start | bytes 3932164

commit v6 on v5

--- a/solution.py
+++ b/solution.py
@@ -404,24 +404,14 @@
 
 
 def stack_kernel(*refs):
-    out_ref, sems = refs[-2:]
-    copies = []
-    for place, ref in enumerate(refs[:-2]):
-        copies.append(pltpu.make_async_copy(ref, out_ref.at[pl.ds(8 * place, 8), :], sems.at[place]))
-    for copy in copies:
-        copy.start()
-    for copy in copies:
-        copy.wait()
+    for place, ref in enumerate(refs[:-1]):
+        refs[-1][8 * place : 8 * place + 8, :] = ref[...]
 
 
 def stacked(blocks):
-    raw = pl.BlockSpec(memory_space=pl.ANY)
     return pl.pallas_call(
         stack_kernel,
         out_shape=jax.ShapeDtypeStruct((8 * len(blocks), blocks[0].shape[1]), f32),
-        in_specs=[raw] * len(blocks),
-        out_specs=raw,
-        scratch_shapes=[pltpu.SemaphoreType.DMA((len(blocks),))],
         name="stacked",
     )(*blocks)
 

time: 139 us -> 101 us (0.73)
  Pallas kernels: 103 us -> 64.8 us
    pallas_call x1, Pallas kernels: 40.8 us -> 2.45 us  [stacked(): pl.pallas_call(stack_kernel, out_shape=jax.ShapeDtypeStruct((8 * len(bloc...]
  transfers between devices with their start and end apart: 7 -> 7, of which waited for: 0 -> 0; matrix products, arithmetic and copies ran while one was open for 2% -> 3% of each run, Pallas kernels for 48% -> 29%
where the time goes in v6:
time: 101 us
  Pallas kernels  64.8 us (64%)
  starting transfers between devices  29 us (29%)
  local copies, waits for them, and re-layouts  5.95 us (6%)
    pallas_call x1, Pallas kernels, other_layer_update(): pl.pallas_call(other_layer_kernel, out_shape=(shape, shape), in_specs=[sm...  32.5 us
    pallas_call x1, Pallas kernels, own_layer_sums(): pl.pallas_call(own_layer_kernel, out_shape=jax.ShapeDtypeStruct((8, point...  17.3 us
    ppermute x4, starting transfers between devices, shift_sector(): lax.ppermute(value, 'blk', [(i, (i + by) % size) for i in range(size)])  13.6 us
    all_to_all x1, starting transfers between devices, on_device(): lax.all_to_all(sent, 'blk', split_axis=2, concat_axis=2, tiled=True)  9.27 us
    ppermute x2, starting transfers between devices, shift_layer(): return lax.ppermute(value, 'layer', pairs)  6.17 us
    pallas_call x1, Pallas kernels, own_table(): pl.pallas_call(own_kernel, out_shape=jax.ShapeDtypeStruct((tiles, 2 * TIL...  4.68 us
    pallas_call x1, Pallas kernels, coupling_update(): pl.pallas_call(coupling_kernel, out_shape=(jax.ShapeDtypeStruct((3, point...  4.39 us
    unnamed x15, local copies, waits for them, and re-layouts  3.63 us
  transfers between devices with their start and end apart: 7, of which 0 were waited for; matrix products, arithmetic and copies ran while one was open for 3% of the time, Pallas kernels for 29%

profile of v6, /device:TPU:1, one launch (start us, length us, event | category | flops | bytes accessed | tf_op | source)
XLA Modules:
  0.0 100.6 jit_solution(11784745986630252714)
XLA Ops:
  0.6 3.5 %coupling_values.1 = (f32[8,8192]{1,0:T(8,128)}, f32[6,8,64]{2,1,0:T(8,128)}) custom-call(f32[3,1,8192]{2,1,0:T(1,128)} %bitcast.37, f32[3,1,8192]{2,1,0:T(1,128)} %bitcast.38, f32[1,8192]{1,0:T(1,128)} %bitcast.41, f32[1,8192]{1,0:T(1,128)} %bitcast.42, f32[3,1,512]{2,1,0:T(1,128)} %bitcast.43, s32[8,64]{1,0:T(8,128)} %bitcast.46, s32[8,64]{1,0:T(8,128)} %bitcast.48), custom_call_target="tpu_custom_call" | custom-call | flops 3000000000 | bytes 6000000 | tf_op jit(solution)/shard_map/coupling_values/pallas_call | solution.py:316
  4.1 3.6 %collective-permute-start = (f32[8,8192]{1,0:T(8,128)}, f32[8,8192]{1,0:T(8,128)S(1)}, u32[]{:S(2)}, u32[]{:S(2)}) collective-permute-start(f32[8,8192]{1,0:T(8,128)} %get-tuple-element.13.field_ref.refs_2_), channel_id=1, source_target_pairs={{0,8},{4,12},{8,16},{12,20},{16,24},{20,28},{24,32},{28,36},{32,40... | collective-permute-start | bytes 786440 | tf_op jit(solution)/shard_map/ppermute | solution.py:427
  7.7 0.3 collective-permute-start.1
  8.0 7.4 %collective-permute-start.2 = (f32[8,8192]{1,0:T(8,128)}, f32[8,8192]{1,0:T(8,128)S(1)}, u32[]{:S(2)}, u32[]{:S(2)}) collective-permute-start(f32[8,8192]{1,0:T(8,128)} %get-tuple-element.13.field_ref.refs_2_), channel_id=1, source_target_pairs={{0,252},{4,0},{8,4},{12,8},{16,12},{20,16},{24,20},{28,24},{32,28}... | collective-permute-start | bytes 786440 | tf_op jit(solution)/shard_map/ppermute | solution.py:427
  15.4 2.3 %collective-permute-start.3 = (f32[8,8192]{1,0:T(8,128)}, f32[8,8192]{1,0:T(8,128)S(1)}, u32[]{:S(2)}, u32[]{:S(2)}) collective-permute-start(f32[8,8192]{1,0:T(8,128)} %get-tuple-element.13.field_ref.refs_2_), channel_id=1, source_target_pairs={{0,248},{4,252},{8,0},{12,4},{16,8},{20,12},{24,16},{28,20},{32,24... | collective-permute-start | bytes 786440 | tf_op jit(solution)/shard_map/ppermute | solution.py:427
  17.7 1.6 %copy.23 = f32[6,8,64]{1,0,2:T(8,128)} copy(f32[6,8,64]{2,1,0:T(8,128)} %get-tuple-element.14.sent_ref) | data formatting | bytes 24576 | tf_op jit(solution)/shard_map/coupling_values/pallas_call | solution.py:316
  19.3 9.3 %all-to-all-start = ((f32[6,8,64]{1,0,2:T(8,128)}), f32[6,8,64]{1,0,2:T(8,128)S(1)}, u32[]{:S(2)}, u32[]{:S(2)}) async-start(f32[6,8,64]{1,0,2:T(8,128)} %copy.23), calls=%async_computation | async-start | bytes 524288 | tf_op jit(solution)/shard_map/all_to_all | solution.py:459
  28.6 0.0 copy-start.4
  28.6 4.7 %own_table.1.lhs_ref = bf16[64,256,64]{2,1,0:T(8,128)(2,1)} custom-call(f32[8,8192]{1,0:T(8,128)} %get-tuple-element.13.field_ref.refs_2_), custom_call_target="tpu_custom_call" | custom-call | flops 8000000000 | bytes 4500000 | tf_op jit(solution)/shard_map/own_table/pallas_call | solution.py:68
  33.3 0.0 copy-done.4
  33.3 0.6 copy.31
  33.9 0.0 collective-permute-done.refs_0_
  33.9 0.0 copy-start
  33.9 0.0 collective-permute-done.1.refs_1_
  33.9 0.0 copy-start.1
  33.9 0.0 collective-permute-done.2.refs_3_
  33.9 0.0 copy-start.2
  33.9 0.0 collective-permute-done.3.refs_4_
  33.9 0.7 copy-done
  34.6 0.1 copy-done.1
  34.7 0.1 copy-done.2
  34.7 0.0 copy-start.3
  34.7 0.7 copy-done.3
  35.5 2.5 %stacked.1.own_ref = f32[40,8192]{1,0:T(8,128)} custom-call(f32[8,8192]{1,0:T(8,128)} %copy-done, f32[8,8192]{1,0:T(8,128)} %copy-done.1, f32[8,8192]{1,0:T(8,128)} %get-tuple-element.13.field_ref.refs_2_, f32[8,8192]{1,0:T(8,128)} %copy-done.2, f32[8,8192]{1,0:T(8,128)} %copy-done.3), custom_call_target="tpu_custom_call" | custom-call | tf_op jit(solution)/shard_map/stacked/pallas_call | solution.py:412
  37.9 4.3 %collective-permute-start.4 = (f32[40,8192]{1,0:T(8,128)}, f32[40,8192]{1,0:T(8,128)S(1)}, u32[]{:S(2)}, u32[]{:S(2)}) collective-permute-start(f32[40,8192]{1,0:T(8,128)} %stacked.1.own_ref), channel_id=1, source_target_pairs={{0,1},{1,2},{2,3},{4,5},{5,6},{6,7},{8,9},{9,10},{10,11},{12,13},{... | collective-permute-start | bytes 3932168 | tf_op jit(solution)/shard_map/ppermute | solution.py:422
  42.2 1.9 %collective-permute-start.5 = (f32[40,8192]{1,0:T(8,128)}, f32[40,8192]{1,0:T(8,128)S(1)}, u32[]{:S(2)}, u32[]{:S(2)}) collective-permute-start(f32[40,8192]{1,0:T(8,128)} %stacked.1.own_ref), channel_id=1, source_target_pairs={{1,0},{2,1},{3,2},{5,4},{6,5},{7,6},{9,8},{10,9},{11,10},{13,12},{... | collective-permute-start | bytes 3932168 | tf_op jit(solution)/shard_map/ppermute | solution.py:422
  44.1 17.3 %own_layer.1.after_ref.sums_ref = f32[8,8192]{1,0:T(8,128)} custom-call(s32[15,64]{1,0:T(8,128)} %bitcast.35, s32[32]{0:T(128)} %bitcast.52, bf16[64,256,64]{2,1,0:T(8,128)(2,1)} %own_table.1.lhs_ref, f32[8,8192]{1,0:T(8,128)} %copy-done, f32[8,8192]{1,0:T(8,128)} %copy-done.1, f32[8,8192]{1,0:T(8,128)} %get-tuple-element.13.field_ref.refs_2_, ...), custom_call_target="tpu_custom_call" | custom-call | flops 17999998976 | bytes 6000000 | tf_op jit(solution)/shard_map/own_layer/pallas_call | solution.py:225
  61.4 0.0 all-to-all-done
  61.4 0.7 copy.24.swapped_ref
  62.2 4.4 %coupling_update.1 = (f32[3,8192]{1,0:T(4,128)}, f32[3,1,512]{2,1,0:T(1,128)}, f32[3,1,512]{2,1,0:T(1,128)}) custom-call(f32[6,8,64]{2,1,0:T(8,128)} %copy.24.swapped_ref, f32[6,8,64]{2,1,0:T(8,128)} %get-tuple-element.14.sent_ref, s32[8,64]{1,0:T(8,128)} %bitcast.47, s32[8,64]{1,0:T(8,128)} %bitcast.49, s32[8,128]{1,0:T(8,128)} %bitcast.50, ...), custom_call_target="tpu_custom_call" | custom-call | flops 4000000000 | bytes 6000000 | tf_op jit(solution)/shard_map/coupling_update/pallas_call | solution.py:393
  66.6 0.0 collective-permute-done.4.below_ref
  66.6 0.0 copy-start.5
  66.6 0.0 collective-permute-done.5.above_ref
  66.6 0.0 copy-start.6
  66.6 1.0 %copy-done.5 = f32[40,8192]{1,0:T(8,128)} copy-done((f32[40,8192]{1,0:T(8,128)}, f32[40,8192]{1,0:T(8,128)S(1)}, u32[]{:S(2)}) %copy-start.5) | copy-done | bytes 1310744
  67.6 0.4 copy-done.6
  68.1 32.5 %other_layer.1 = (f32[3,1,8192]{2,1,0:T(1,128)}, f32[3,1,8192]{2,1,0:T(1,128)}) custom-call(s32[15,64]{1,0:T(8,128)} %bitcast.36, s32[32]{0:T(128)} %bitcast.53, s32[1]{0:T(128)} %bitcast.2.layer_ref, bf16[64,256,64]{2,1,0:T(8,128)(2,1)} %own_table.1.lhs_ref, f32[40,8192]{1,0:T(8,128)} %copy-done.5, f32[40,8192]{1,0:T(8,128)} %stacked.1.own_ref, ...), custom_call_target="tpu_custom_call" | custom-call | flops 35999997952 | bytes 6000000 | tf_op jit(solution)/shard_map/other_layer/pallas_call | solution.py:239
Async XLA Ops:
  4.1 29.8 %collective-permute-start = (f32[8,8192]{1,0:T(8,128)}, f32[8,8192]{1,0:T(8,128)S(1)}, u32[]{:S(2)}, u32[]{:S(2)}) collective-permute-start(f32[8,8192]{1,0:T(8,128)} %get-tuple-element.13.field_ref.refs_2_), channel_id=1, source_target_pairs={{0,8},{4,12},{8,16},{12,20},{16,24},{20,28},{24,32},{28,36},{32,40... | collective-permute-start | bytes 786440 | tf_op jit(solution)/shard_map/ppermute | solution.py:427
  7.7 26.2 %collective-permute-start.1 = (f32[8,8192]{1,0:T(8,128)}, f32[8,8192]{1,0:T(8,128)S(1)}, u32[]{:S(2)}, u32[]{:S(2)}) collective-permute-start(f32[8,8192]{1,0:T(8,128)} %get-tuple-element.13.field_ref.refs_2_), channel_id=1, source_target_pairs={{0,4},{4,8},{8,12},{12,16},{16,20},{20,24},{24,28},{28,32},{32,36}... | collective-permute-start | bytes 786440 | tf_op jit(solution)/shard_map/ppermute | solution.py:427
  8.0 25.9 %collective-permute-start.2 = (f32[8,8192]{1,0:T(8,128)}, f32[8,8192]{1,0:T(8,128)S(1)}, u32[]{:S(2)}, u32[]{:S(2)}) collective-permute-start(f32[8,8192]{1,0:T(8,128)} %get-tuple-element.13.field_ref.refs_2_), channel_id=1, source_target_pairs={{0,252},{4,0},{8,4},{12,8},{16,12},{20,16},{24,20},{28,24},{32,28}... | collective-permute-start | bytes 786440 | tf_op jit(solution)/shard_map/ppermute | solution.py:427
  15.4 18.5 %collective-permute-start.3 = (f32[8,8192]{1,0:T(8,128)}, f32[8,8192]{1,0:T(8,128)S(1)}, u32[]{:S(2)}, u32[]{:S(2)}) collective-permute-start(f32[8,8192]{1,0:T(8,128)} %get-tuple-element.13.field_ref.refs_2_), channel_id=1, source_target_pairs={{0,248},{4,252},{8,0},{12,4},{16,8},{20,12},{24,16},{28,20},{32,24... | collective-permute-start | bytes 786440 | tf_op jit(solution)/shard_map/ppermute | solution.py:427
  19.3 42.1 %all-to-all-start = ((f32[6,8,64]{1,0,2:T(8,128)}), f32[6,8,64]{1,0,2:T(8,128)S(1)}, u32[]{:S(2)}, u32[]{:S(2)}) async-start(f32[6,8,64]{1,0,2:T(8,128)} %copy.23), calls=%async_computation | async-start | bytes 524288 | tf_op jit(solution)/shard_map/all_to_all | solution.py:459
  28.6 4.7 %copy-start.4 = (s32[1,1,64,15]{2,1,3,0:T(1,128)S(1)}, s32[1,1,64,15]{2,1,3,0:T(1,128)}, u32[]{:S(2)}) copy-start(s32[1,1,64,15]{2,1,3,0:T(1,128)} %param.21) | copy-start | bytes 11524
  33.9 0.7 copy-start
  33.9 0.8 copy-start.1
  33.9 0.9 copy-start.2
  34.7 0.7 copy-start.3
  37.9 28.6 %collective-permute-start.4 = (f32[40,8192]{1,0:T(8,128)}, f32[40,8192]{1,0:T(8,128)S(1)}, u32[]{:S(2)}, u32[]{:S(2)}) collective-permute-start(f32[40,8192]{1,0:T(8,128)} %stacked.1.own_ref), channel_id=1, source_target_pairs={{0,1},{1,2},{2,3},{4,5},{5,6},{6,7},{8,9},{9,10},{10,11},{12,13},{... | collective-permute-start | bytes 3932168 | tf_op jit(solution)/shard_map/ppermute | solution.py:422
  42.2 24.4 %collective-permute-start.5 = (f32[40,8192]{1,0:T(8,128)}, f32[40,8192]{1,0:T(8,128)S(1)}, u32[]{:S(2)}, u32[]{:S(2)}) collective-permute-start(f32[40,8192]{1,0:T(8,128)} %stacked.1.own_ref), channel_id=1, source_target_pairs={{1,0},{2,1},{3,2},{5,4},{6,5},{7,6},{9,8},{10,9},{11,10},{13,12},{... | collective-permute-start | bytes 3932168 | tf_op jit(solution)/shard_map/ppermute | solution.py:422
  66.6 1.1 %copy-start.5 = (f32[40,8192]{1,0:T(8,128)}, f32[40,8192]{1,0:T(8,128)S(1)}, u32[]{:S(2)}) copy-start(f32[40,8192]{1,0:T(8,128)S(1)} %collective-permute-done.4.below_ref) | copy-start | bytes 3932164
  66.6 1.5 %copy-start.6 = (f32[40,8192]{1,0:T(8,128)}, f32[40,8192]{1,0:T(8,128)S(1)}, u32[]{:S(2)}) copy-start(f32[40,8192]{1,0:T(8,128)S(1)} %collective-permute-done.5.above_ref) | copy-start | bytes 3932164
